TPU v7x, 128 devices: a whole 4x4x4 slice. The times are simulated.
128 devices in a mesh: req: 32 (over z, x, core), mlp: 4 (over y).
Axes of the slice: x: 4, y: 4, z: 4, core: 2. Of those that a mesh axis runs over, the one named last changes fastest.
Arguments:
- residual_in: bfloat16 [32768, 1664], P('req'), may hold values from -6 to 6
- lengths: int32 [4096], P(('req', 'mlp')), may hold values from 0 to 16, as said below
- owners: int32 [4096], P(('req', 'mlp')), may hold values from 0 to 31, as said below
- merge_dest: int32 [32768], P('req'), may hold values from 0 to 255, as said below
- segment_ids: int32 [32768], P('req'), may hold values from 0 to 3, as said below
- norm2_gain: float32 [1664], replicated, may hold values from 0.5 to 1.5
- norm2_bias: float32 [1664], replicated, may hold values from -3 to 3
- up_weight: bfloat16 [4096, 1664], P('mlp'), may hold values from -0.15625 to 0.15625
- up_bias: float32 [4096], P('mlp'), may hold values from -3 to 3
- down_weight: bfloat16 [4096, 1664], P('mlp'), may hold values from -0.09375 to 0.09375
- down_bias: float32 [1664], replicated, may hold values from -3 to 3
- proj_weight: bfloat16 [6656, 1664], P('mlp'), may hold values from -0.078125 to 0.078125
- norm3_gain: float32 [1664], replicated, may hold values from 0.5 to 1.5
- norm3_bias: float32 [1664], replicated, may hold values from -3 to 3
- next_weight: bfloat16 [1664, 3, 1664], P('req'), may hold values from -0.15625 to 0.15625
Outputs:
- merged_out: bfloat16 [16384, 1664], P(('req', 'mlp'))
- next_mixed: bfloat16 [16384, 1664], P(('req', 'mlp'))
Inputs may be any that keep to these rules, and one draw needn't show every extreme that they name: The 32 pieces of each block of 256 tokens (one device, req-major order) have lengths that are multiples of 4 and sum to 256; in every block one piece has exactly 16 tokens. The owners of the 32 pieces of one block are a permutation of 0 to 31; for each index of mlp, one piece of 16 tokens of each block of that index goes to one owner shared by all blocks of that index. `merge_dest`: within each device block a permutation of 0 to 255 that maps the tokens of each piece onto that piece's own positions. `segment_ids`: the four tokens of a block whose merge_dest values have the same quotient by 4 carry one segment id.
All inputs are finite; a program needn't handle non-finite values.
Results may differ from a plain program's by a relative error of at most 0.023.
Values may be sent and summed in bfloat16 or wider, within the bound.
No kernel may reach another device: no remote copies, remote signals or barrier semaphores. Data moves between devices by JAX's collectives and lax.ppermute only.
A program may use at most 128 MiB of HBM per device.

v0:
```python
import math

import jax
import jax.numpy as jnp
from jax import lax
from jax.sharding import PartitionSpec as P

HEAD_DIM = 104


EPSILON = 1e-06


def layer_norm(rows, gain, bias):
    values = rows.astype(jnp.float32)
    mean_value = jnp.mean(values, axis=-1, keepdims=True)
    centred = values - mean_value
    spread = jnp.mean(centred * centred, axis=-1, keepdims=True)
    return centred * lax.rsqrt(spread + EPSILON) * gain + bias


def block_attention(heads_in, slot_tags):
    queries = heads_in[:, :, 0]
    key_rows = heads_in[:, :, 1]
    value_rows = heads_in[:, :, 2]
    score_scale = 1.0 / math.sqrt(heads_in.shape[-1])
    scores = (
        jnp.einsum("bqhe,bkhe->bhqk", queries, key_rows, preferred_element_type=jnp.float32)
        * score_scale
    )
    slot_total = heads_in.shape[1]
    itself = lax.broadcasted_iota(jnp.int32, (slot_total, slot_total), 0) == lax.broadcasted_iota(
        jnp.int32, (slot_total, slot_total), 1
    )
    live_slots = slot_tags >= 0
    same_request = slot_tags[:, :, None] == slot_tags[:, None, :]
    allowed = same_request & live_slots[:, None, :] | itself[None]
    weights = jnp.where(allowed[:, None], jnp.exp(scores), 0.0)
    probs = (weights / jnp.sum(weights, axis=-1, keepdims=True)).astype(jnp.bfloat16)
    mixed_out = jnp.einsum("bhqk,bkhe->bqhe", probs, value_rows, preferred_element_type=jnp.float32)
    mixed_out = jnp.where(live_slots[:, :, None, None], mixed_out, 0.0)
    return mixed_out.astype(jnp.bfloat16)


def body(
    residual_in,
    lengths,
    owners,
    merge_dest,
    segment_ids,
    norm2_gain,
    norm2_bias,
    up_weight,
    up_bias,
    down_weight,
    down_bias,
    proj_weight,
    norm3_gain,
    norm3_bias,
    next_weight,
):
    group_rows, model_width = residual_in.shape
    lane_count = lax.axis_size("mlp")
    sender_count = lax.axis_size("req")
    lane_index = lax.axis_index("mlp")
    own_rows = group_rows // lane_count
    merged_rows = own_rows // 4
    slot_count = 2 * merged_rows // sender_count
    normed = layer_norm(residual_in, norm2_gain, norm2_bias).astype(jnp.bfloat16)
    upward = lax.dot_general(
        normed, up_weight, (((1,), (1,)), ((), ())), preferred_element_type=jnp.float32
    )
    hidden = jax.nn.gelu(upward + up_bias, approximate=False).astype(jnp.bfloat16)
    partial_sums = jnp.dot(hidden, down_weight, preferred_element_type=jnp.float32)
    places = merge_dest.reshape(lane_count, own_rows)
    block_ids = lax.broadcasted_iota(jnp.int32, (lane_count, own_rows), 0)
    token_ids = lax.broadcasted_iota(jnp.int32, (lane_count, own_rows), 1)
    sources = jnp.zeros((lane_count, own_rows), jnp.int32).at[block_ids, places].set(token_ids)
    block_offset = own_rows * lax.broadcasted_iota(jnp.int32, (lane_count, merged_rows, 4), 0)
    group_index = sources.reshape(lane_count, merged_rows, 4) + block_offset
    quadrant_rows = lax.dynamic_index_in_dim(group_index, lane_index, 2, False).reshape(-1)
    feed_out = lax.psum(partial_sums.astype(jnp.bfloat16), "mlp").astype(jnp.float32)
    layer_out = (residual_in.astype(jnp.float32) + feed_out + down_bias).astype(jnp.bfloat16)
    quarter = jnp.take(layer_out, quadrant_rows, axis=0)
    projected = lax.psum_scatter(
        jnp.dot(quarter, proj_weight, preferred_element_type=jnp.float32).astype(jnp.bfloat16),
        "mlp",
        scatter_dimension=0,
        tiled=True,
    )
    first_tokens = lax.dynamic_index_in_dim(group_index[:, :, 0], lane_index, 0, False)
    row_segment = jnp.take(segment_ids, first_tokens, axis=0)
    counts = lengths // 4
    starts = jnp.cumsum(counts) - counts
    index = lax.broadcasted_iota(jnp.int32, (merged_rows, 1), 0)
    inside = ((index >= starts[None, :]) & (index < (starts + counts)[None, :])).astype(jnp.int32)
    owner_of = jnp.sum(inside * owners[None, :], axis=1)
    rank = index[:, 0] - jnp.sum(inside * starts[None, :], axis=1)
    target = owner_of * slot_count + rank
    slot_ids = lax.broadcasted_iota(jnp.int32, (sender_count * slot_count, 1), 0)
    route_hits = slot_ids == target[None, :]
    outgoing = jnp.dot(
        route_hits.astype(jnp.bfloat16), projected, preferred_element_type=jnp.float32
    ).astype(jnp.bfloat16)
    sent_tags = jnp.sum(route_hits.astype(jnp.int32) * (row_segment + 1)[None, :], axis=1) - 1
    received, arrived_tags = (
        lax.all_to_all(outgoing, "req", split_axis=0, concat_axis=0, tiled=True),
        lax.all_to_all(sent_tags, "req", split_axis=0, concat_axis=0, tiled=True),
    )
    normed3 = layer_norm(received, norm3_gain, norm3_bias).astype(jnp.bfloat16)
    recv_rows = received.shape[0]
    piece = lax.all_gather(next_weight, "req", axis=0, tiled=True)
    heads_in = jnp.dot(
        normed3, piece.reshape(piece.shape[0], -1), preferred_element_type=jnp.float32
    )
    heads_in = heads_in.astype(jnp.bfloat16).reshape(1, recv_rows, 3, -1, HEAD_DIM)
    next_mixed = block_attention(heads_in, arrived_tags.reshape(1, recv_rows)).reshape(
        recv_rows, model_width
    )
    return (received, next_mixed)


def solution(mesh):
    return jax.shard_map(
        body,
        mesh=mesh,
        in_specs=(
            P("req", None),
            P(("req", "mlp")),
            P(("req", "mlp")),
            P("req"),
            P("req"),
            P(),
            P(),
            P("mlp", None),
            P("mlp"),
            P("mlp", None),
            P(),
            P("mlp", None),
            P(),
            P(),
            P("req", None, None),
        ),
        out_specs=(P(("req", "mlp"), None), P(("req", "mlp"), None)),
        check_vma=False,
    )
```

profile of v0, /device:TPU:1, one launch (start us, length us, event | category | flops | bytes accessed | tf_op | source)
XLA Modules:
  0.0 286.2 jit_solution(13230346240546526583)
XLA Ops:
  8.1 2.6 convert_reduce_fusion
  10.8 0.5 copy-done.3
  11.2 1.0 fusion.2
  12.3 20.5 %convolution_convert_fusion.1 = bf16[1024,1664]{1,0:T(8,128)(2,1)} fusion(bf16[1024,1664]{1,0:T(8,128)(2,1)S(1)} %copy-done, bf16[1024,1664]{1,0:T(8,128)(2,1)} %param.22, bf16[1024,1664]{1,0:T(8,128)(2,1)} %param.15, f32[1664]{0:T(1024)S(1)} %copy-done.13, f32[1664]{0:T(1024)S(1)} %copy-done.14, f32[1024]{0:T(1024)S(1)} %add_rsqrt_fusion.1, ...), kind=kOutput, calls=%fused_computation.34 | convolution fusion | flops 7060455424 | bytes 13657088 | tf_op jit(solution)/shard_map/dot_general | solution.py:74
  33.0 0.1 multiply_reduce_fusion
  33.1 0.1 and_reduce_fusion
  33.2 4.5 %scatter_custom_fusion = s32[1024]{0:T(1024)S(1)} fusion(s32[1024]{0:T(1024)S(1)} %bitcast.53, s32[1024]{0:T(1024)S(1)} %bitcast.54, s32[]{:T(128)} %constant.46.clone.1), kind=kCustom, calls=%fused_computation.124 | custom fusion | bytes 4100
  37.7 0.1 reshape.396
  37.8 0.1 broadcast_add_fusion
  37.9 0.2 fusion.116
  38.2 0.1 reshape.398
  38.2 0.7 reshape.397
  38.9 0.7 compare_and_fusion
  39.6 76.7 %all-reduce.2.cloned.1.call-done = bf16[1024,1664]{1,0:T(8,128)(2,1)} async-done(((bf16[1024,1664]{1,0:T(8,128)(2,1)}), bf16[1024,1664]{1,0:T(8,128)(2,1)}) %all-reduce.2.cloned.1.call-update) | async-done | bytes 3407888 | tf_op jit(solution)/shard_map/psum | solution.py:82
  116.3 4.8 %fusion.7 = bf16[1024,1664]{1,0:T(8,128)(2,1)} fusion(bf16[1024,1664]{1,0:T(8,128)(2,1)S(1)} %copy-done.4, bf16[1024,1664]{1,0:T(8,128)(2,1)} %all-reduce.2.cloned.1.call-done, f32[1664]{0:T(1024)S(1)} %copy-done.8), kind=kLoop, calls=%fused_computation.13 | loop fusion | flops 8519680 | bytes 10230272 | tf_op jit(solution)/shard_map/convert_element_type | solution.py:83
  121.1 4.5 %gather_fusion = bf16[256,1664]{1,0:T(8,128)(2,1)S(1)} fusion(bf16[1024,1664]{1,0:T(8,128)(2,1)} %fusion.7, s32[1024]{0:T(1024)S(1)} %pad_clamp_fusion.1), kind=kCustom, calls=%fused_computation | custom fusion | bytes 1704960 | tf_op jit(solution)/shard_map/jit(_take)/gather | solution.py:84
  125.7 5.5 %convolution_convert_fusion.2 = bf16[256,1664]{1,0:T(8,128)(2,1)} fusion(bf16[1664,1664]{1,0:T(8,128)(2,1)} %param.26, bf16[256,1664]{1,0:T(8,128)(2,1)S(1)} %gather_fusion, pred[256]{0:T(512)(128)(4,1)S(1)} %compare_and_fusion), kind=kOutput, calls=%fused_computation.40 | convolution fusion | flops 1418526720 | bytes 7241984 | tf_op jit(solution)/shard_map/dot_general | solution.py:86
  131.2 1.1 copy.42
  132.4 0.1 copy.40
  132.5 0.1 reduce-window.8
  132.6 0.1 reduce.6
  132.7 0.1 dynamic-slice_reduce_fusion.1
  132.8 0.7 gather_fusion.1
  133.6 0.1 select_reduce_fusion.2
  133.7 0.1 select_reduce_fusion
  133.8 0.1 sub.46
  133.9 14.4 %all_to_all.21 = s32[32,4,1]{1,2,0:T(1,128)S(1)} all-to-all(s32[32,4,1]{1,2,0:T(1,128)S(1)} %bitcast.51), channel_id=1, replica_groups=mesh['req'=32,'mlp'=4] {'req'}, dimensions={0} | all-to-all | bytes 1024 | tf_op jit(solution)/shard_map/all_to_all | solution.py:108
  148.3 0.5 broadcast.328
  148.8 0.7 reduce.18
  149.5 0.1 all_to_all.18
  149.6 3.1 %reduce-scatter.2.cloned.1.call-done = bf16[64,1664]{1,0:T(8,128)(2,1)} async-done(((bf16[256,1664]{1,0:T(8,128)(2,1)}), bf16[64,1664]{1,0:T(8,128)(2,1)}) %reduce-scatter.2.cloned.1.call-update) | async-done | bytes 213008 | tf_op jit(solution)/shard_map/reduce_scatter | solution.py:85
  152.7 1.3 convolution_convert_fusion.3
  154.0 0.9 all_to_all.14
  154.9 8.8 %all-to-all-start = ((bf16[32,4,1664]{2,1,0:T(4,128)(2,1)}), bf16[32,4,1664]{2,1,0:T(4,128)(2,1)S(1)}, u32[]{:S(2)}, u32[]{:S(2)}) async-start(bf16[32,4,1664]{2,1,0:T(4,128)(2,1)} %all_to_all.14), calls=%async_computation.1 | async-start | bytes 851968 | tf_op jit(solution)/shard_map/all_to_all | solution.py:107
  163.7 0.1 fusion.74
  163.9 10.4 %all-to-all-done = bf16[32,4,1664]{2,1,0:T(4,128)(2,1)S(1)} async-done(((bf16[32,4,1664]{2,1,0:T(4,128)(2,1)}), bf16[32,4,1664]{2,1,0:T(4,128)(2,1)S(1)}, u32[]{:S(2)}, u32[]{:S(2)}) %all-to-all-start) | async-done | bytes 426016 | tf_op jit(solution)/shard_map/all_to_all | solution.py:107
  174.3 0.2 convert_reduce_fusion.1
  174.5 0.4 fusion.65
  175.0 0.4 fusion.68
  175.4 0.1 convert_element_type.63
  175.5 0.9 all_to_all.16
  176.4 44.4 %all-gather.2.cloned.1.call-done = bf16[1664,3,1664]{2,1,0:T(4,128)(2,1)} async-done(((bf16[52,3,1664]{2,1,0:T(4,128)(2,1)}), bf16[1664,3,1664]{2,1,0:T(4,128)(2,1)}) %all-gather.2.cloned.1.call-update) | async-done | bytes 16613392 | tf_op jit(solution)/shard_map/all_gather | solution.py:112
  220.8 36.4 %copy.43 = bf16[1664,3,1664]{0,2,1:T(8,128)(2,1)} copy(bf16[1664,3,1664]{2,1,0:T(4,128)(2,1)} %all-gather.2.cloned.1.call-done) | data formatting | bytes 33226752 | tf_op jit(solution)/shard_map/all_gather | solution.py:112
  257.2 11.7 %convolution_convert_fusion = bf16[128,4992]{1,0:T(8,128)(2,1)} fusion(bf16[128,1664]{1,0:T(8,128)(2,1)S(1)} %convert_element_type.63, bf16[1664,4992]{0,1:T(8,128)(2,1)} %bitcast.47), kind=kOutput, calls=%fused_computation.15 | convolution fusion | flops 2127151104 | bytes 18317312 | tf_op jit(solution)/shard_map/dot_general | solution.py:113
  268.8 2.6 copy.44
  271.4 2.5 fusion.60
  273.9 2.8 fusion.62
  276.8 2.0 copy.46
  (61 shorter events, 0.4 us)
Async XLA Ops:
  8.0 4.3 %copy-start = (bf16[1024,1664]{1,0:T(8,128)(2,1)S(1)}, bf16[1024,1664]{1,0:T(8,128)(2,1)}, u32[]{:S(2)}) copy-start(bf16[1024,1664]{1,0:T(8,128)(2,1)} %param.24) | copy-start | bytes 10223620
  8.0 4.3 %copy-start.15 = (f32[1024]{0:T(1024)S(1)}, f32[1024]{0:T(1024)}, u32[]{:S(2)}) copy-start(f32[1024]{0:T(1024)} %param.23) | copy-start | bytes 12292
  8.0 4.3 %copy-start.13 = (f32[1664]{0:T(1024)S(1)}, f32[1664]{0:T(1024)}, u32[]{:S(2)}) copy-start(f32[1664]{0:T(1024)} %param.21) | copy-start | bytes 19972
  8.0 108.3 %all-reduce.2.cloned.1.call-start = ((), (), s32[]{:S(2)}) async-start(), calls=%async_computation.3 | async-start | bytes 6815744 | tf_op jit(solution)/shard_map/psum | solution.py:82
  8.1 3.1 %copy-start.3 = (bf16[1024,1664]{1,0:T(8,128)(2,1)S(1)}, bf16[1024,1664]{1,0:T(8,128)(2,1)}, u32[]{:S(2)}) copy-start(bf16[1024,1664]{1,0:T(8,128)(2,1)} %param.15) | copy-start | bytes 10223620
  8.1 4.2 %copy-start.14 = (f32[1664]{0:T(1024)S(1)}, f32[1664]{0:T(1024)}, u32[]{:S(2)}) copy-start(f32[1664]{0:T(1024)} %param.20) | copy-start | bytes 19972
  12.3 20.6 %copy-start.9 = (s32[1024]{0:T(1024)S(1)}, s32[1024]{0:T(1024)}, u32[]{:S(2)}) copy-start(s32[1024]{0:T(1024)} %param.18) | copy-start | bytes 12292
  12.3 20.7 %copy-start.12 = (s32[2]{0:T(128)S(1)}, s32[2]{0:T(128)}, u32[]{:S(2)}) copy-start(s32[2]{0:T(128)} %constant.153) | copy-start | bytes 28
  12.3 20.7 %copy-start.11 = (s32[2]{0:T(128)S(1)}, s32[2]{0:T(128)}, u32[]{:S(2)}) copy-start(s32[2]{0:T(128)} %constant.156) | copy-start | bytes 28
  32.9 83.4 %copy-start.4 = (bf16[1024,1664]{1,0:T(8,128)(2,1)S(1)}, bf16[1024,1664]{1,0:T(8,128)(2,1)}, u32[]{:S(2)}) copy-start(bf16[1024,1664]{1,0:T(8,128)(2,1)} %param.15) | copy-start | bytes 10223620
  32.9 83.4 %copy-start.8 = (f32[1664]{0:T(1024)S(1)}, f32[1664]{0:T(1024)}, u32[]{:S(2)}) copy-start(f32[1664]{0:T(1024)} %param.25) | copy-start | bytes 19972
  32.9 119.8 %reduce-scatter.2.cloned.1.call-start = ((), (), s32[]{:S(2)}) async-start(), calls=%async_computation.4 | async-start | bytes 1064960 | tf_op jit(solution)/shard_map/reduce_scatter | solution.py:85
  125.6 5.6 %copy-start.5 = (bf16[52,3,1664]{2,0,1:T(8,128)(2,1)S(1)}, bf16[52,3,1664]{2,0,1:T(8,128)(2,1)}, u32[]{:S(2)}) copy-start(bf16[52,3,1664]{2,0,1:T(8,128)(2,1)} %param.29) | copy-start | bytes 1557508
  125.6 6.8 %copy-start.16 = (s32[32]{0:T(128)S(1)}, s32[32]{0:T(128)}, u32[]{:S(2)}) copy-start(s32[32]{0:T(128)} %param.16) | copy-start | bytes 388
  125.7 7.2 %copy-start.2 = (s32[1024]{0:T(1024)S(1)}, s32[1024]{0:T(1024)}, u32[]{:S(2)}) copy-start(s32[1024]{0:T(1024)} %param.19) | copy-start | bytes 12292
  125.7 7.9 %copy-start.10 = (s32[32]{0:T(128)S(1)}, s32[32]{0:T(128)}, u32[]{:S(2)}) copy-start(s32[32]{0:T(128)} %param.17) | copy-start | bytes 388
  131.2 43.8 %copy-start.6 = (f32[1664]{0:T(1024)S(1)}, f32[1664]{0:T(1024)}, u32[]{:S(2)}) copy-start(f32[1664]{0:T(1024)} %param.28) | copy-start | bytes 19972
  131.2 43.8 %copy-start.7 = (f32[1664]{0:T(1024)S(1)}, f32[1664]{0:T(1024)}, u32[]{:S(2)}) copy-start(f32[1664]{0:T(1024)} %param.27) | copy-start | bytes 19972
  131.2 89.6 %all-gather.2.cloned.1.call-start = ((), (), s32[]{:S(2)}) async-start(), calls=%async_computation.5 | async-start | bytes 22843392 | tf_op jit(solution)/shard_map/all_gather | solution.py:112
  154.9 19.4 %all-to-all-start = ((bf16[32,4,1664]{2,1,0:T(4,128)(2,1)}), bf16[32,4,1664]{2,1,0:T(4,128)(2,1)S(1)}, u32[]{:S(2)}, u32[]{:S(2)}) async-start(bf16[32,4,1664]{2,1,0:T(4,128)(2,1)} %all_to_all.14), calls=%async_computation.1 | async-start | bytes 851968 | tf_op jit(solution)/shard_map/all_to_all | solution.py:107
  268.8 9.9 %copy-start.1 = (bf16[1024,1664]{1,0:T(8,128)(2,1)S(1)}, bf16[1024,1664]{1,0:T(8,128)(2,1)}, u32[]{:S(2)}) copy-start(bf16[1024,1664]{1,0:T(8,128)(2,1)} %param.24) | copy-start | bytes 10223620
Sparse Core Ops, SparseCore 0:
  33.0 83.2 all-reduce.1
  131.3 21.3 reduce-scatter.1
Sparse Core Ops, SparseCore 1:
  134.3 86.4 all-gather.1
where the time goes:
time: 288 us; the launch traced here: 286 us
  waiting for transfers between devices  135 us (47%)
  local copies, waits for them, and re-layouts  56.2 us (20%)
  matrix products  44.3 us (15%)
  between operations  15.9 us (6%)
  blocking collectives  14.4 us (5%)
  other arithmetic  11.7 us (4%)
  starting transfers between devices  8.95 us (3%)
    psum x1, waiting for transfers between devices, body(): lax.psum(partial_sums.astype(jnp.bfloat16), 'mlp').astype(jnp.float32)  76.7 us
    all_gather x1, waiting for transfers between devices, body(): piece = lax.all_gather(next_weight, 'req', axis=0, tiled=True)  44.4 us
    all_gather x1, local copies, waits for them, and re-layouts, body(): piece = lax.all_gather(next_weight, 'req', axis=0, tiled=True)  36.4 us
    dot_general x1, matrix products, body(): jnp.dot(hidden, down_weight, preferred_element_type=jnp.float32)  20.5 us
    all_to_all x1, blocking collectives, body(): lax.all_to_all(sent_tags, 'req', split_axis=0, concat_axis=0, tiled=True)  14.4 us
    dot_general x1, matrix products, body(): jnp.dot(normed3, piece.reshape(piece.shape[0], -1), preferred_element_typ...  11.7 us
    all_to_all x1, waiting for transfers between devices, body(): lax.all_to_all(outgoing, 'req', split_axis=0, concat_axis=0, tiled=True)  10.4 us
    all_to_all x1, starting transfers between devices, body(): lax.all_to_all(outgoing, 'req', split_axis=0, concat_axis=0, tiled=True)  8.83 us
  transfers between devices with their start and end apart: 4, of which 4 were waited for; matrix products, arithmetic and copies ran while one was open for 5% of the time, Pallas kernels for 0%

commit v1 on v0

v1 whole, which is shorter than its diff:
```python
import math

import jax
import jax.numpy as jnp
from jax import lax
from jax.experimental import pallas as pl
from jax.experimental.pallas import tpu as pltpu
from jax.sharding import PartitionSpec as P

HEAD_DIM = 104
EPSILON = 1e-06
MIB = 1 << 20


def normalise(values, gain, bias):
    mean_value = jnp.mean(values, axis=-1, keepdims=True)
    centred = values - mean_value
    spread = jnp.mean(centred * centred, axis=-1, keepdims=True)
    return centred * lax.rsqrt(spread + EPSILON) * gain + bias


def relative_offset(step):
    return jnp.where(step == 0, 2, jnp.where(step == 1, 1, jnp.where(step == 2, 3, 0)))


def arrange_kernel(lane_ref, rows_ref, dest_ref, gain_ref, bias_ref, normed_ref, own_ref):
    lane = lane_ref[0]
    rows = rows_ref[...]
    count = rows.shape[0]
    part = count // 4
    normed = normalise(rows.astype(jnp.float32), gain_ref[...], bias_ref[...]).astype(jnp.bfloat16)
    index = lax.broadcasted_iota(jnp.int32, (count, count), 0)
    step = index // part
    wanted = 4 * (index - step * part) + ((lane + relative_offset(step)) & 3)
    hits = jnp.where(dest_ref[0] == wanted, 1.0, 0.0).astype(jnp.bfloat16)
    moved = jnp.dot(hits, normed, preferred_element_type=jnp.float32).astype(jnp.bfloat16)
    normed_ref[...] = moved.reshape(normed_ref.shape)
    own = jnp.dot(hits[3 * part :], rows, preferred_element_type=jnp.float32).astype(jnp.bfloat16)
    own_ref[...] = own.reshape(own_ref.shape)


def arrange(lane, residual_in, merge_dest, gain, bias):
    group_rows, width = residual_in.shape
    block = group_rows // 4
    part = block // 4
    return pl.pallas_call(
        arrange_kernel,
        grid_spec=pltpu.PrefetchScalarGridSpec(
            num_scalar_prefetch=1,
            grid=(4,),
            in_specs=[
                pl.BlockSpec((block, width), lambda b, s: (b, 0)),
                pl.BlockSpec((1, 1, block), lambda b, s: (b, 0, 0)),
                pl.BlockSpec((1, width), lambda b, s: (0, 0)),
                pl.BlockSpec((1, width), lambda b, s: (0, 0)),
            ],
            out_specs=[
                pl.BlockSpec((4, 1, part, width), lambda b, s: (0, b, 0, 0)),
                pl.BlockSpec((1, part, width), lambda b, s: (b, 0, 0)),
            ],
        ),
        out_shape=[
            jax.ShapeDtypeStruct((4, 4, part, width), jnp.bfloat16),
            jax.ShapeDtypeStruct((4, part, width), jnp.bfloat16),
        ],
        compiler_params=pltpu.CompilerParams(vmem_limit_bytes=24 * MIB),
        name="arrange",
    )(lane, residual_in, merge_dest.reshape(4, 1, block), gain, bias)


def gelu(value):
    return 0.5 * value * (1.0 + lax.erf(value * (1.0 / math.sqrt(2.0))))


def feed_step(rows_ref, up_ref, up_bias_ref, down_ref, total_ref):
    upward = lax.dot_general(
        rows_ref[...], up_ref[...], (((1,), (1,)), ((), ())), preferred_element_type=jnp.float32
    )
    hidden = gelu(upward + up_bias_ref[...]).astype(jnp.bfloat16)
    part = jnp.dot(hidden, down_ref[...], preferred_element_type=jnp.float32)

    @pl.when(pl.program_id(0) == 0)
    def _():
        total_ref[...] = part

    @pl.when(pl.program_id(0) > 0)
    def _():
        total_ref[...] += part


def feed_kernel(rows_ref, up_ref, up_bias_ref, down_ref, first_ref, second_ref, total_ref):
    feed_step(rows_ref, up_ref, up_bias_ref, down_ref, total_ref)

    @pl.when(pl.program_id(0) == pl.num_programs(0) - 1)
    def _():
        half = first_ref.shape[0]
        first_ref[...] = total_ref[:half].astype(jnp.bfloat16)
        second_ref[...] = total_ref[half:].astype(jnp.bfloat16)


def feed_own_kernel(
    rows_ref, up_ref, up_bias_ref, down_ref, residual_ref, down_bias_ref, out_ref, total_ref
):
    feed_step(rows_ref, up_ref, up_bias_ref, down_ref, total_ref)

    @pl.when(pl.program_id(0) == pl.num_programs(0) - 1)
    def _():
        out_ref[...] = total_ref[...] + (
            residual_ref[...].astype(jnp.float32) + down_bias_ref[...]
        )


def feed(rows, step, up_weight, up_bias, down_weight, extra=None):
    _, count, width = rows.shape
    hidden_units = up_weight.shape[0]
    tile = 256
    in_specs = [
        pl.BlockSpec((None, count, width), lambda j: (step, 0, 0)),
        pl.BlockSpec((tile, width), lambda j: (j, 0)),
        pl.BlockSpec((1, tile), lambda j: (0, j)),
        pl.BlockSpec((tile, width), lambda j: (j, 0)),
    ]
    args = [rows, up_weight, up_bias, down_weight]
    if extra is None:
        half = count // 2
        out_specs = [pl.BlockSpec((half, width), lambda j: (0, 0))] * 2
        out_shape = [jax.ShapeDtypeStruct((half, width), jnp.bfloat16)] * 2
        kernel = feed_kernel
    else:
        in_specs += [
            pl.BlockSpec((count, width), lambda j: (0, 0)),
            pl.BlockSpec((1, width), lambda j: (0, 0)),
        ]
        args += list(extra)
        out_specs = pl.BlockSpec((count, width), lambda j: (0, 0))
        out_shape = jax.ShapeDtypeStruct((count, width), jnp.float32)
        kernel = feed_own_kernel
    return pl.pallas_call(
        kernel,
        grid=(hidden_units // tile,),
        in_specs=in_specs,
        out_specs=out_specs,
        out_shape=out_shape,
        scratch_shapes=[pltpu.VMEM((count, width), jnp.float32)],
        compiler_params=pltpu.CompilerParams(vmem_limit_bytes=24 * MIB),
        cost_estimate=pl.CostEstimate(
            flops=4 * count * width * hidden_units,
            bytes_accessed=4 * hidden_units * width + 8 * count * width,
            transcendentals=count * hidden_units,
        ),
        name="feed",
    )(*args)


def project_kernel(
    lane_ref, base_ref, a1_ref, a2_ref, b1_ref, b2_ref, weight_ref, o0, o1, o2, own, total_ref
):
    half = a1_ref.shape[0]
    part = half // 2
    top = base_ref[:half] + a1_ref[...].astype(jnp.float32) + a2_ref[...].astype(jnp.float32)
    low = base_ref[half:] + b1_ref[...].astype(jnp.float32) + b2_ref[...].astype(jnp.float32)
    rows = jnp.concatenate([top, low], axis=0).astype(jnp.bfloat16)
    total_ref[...] = jnp.dot(rows, weight_ref[...], preferred_element_type=jnp.float32)
    lane = lane_ref[0]
    for offset, ref in ((2, o0), (1, o1), (3, o2), (0, own)):
        start = pl.multiple_of(((lane + offset) & 3) * part, part)
        ref[...] = total_ref[pl.ds(start, part)].astype(ref.dtype)


def project(lane, base, a1, a2, b1, b2, weight):
    count, width = base.shape
    part = count // 4
    vmem = pl.BlockSpec(memory_space=pltpu.VMEM)
    return pl.pallas_call(
        project_kernel,
        in_specs=[pl.BlockSpec(memory_space=pltpu.SMEM)] + [vmem] * 6,
        out_specs=[vmem] * 4,
        out_shape=[jax.ShapeDtypeStruct((part, width), jnp.bfloat16)] * 3
        + [jax.ShapeDtypeStruct((part, width), jnp.float32)],
        scratch_shapes=[pltpu.VMEM((count, width), jnp.float32)],
        compiler_params=pltpu.CompilerParams(vmem_limit_bytes=24 * MIB),
        cost_estimate=pl.CostEstimate(
            flops=2 * count * width * width,
            bytes_accessed=2 * width * width + 12 * count * width,
            transcendentals=0,
        ),
        name="project",
    )(lane, base, a1, a2, b1, b2, weight)


def turn(column):
    count = column.shape[0]
    same = lax.broadcasted_iota(jnp.int32, (count, count), 0) == lax.broadcasted_iota(
        jnp.int32, (count, count), 1
    )
    return jnp.sum(jnp.where(same, column, 0), axis=0, keepdims=True)


def route_kernel(
    lane_ref, own_ref, r0, r1, r2, counts_ref, owners_ref, dest_ref, seg_ref, out_ref
):
    lane = lane_ref[0]
    rows, width = own_ref.shape
    pieces = counts_ref.shape[1]
    slots = 2 * rows // pieces
    projected = (
        own_ref[...]
        + r0[...].astype(jnp.float32)
        + r1[...].astype(jnp.float32)
        + r2[...].astype(jnp.float32)
    ).astype(jnp.bfloat16)
    counts = counts_ref[...] // 4
    earlier = lax.broadcasted_iota(jnp.int32, (pieces, pieces), 1) < lax.broadcasted_iota(
        jnp.int32, (pieces, pieces), 0
    )
    starts = jnp.sum(jnp.where(earlier, counts, 0), axis=1, keepdims=True)
    upto = earlier | (
        lax.broadcasted_iota(jnp.int32, (pieces, pieces), 1)
        == lax.broadcasted_iota(jnp.int32, (pieces, pieces), 0)
    )
    ends = jnp.sum(jnp.where(upto, counts, 0), axis=1, keepdims=True)
    index = lax.broadcasted_iota(jnp.int32, (pieces, rows), 1)
    inside = (index >= starts) & (index < ends)
    owner_col = jnp.sum(
        jnp.where(
            lax.broadcasted_iota(jnp.int32, (pieces, pieces), 0)
            == lax.broadcasted_iota(jnp.int32, (pieces, pieces), 1),
            owners_ref[...],
            0,
        ),
        axis=1,
        keepdims=True,
    )
    target = jnp.sum(jnp.where(inside, owner_col * slots - starts, 0), axis=0, keepdims=True)
    target = target + lax.broadcasted_iota(jnp.int32, (1, rows), 1)
    out_rows = pieces * slots
    hits = lax.broadcasted_iota(jnp.int32, (out_rows, rows), 0) == target
    moved = jnp.dot(
        jnp.where(hits, 1.0, 0.0).astype(jnp.bfloat16),
        projected,
        preferred_element_type=jnp.float32,
    ).astype(jnp.bfloat16)
    dest = dest_ref[lane]
    seg = seg_ref[lane]
    tokens = dest.shape[1]
    first = dest == 4 * lax.broadcasted_iota(jnp.int32, (rows, tokens), 0)
    marks = turn(jnp.sum(jnp.where(first, seg, 0), axis=1, keepdims=True)) + 1
    tags = jnp.sum(jnp.where(hits, marks, 0), axis=1, keepdims=True)
    out_ref[:, :width] = moved
    out_ref[:, width:] = jnp.broadcast_to(
        tags.astype(jnp.float32), (out_rows, out_ref.shape[1] - width)
    ).astype(jnp.bfloat16)


def route(lane, own, others, lengths, owners, merge_dest, segment_ids):
    rows, width = own.shape
    pieces = lengths.shape[0]
    block = merge_dest.shape[0] // 4
    vmem = pl.BlockSpec(memory_space=pltpu.VMEM)
    return pl.pallas_call(
        route_kernel,
        in_specs=[pl.BlockSpec(memory_space=pltpu.SMEM)] + [vmem] * 8,
        out_specs=vmem,
        out_shape=jax.ShapeDtypeStruct((2 * rows, width + 128), jnp.bfloat16),
        compiler_params=pltpu.CompilerParams(vmem_limit_bytes=24 * MIB),
        name="route",
    )(
        lane,
        own,
        *others,
        lengths.reshape(1, pieces),
        owners.reshape(1, pieces),
        merge_dest.reshape(4, 1, block),
        segment_ids.reshape(4, 1, block),
    )


def attend_kernel(got_ref, gain_ref, bias_ref, weight_ref, merged_ref, mixed_ref, heads_ref):
    count, width = merged_ref.shape
    rows = got_ref[:, :width]
    merged_ref[...] = rows
    tags = got_ref[:, width:].astype(jnp.float32)
    tag_col = tags[:, :1]
    itself = lax.broadcasted_iota(jnp.int32, (count, count), 0) == lax.broadcasted_iota(
        jnp.int32, (count, count), 1
    )
    tag_row = jnp.sum(jnp.where(itself, tag_col, 0.0), axis=0, keepdims=True)
    allowed = ((tag_col == tag_row) & (tag_row > 0.5)) | itself
    live = tag_col > 0.5
    normed = normalise(rows.astype(jnp.float32), gain_ref[...], bias_ref[...]).astype(jnp.bfloat16)
    heads_ref[...] = jnp.dot(normed, weight_ref[...], preferred_element_type=jnp.float32).astype(
        jnp.bfloat16
    )
    scale = 1.0 / math.sqrt(HEAD_DIM)
    for head in range(width // HEAD_DIM):
        at = head * HEAD_DIM
        query = heads_ref[:, at : at + HEAD_DIM]
        keys = heads_ref[:, width + at : width + at + HEAD_DIM]
        value = heads_ref[:, 2 * width + at : 2 * width + at + HEAD_DIM]
        scores = (
            lax.dot_general(
                query, keys, (((1,), (1,)), ((), ())), preferred_element_type=jnp.float32
            )
            * scale
        )
        weights = jnp.where(allowed, jnp.exp(scores), 0.0)
        probs = (weights / jnp.sum(weights, axis=-1, keepdims=True)).astype(jnp.bfloat16)
        mixed = jnp.dot(probs, value, preferred_element_type=jnp.float32)
        mixed_ref[:, at : at + HEAD_DIM] = jnp.where(live, mixed, 0.0).astype(jnp.bfloat16)


def attend(got, gain, bias, weight):
    count = got.shape[0]
    width, columns = weight.shape
    vmem = pl.BlockSpec(memory_space=pltpu.VMEM)
    return pl.pallas_call(
        attend_kernel,
        in_specs=[vmem] * 4,
        out_specs=[vmem] * 2,
        out_shape=[jax.ShapeDtypeStruct((count, width), jnp.bfloat16)] * 2,
        scratch_shapes=[pltpu.VMEM((count, columns), jnp.bfloat16)],
        compiler_params=pltpu.CompilerParams(vmem_limit_bytes=32 * MIB),
        cost_estimate=pl.CostEstimate(
            flops=2 * count * width * columns,
            bytes_accessed=2 * width * columns,
            transcendentals=count * count * 16,
        ),
        name="attend",
    )(got, gain, bias, weight)


def body(
    residual_in,
    lengths,
    owners,
    merge_dest,
    segment_ids,
    norm2_gain,
    norm2_bias,
    up_weight,
    up_bias,
    down_weight,
    down_bias,
    proj_weight,
    norm3_gain,
    norm3_bias,
    next_weight,
):
    width = residual_in.shape[1]
    lanes = lax.axis_size("mlp")
    lane = lax.axis_index("mlp").astype(jnp.int32).reshape(1)
    onward = [(i, (i + 1) % lanes) for i in range(lanes)]
    back = [(i, (i - 1) % lanes) for i in range(lanes)]
    across = [(i, (i + 2) % lanes) for i in range(lanes)]

    def row(vector):
        return vector.reshape(1, -1)

    depth = next_weight.shape[0]
    padded = -(-depth // 8) * 8
    shard = jnp.pad(next_weight.reshape(depth, -1), ((0, padded - depth), (0, 0)))
    gathered = lax.all_gather(shard, "req", axis=0, tiled=True)
    full = gathered.reshape(-1, padded, 3 * width)[:, :depth].reshape(width, 3 * width)

    normed, own_rows = arrange(lane, residual_in, merge_dest, row(norm2_gain), row(norm2_bias))
    count = residual_in.shape[0] // lanes
    normed = normed.reshape(4, count, width)
    bias_up = row(up_bias)
    far_a, far_b = feed(normed, 0, up_weight, bias_up, down_weight)
    far_a = lax.ppermute(far_a, "mlp", onward)
    far_b = lax.ppermute(far_b, "mlp", back)
    next_a, next_b = feed(normed, 1, up_weight, bias_up, down_weight)
    b1 = lax.ppermute(next_b, "mlp", onward)
    prev_a, prev_b = feed(normed, 2, up_weight, bias_up, down_weight)
    a2 = lax.ppermute(prev_a, "mlp", back)

    def join(first, second):
        return (first.astype(jnp.float32) + second.astype(jnp.float32)).astype(jnp.bfloat16)

    a1 = lax.ppermute(join(far_a, next_a), "mlp", onward)
    b2 = lax.ppermute(join(far_b, prev_b), "mlp", back)
    base = feed(
        normed,
        3,
        up_weight,
        bias_up,
        down_weight,
        (own_rows.reshape(count, width), row(down_bias)),
    )
    p0, p1, p2, own = project(lane, base, a1, a2, b1, b2, proj_weight)
    others = (
        lax.ppermute(p0, "mlp", across),
        lax.ppermute(p1, "mlp", onward),
        lax.ppermute(p2, "mlp", back),
    )
    outgoing = route(lane, own, others, lengths, owners, merge_dest, segment_ids)
    got = lax.all_to_all(outgoing, "req", split_axis=0, concat_axis=0, tiled=True)
    return tuple(attend(got, row(norm3_gain), row(norm3_bias), full))


def solution(mesh):
    return jax.shard_map(
        body,
        mesh=mesh,
        in_specs=(
            P("req", None),
            P(("req", "mlp")),
            P(("req", "mlp")),
            P("req"),
            P("req"),
            P(),
            P(),
            P("mlp", None),
            P("mlp"),
            P("mlp", None),
            P(),
            P("mlp", None),
            P(),
            P(),
            P("req", None, None),
        ),
        out_specs=(P(("req", "mlp"), None), P(("req", "mlp"), None)),
        check_vma=False,
    )
```

time: 288 us -> 139 us (0.48)
  waiting for transfers between devices: 135 us -> 30.3 us
  matrix products: 44.3 us -> 0 us
  Pallas kernels: 0 us -> 36.8 us
  local copies, waits for them, and re-layouts: 56.2 us -> 32 us
  starting transfers between devices: 8.95 us -> 24.8 us
  blocking collectives: 14.4 us -> 0 us
  other arithmetic: 11.7 us -> 0.2 us
    psum x1 -> x0, waiting for transfers between devices: 76.7 us -> none  [body(): lax.psum(partial_sums.astype(jnp.bfloat16), 'mlp').astype(jnp.float32)]
    all_gather x1, waiting for transfers between devices: 44.4 us -> 0.02 us  [body(): gathered = lax.all_gather(shard, 'req', axis=0, tiled=True)]
    dot_general x6 -> x0, matrix products: 44.3 us -> none  [the longest x1 20.5 us: body(): jnp.dot(hidden, down_weight, preferred_element_type=jnp.float32)]
    pallas_call x0 -> x8, Pallas kernels: none -> 36.8 us  [the longest x4 22.1 us: feed(): pl.pallas_call(kernel, grid=(hidden_units // tile,), in_specs=in_specs, o...]
    all_gather x1 -> x0, local copies, waits for them, and re-layouts: 36.4 us -> none  [body(): piece = lax.all_gather(next_weight, 'req', axis=0, tiled=True)]
    ppermute x0 -> x9, waiting for transfers between devices: none -> 19.4 us  [the longest x1 9.7 us: body(): far_b = lax.ppermute(far_b, 'mlp', back)]
    reshape x4 -> x6, local copies, waits for them, and re-layouts: 0.87 us -> 18.6 us  [the longest x1 18.6 us: body(): gathered.reshape(-1, padded, 3 * width)[:, :depth].reshape(width, 3 * width)]
    all_to_all x1 -> x0, blocking collectives: 14.4 us -> none  [body(): lax.all_to_all(sent_tags, 'req', split_axis=0, concat_axis=0, tiled=True)]
  transfers between devices with their start and end apart: 4 -> 11, of which waited for: 4 -> 6; matrix products, arithmetic and copies ran while one was open for 5% -> 0% of each run, Pallas kernels for 0% -> 21%
where the time goes in v1:
time: 139 us
  Pallas kernels  36.8 us (26%)
  local copies, waits for them, and re-layouts  32 us (23%)
  waiting for transfers between devices  30.3 us (22%)
  starting transfers between devices  24.8 us (18%)
  between operations  14.4 us (10%)
    pallas_call x4, Pallas kernels, feed(): pl.pallas_call(kernel, grid=(hidden_units // tile,), in_specs=in_specs, o...  22.1 us
    reshape x1, local copies, waits for them, and re-layouts, body(): gathered.reshape(-1, padded, 3 * width)[:, :depth].reshape(width, 3 * width)  18.6 us
    unnamed x37, local copies, waits for them, and re-layouts  11.6 us
    all_to_all x1, waiting for transfers between devices, body(): lax.all_to_all(outgoing, 'req', split_axis=0, concat_axis=0, tiled=True)  10.8 us
    all_to_all x1, starting transfers between devices, body(): lax.all_to_all(outgoing, 'req', split_axis=0, concat_axis=0, tiled=True)  10.4 us
    ppermute x1, waiting for transfers between devices, body(): far_b = lax.ppermute(far_b, 'mlp', back)  9.7 us
    pallas_call x1, Pallas kernels, attend(): pl.pallas_call(attend_kernel, in_specs=[vmem] * 4, out_specs=[vmem] * 2,...  7.86 us
    ppermute x1, waiting for transfers between devices, body(): lax.ppermute(p1, 'mlp', onward)  5.73 us
  transfers between devices with their start and end apart: 11, of which 6 were waited for; matrix products, arithmetic and copies ran while one was open for 0% of the time, Pallas kernels for 21%

profile of v1, /device:TPU:1, one launch (start us, length us, event | category | flops | bytes accessed | tf_op | source)
XLA Modules:
  0.0 138.5 jit_solution(5847802567419728226)
XLA Ops:
  7.2 0.0 all-gather.2.cloned.1.call-start
  7.2 1.3 copy.17
  8.6 0.0 copy-start.5
  8.6 0.3 pad.5
  8.9 0.0 copy-start.1
  8.9 0.1 copy.18
  8.9 0.9 pad.4
  9.8 0.0 all-gather.2.cloned.1.call-update
  9.9 0.0 copy-start.4
  9.9 2.2 %copy-done.4 = bf16[1024,1664]{1,0:T(8,128)(2,1)S(1)} copy-done((bf16[1024,1664]{1,0:T(8,128)(2,1)S(1)}, bf16[1024,1664]{1,0:T(8,128)(2,1)}, u32[]{:S(2)}) %copy-start.4) | copy-done | bytes 3407896
  12.1 4.3 %arrange.1 = (bf16[4,4,64,1664]{3,2,1,0:T(8,128)(2,1)S(1)}, bf16[4,64,1664]{2,1,0:T(8,128)(2,1)S(1)}) custom-call(s32[1]{0:T(128)} %bitcast.lane_ref, bf16[1024,1664]{1,0:T(8,128)(2,1)S(1)} %copy-done.4, s32[4,1,256]{2,1,0:T(1,128)S(1)} %bitcast.24, f32[1,1664]{1,0:T(1,128)S(1)} %reshape.57.gain_ref, f32[1,1664]{1,0:T(1,128)S(1)} %reshape.58.bias_ref), custom_call_target="tpu_custom_call" | custom-call | tf_op jit(solution)/shard_map/arrange/pallas_call | solution.py:46
  16.4 0.0 copy-start.2
  16.4 2.0 %copy-done.2 = bf16[1024,1664]{1,0:T(8,128)(2,1)S(1)} copy-done((bf16[1024,1664]{1,0:T(8,128)(2,1)S(1)}, bf16[1024,1664]{1,0:T(8,128)(2,1)}, u32[]{:S(2)}) %copy-start.2) | copy-done | bytes 3407896
  18.4 5.5 %feed.5 = (bf16[128,1664]{1,0:T(8,128)(2,1)S(1)}, bf16[128,1664]{1,0:T(8,128)(2,1)S(1)}) custom-call(bf16[4,256,1664]{2,1,0:T(8,128)(2,1)S(1)} %bitcast.13, bf16[1024,1664]{1,0:T(8,128)(2,1)S(1)} %copy-done.1, f32[1,1024]{1,0:T(1,128)S(1)} %bitcast.20, bf16[1024,1664]{1,0:T(8,128)(2,1)S(1)} %copy-done.2), custom_call_target="tpu_custom_call" | custom-call | flops 1744830464 | bytes 10223616 | tf_op jit(solution)/shard_map/feed/pallas_call | solution.py:138
  23.9 2.2 %collective-permute-start = (bf16[128,1664]{1,0:T(8,128)(2,1)S(1)}, bf16[128,1664]{1,0:T(8,128)(2,1)S(1)}, u32[]{:S(2)}, u32[]{:S(2)}) collective-permute-start(bf16[128,1664]{1,0:T(8,128)(2,1)S(1)} %get-tuple-element.16), channel_id=1, source_target_pairs={{0,1},{1,2},{2,3},{3,0},{4,5},{5,6},{6,7},{7,4},{8,9},{9,10},{10,1... | collective-permute-start | bytes 1277960 | tf_op jit(solution)/shard_map/ppermute | solution.py:370
  26.1 5.5 %feed.7 = (bf16[128,1664]{1,0:T(8,128)(2,1)S(1)}, bf16[128,1664]{1,0:T(8,128)(2,1)S(1)}) custom-call(bf16[4,256,1664]{2,1,0:T(8,128)(2,1)S(1)} %bitcast.14, bf16[1024,1664]{1,0:T(8,128)(2,1)S(1)} %copy-done.1, f32[1,1024]{1,0:T(1,128)S(1)} %bitcast.21, bf16[1024,1664]{1,0:T(8,128)(2,1)S(1)} %copy-done.2), custom_call_target="tpu_custom_call" | custom-call | flops 1744830464 | bytes 10223616 | tf_op jit(solution)/shard_map/feed/pallas_call | solution.py:138
  31.6 0.0 copy-start.12
  31.6 1.5 %collective-permute-start.2 = (bf16[128,1664]{1,0:T(8,128)(2,1)S(1)}, bf16[128,1664]{1,0:T(8,128)(2,1)S(1)}, u32[]{:S(2)}, u32[]{:S(2)}) collective-permute-start(bf16[128,1664]{1,0:T(8,128)(2,1)S(1)} %get-tuple-element.18), channel_id=1, source_target_pairs={{0,3},{1,0},{2,1},{3,2},{4,7},{5,4},{6,5},{7,6},{8,11},{9,8},{10,9... | collective-permute-start | bytes 1277960 | tf_op jit(solution)/shard_map/ppermute | solution.py:375
  33.1 5.5 %feed.6 = (bf16[128,1664]{1,0:T(8,128)(2,1)S(1)}, bf16[128,1664]{1,0:T(8,128)(2,1)S(1)}) custom-call(bf16[4,256,1664]{2,1,0:T(8,128)(2,1)S(1)} %bitcast.15, bf16[1024,1664]{1,0:T(8,128)(2,1)S(1)} %copy-done.1, f32[1,1024]{1,0:T(1,128)S(1)} %bitcast.22, bf16[1024,1664]{1,0:T(8,128)(2,1)S(1)} %copy-done.2), custom_call_target="tpu_custom_call" | custom-call | flops 1744830464 | bytes 10223616 | tf_op jit(solution)/shard_map/feed/pallas_call | solution.py:138
  38.6 0.1 collective-permute-start.3
  38.7 2.7 %collective-permute-start.4 = (bf16[128,1664]{1,0:T(8,128)(2,1)S(1)}, bf16[128,1664]{1,0:T(8,128)(2,1)S(1)}, u32[]{:S(2)}, u32[]{:S(2)}) collective-permute-start(bf16[128,1664]{1,0:T(8,128)(2,1)S(1)} %get-tuple-element.20), channel_id=1, source_target_pairs={{0,3},{1,0},{2,1},{3,2},{4,7},{5,4},{6,5},{7,6},{8,11},{9,8},{10,9... | collective-permute-start | bytes 1277960 | tf_op jit(solution)/shard_map/ppermute | solution.py:371
  41.4 0.1 add_convert_fusion.1
  41.5 0.1 collective-permute-start.1
  41.6 9.7 %collective-permute-done.4 = bf16[128,1664]{1,0:T(8,128)(2,1)S(1)} collective-permute-done((bf16[128,1664]{1,0:T(8,128)(2,1)S(1)}, bf16[128,1664]{1,0:T(8,128)(2,1)S(1)}, u32[]{:S(2)}, u32[]{:S(2)}) %collective-permute-start.4) | collective-permute-done | bytes 426016 | tf_op jit(solution)/shard_map/ppermute | solution.py:371
  51.3 0.1 add_convert_fusion
  51.4 3.2 %collective-permute-start.5 = (bf16[128,1664]{1,0:T(8,128)(2,1)S(1)}, bf16[128,1664]{1,0:T(8,128)(2,1)S(1)}, u32[]{:S(2)}, u32[]{:S(2)}) collective-permute-start(bf16[128,1664]{1,0:T(8,128)(2,1)S(1)} %add_convert_fusion), channel_id=1, source_target_pairs={{0,3},{1,0},{2,1},{3,2},{4,7},{5,4},{6,5},{7,6},{8,11},{9,8},{10,9... | collective-permute-start | bytes 1277960 | tf_op jit(solution)/shard_map/ppermute | solution.py:381
  54.6 0.0 slice-start
  54.6 5.6 %feed.4.base_ref = f32[256,1664]{1,0:T(8,128)S(1)} custom-call(bf16[4,256,1664]{2,1,0:T(8,128)(2,1)S(1)} %bitcast.16, bf16[1024,1664]{1,0:T(8,128)(2,1)S(1)} %copy-done.1, f32[1,1024]{1,0:T(1,128)S(1)} %bitcast.23, bf16[1024,1664]{1,0:T(8,128)(2,1)S(1)} %copy-done.3, bf16[256,1664]{1,0:T(8,128)(2,1)S(1)} %bitcast.19, f32[1,1664]{1,0:T(1,128)S(1)} %reshape.62.down_bias_ref), custom_call_target="tpu_custom_call" | custom-call | flops 1744830464 | bytes 10223616 | tf_op jit(solution)/shard_map/feed/pallas_call | solution.py:138
  60.3 0.0 copy-start.7
  60.3 0.0 copy-start.8
  60.3 0.0 copy-start.9
  60.4 2.1 %collective-permute-done.5.b2_ref = bf16[128,1664]{1,0:T(8,128)(2,1)S(1)} collective-permute-done((bf16[128,1664]{1,0:T(8,128)(2,1)S(1)}, bf16[128,1664]{1,0:T(8,128)(2,1)S(1)}, u32[]{:S(2)}, u32[]{:S(2)}) %collective-permute-start.5) | collective-permute-done | bytes 426016 | tf_op jit(solution)/shard_map/ppermute | solution.py:381
  62.4 2.1 %project.1 = (bf16[64,1664]{1,0:T(8,128)(2,1)S(1)}, bf16[64,1664]{1,0:T(8,128)(2,1)S(1)}, bf16[64,1664]{1,0:T(8,128)(2,1)S(1)}, f32[64,1664]{1,0:T(8,128)S(1)}) custom-call(s32[1]{0:T(128)} %bitcast.lane_ref, f32[256,1664]{1,0:T(8,128)S(1)} %feed.4.base_ref, bf16[128,1664]{1,0:T(8,128)(2,1)S(1)} %collective-permute-done.1.a1_ref, ...), custom_call_target="tpu_custom_call" | custom-call | flops 1417674752 | bytes 10649600 | tf_op jit(solution)/shard_map/project/pallas_call | solution.py:174
  64.6 1.9 %collective-permute-start.6 = (bf16[64,1664]{1,0:T(8,128)(2,1)S(1)}, bf16[64,1664]{1,0:T(8,128)(2,1)S(1)}, u32[]{:S(2)}, u32[]{:S(2)}) collective-permute-start(bf16[64,1664]{1,0:T(8,128)(2,1)S(1)} %get-tuple-element.23), channel_id=1, source_target_pairs={{0,2},{1,3},{2,0},{3,1},{4,6},{5,7},{6,4},{7,5},{8,10},{9,11},{10,... | collective-permute-start | bytes 638984 | tf_op jit(solution)/shard_map/ppermute | solution.py:392
  66.5 2.3 %collective-permute-start.7 = (bf16[64,1664]{1,0:T(8,128)(2,1)S(1)}, bf16[64,1664]{1,0:T(8,128)(2,1)S(1)}, u32[]{:S(2)}, u32[]{:S(2)}) collective-permute-start(bf16[64,1664]{1,0:T(8,128)(2,1)S(1)} %get-tuple-element.24), channel_id=1, source_target_pairs={{0,1},{1,2},{2,3},{3,0},{4,5},{5,6},{6,7},{7,4},{8,9},{9,10},{10,1... | collective-permute-start | bytes 638984 | tf_op jit(solution)/shard_map/ppermute | solution.py:393
  68.7 0.4 collective-permute-start.8
  69.1 1.8 %collective-permute-done.6.r0 = bf16[64,1664]{1,0:T(8,128)(2,1)S(1)} collective-permute-done((bf16[64,1664]{1,0:T(8,128)(2,1)S(1)}, bf16[64,1664]{1,0:T(8,128)(2,1)S(1)}, u32[]{:S(2)}, u32[]{:S(2)}) %collective-permute-start.6) | collective-permute-done | bytes 213024 | tf_op jit(solution)/shard_map/ppermute | solution.py:392
  70.9 5.7 %collective-permute-done.7.r1 = bf16[64,1664]{1,0:T(8,128)(2,1)S(1)} collective-permute-done((bf16[64,1664]{1,0:T(8,128)(2,1)S(1)}, bf16[64,1664]{1,0:T(8,128)(2,1)S(1)}, u32[]{:S(2)}, u32[]{:S(2)}) %collective-permute-start.7) | collective-permute-done | bytes 213024 | tf_op jit(solution)/shard_map/ppermute | solution.py:393
  76.6 0.2 collective-permute-done.8.r2
  76.8 0.4 route.1
  77.2 0.9 all_to_all.7
  78.1 10.4 %all-to-all-start = ((bf16[32,4,1792]{2,1,0:T(4,128)(2,1)}), bf16[32,4,1792]{2,1,0:T(4,128)(2,1)S(1)}, u32[]{:S(2)}, u32[]{:S(2)}) async-start(bf16[32,4,1792]{2,1,0:T(4,128)(2,1)} %all_to_all.7), calls=%async_computation | async-start | bytes 917504 | tf_op jit(solution)/shard_map/all_to_all | solution.py:397
  88.6 10.8 %all-to-all-done = bf16[32,4,1792]{2,1,0:T(4,128)(2,1)S(1)} async-done(((bf16[32,4,1792]{2,1,0:T(4,128)(2,1)}), bf16[32,4,1792]{2,1,0:T(4,128)(2,1)S(1)}, u32[]{:S(2)}, u32[]{:S(2)}) %all-to-all-start) | async-done | bytes 458784 | tf_op jit(solution)/shard_map/all_to_all | solution.py:397
  99.4 0.1 all_to_all.9.got_ref
  99.5 0.0 all-gather.2.cloned.1.call-done
  99.5 18.6 %reshape.70.weight_ref = bf16[1664,4992]{1,0:T(8,128)(2,1)} reshape(bf16[32,52,4992]{2,1,0:T(8,128)(2,1)} %bitcast.29) | data formatting | bytes 33226752 | tf_op jit(solution)/shard_map/reshape | solution.py:363
  118.1 5.7 %copy-done = bf16[1664,4992]{1,0:T(8,128)(2,1)S(1)} copy-done((bf16[1664,4992]{1,0:T(8,128)(2,1)S(1)}, bf16[1664,4992]{1,0:T(8,128)(2,1)}, u32[]{:S(2)}) %copy-start) | copy-done | bytes 16613400
  123.8 7.9 %attend.1 = (bf16[128,1664]{1,0:T(8,128)(2,1)}, bf16[128,1664]{1,0:T(8,128)(2,1)}) custom-call(bf16[128,1792]{1,0:T(8,128)(2,1)S(1)} %all_to_all.9.got_ref, f32[1,1664]{1,0:T(1,128)S(1)} %reshape.66.gain_ref, f32[1,1664]{1,0:T(1,128)S(1)} %reshape.67.bias_ref, bf16[1664,4992]{1,0:T(8,128)(2,1)S(1)} %copy-done), custom_call_target="tpu_custom_call" | custom-call | flops 2126512128 | bytes 16613376 | tf_op jit(solution)/shard_map/attend/pallas_call | solution.py:316
  (32 shorter events, 0.1 us)
Async XLA Ops:
  7.2 2.7 %copy-start.10 = (f32[1664]{0:T(1024)S(1)}, f32[1664]{0:T(1024)}, u32[]{:S(2)}) copy-start(f32[1664]{0:T(1024)} %param.20) | copy-start | bytes 19972
  7.2 2.7 %copy-start.11 = (f32[1664]{0:T(1024)S(1)}, f32[1664]{0:T(1024)}, u32[]{:S(2)}) copy-start(f32[1664]{0:T(1024)} %param.21) | copy-start | bytes 19972
  7.2 2.7 %copy-start.6 = (s32[1024]{0:T(1024)S(1)}, s32[1024]{0:T(1024)}, u32[]{:S(2)}) copy-start(s32[1024]{0:T(1024)} %param.18) | copy-start | bytes 12292
  7.2 92.3 %all-gather.2.cloned.1.call-start = ((), (), s32[]{:S(2)}) async-start(), calls=%async_computation.1 | async-start | bytes 18450432 | tf_op jit(solution)/shard_map/all_gather | solution.py:362
  8.6 7.8 %copy-start.5 = (f32[1024]{0:T(1024)S(1)}, f32[1024]{0:T(1024)}, u32[]{:S(2)}) copy-start(f32[1024]{0:T(1024)} %param.23) | copy-start | bytes 12292
  8.9 7.5 %copy-start.1 = (bf16[1024,1664]{1,0:T(8,128)(2,1)S(1)}, bf16[1024,1664]{1,0:T(8,128)(2,1)}, u32[]{:S(2)}) copy-start(bf16[1024,1664]{1,0:T(8,128)(2,1)} %up_ref.7) | copy-start | bytes 10223620
  9.9 2.2 %copy-start.4 = (bf16[1024,1664]{1,0:T(8,128)(2,1)S(1)}, bf16[1024,1664]{1,0:T(8,128)(2,1)}, u32[]{:S(2)}) copy-start(bf16[1024,1664]{1,0:T(8,128)(2,1)} %rows_ref.1) | copy-start | bytes 10223620
  16.4 2.0 %copy-start.2 = (bf16[1024,1664]{1,0:T(8,128)(2,1)S(1)}, bf16[1024,1664]{1,0:T(8,128)(2,1)}, u32[]{:S(2)}) copy-start(bf16[1024,1664]{1,0:T(8,128)(2,1)} %down_ref.7) | copy-start | bytes 10223620
  23.9 17.5 %collective-permute-start = (bf16[128,1664]{1,0:T(8,128)(2,1)S(1)}, bf16[128,1664]{1,0:T(8,128)(2,1)S(1)}, u32[]{:S(2)}, u32[]{:S(2)}) collective-permute-start(bf16[128,1664]{1,0:T(8,128)(2,1)S(1)} %get-tuple-element.16), channel_id=1, source_target_pairs={{0,1},{1,2},{2,3},{3,0},{4,5},{5,6},{6,7},{7,4},{8,9},{9,10},{10,1... | collective-permute-start | bytes 1277960 | tf_op jit(solution)/shard_map/ppermute | solution.py:370
  31.6 23.0 %copy-start.12 = (f32[1664]{0:T(1024)S(1)}, f32[1664]{0:T(1024)}, u32[]{:S(2)}) copy-start(f32[1664]{0:T(1024)} %param.25) | copy-start | bytes 19972
  31.6 28.7 %collective-permute-start.2 = (bf16[128,1664]{1,0:T(8,128)(2,1)S(1)}, bf16[128,1664]{1,0:T(8,128)(2,1)S(1)}, u32[]{:S(2)}, u32[]{:S(2)}) collective-permute-start(bf16[128,1664]{1,0:T(8,128)(2,1)S(1)} %get-tuple-element.18), channel_id=1, source_target_pairs={{0,3},{1,0},{2,1},{3,2},{4,7},{5,4},{6,5},{7,6},{8,11},{9,8},{10,9... | collective-permute-start | bytes 1277960 | tf_op jit(solution)/shard_map/ppermute | solution.py:375
  33.1 21.5 %copy-start.3 = (bf16[1024,1664]{1,0:T(8,128)(2,1)S(1)}, bf16[1024,1664]{1,0:T(8,128)(2,1)}, u32[]{:S(2)}) copy-start(bf16[1024,1664]{1,0:T(8,128)(2,1)} %down_ref.7) | copy-start | bytes 10223620
  38.6 21.7 %collective-permute-start.3 = (bf16[128,1664]{1,0:T(8,128)(2,1)S(1)}, bf16[128,1664]{1,0:T(8,128)(2,1)S(1)}, u32[]{:S(2)}, u32[]{:S(2)}) collective-permute-start(bf16[128,1664]{1,0:T(8,128)(2,1)S(1)} %get-tuple-element.19), channel_id=1, source_target_pairs={{0,1},{1,2},{2,3},{3,0},{4,5},{5,6},{6,7},{7,4},{8,9},{9,10},{10,1... | collective-permute-start | bytes 1277960 | tf_op jit(solution)/shard_map/ppermute | solution.py:373
  38.7 12.6 %collective-permute-start.4 = (bf16[128,1664]{1,0:T(8,128)(2,1)S(1)}, bf16[128,1664]{1,0:T(8,128)(2,1)S(1)}, u32[]{:S(2)}, u32[]{:S(2)}) collective-permute-start(bf16[128,1664]{1,0:T(8,128)(2,1)S(1)} %get-tuple-element.20), channel_id=1, source_target_pairs={{0,3},{1,0},{2,1},{3,2},{4,7},{5,4},{6,5},{7,6},{8,11},{9,8},{10,9... | collective-permute-start | bytes 1277960 | tf_op jit(solution)/shard_map/ppermute | solution.py:371
  41.5 18.9 %collective-permute-start.1 = (bf16[128,1664]{1,0:T(8,128)(2,1)S(1)}, bf16[128,1664]{1,0:T(8,128)(2,1)S(1)}, u32[]{:S(2)}, u32[]{:S(2)}) collective-permute-start(bf16[128,1664]{1,0:T(8,128)(2,1)S(1)} %add_convert_fusion.1), channel_id=1, source_target_pairs={{0,1},{1,2},{2,3},{3,0},{4,5},{5,6},{6,7},{7,4},{8,9},{9,10},{10,1... | collective-permute-start | bytes 1277960 | tf_op jit(solution)/shard_map/ppermute | solution.py:380
  51.4 11.0 %collective-permute-start.5 = (bf16[128,1664]{1,0:T(8,128)(2,1)S(1)}, bf16[128,1664]{1,0:T(8,128)(2,1)S(1)}, u32[]{:S(2)}, u32[]{:S(2)}) collective-permute-start(bf16[128,1664]{1,0:T(8,128)(2,1)S(1)} %add_convert_fusion), channel_id=1, source_target_pairs={{0,3},{1,0},{2,1},{3,2},{4,7},{5,4},{6,5},{7,6},{8,11},{9,8},{10,9... | collective-permute-start | bytes 1277960 | tf_op jit(solution)/shard_map/ppermute | solution.py:381
  54.6 7.8 %slice-start = ((s8[5537792]{0:T(1024)(128)(4,1)}), s8[4194304]{0:T(1024)(128)(4,1)S(1)}, s32[]{:S(2)}) async-start(s8[5537792]{0:T(1024)(128)(4,1)} %bitcast.17), calls=%async_computation.2 | async-start | bytes 8388608
  54.6 7.8 %slice-start.1 = ((s8[5537792]{0:T(1024)(128)(4,1)}), s8[1343488]{0:T(1024)(128)(4,1)S(1)}, s32[]{:S(2)}) async-start(s8[5537792]{0:T(1024)(128)(4,1)} %bitcast.17), calls=%async_computation.3 | async-start | bytes 2686976
  60.3 16.6 %copy-start.7 = (s32[1024]{0:T(1024)S(1)}, s32[1024]{0:T(1024)}, u32[]{:S(2)}) copy-start(s32[1024]{0:T(1024)} %param.19) | copy-start | bytes 12292
  60.3 16.6 %copy-start.8 = (s32[32]{0:T(128)S(1)}, s32[32]{0:T(128)}, u32[]{:S(2)}) copy-start(s32[32]{0:T(128)} %param.16) | copy-start | bytes 388
  60.3 16.5 %copy-start.9 = (s32[32]{0:T(128)S(1)}, s32[32]{0:T(128)}, u32[]{:S(2)}) copy-start(s32[32]{0:T(128)} %param.17) | copy-start | bytes 388
  60.3 28.3 %copy-start.13 = (f32[1664]{0:T(1024)S(1)}, f32[1664]{0:T(1024)}, u32[]{:S(2)}) copy-start(f32[1664]{0:T(1024)} %param.27) | copy-start | bytes 19972
  60.3 28.3 %copy-start.14 = (f32[1664]{0:T(1024)S(1)}, f32[1664]{0:T(1024)}, u32[]{:S(2)}) copy-start(f32[1664]{0:T(1024)} %param.28) | copy-start | bytes 19972
  64.6 6.4 %collective-permute-start.6 = (bf16[64,1664]{1,0:T(8,128)(2,1)S(1)}, bf16[64,1664]{1,0:T(8,128)(2,1)S(1)}, u32[]{:S(2)}, u32[]{:S(2)}) collective-permute-start(bf16[64,1664]{1,0:T(8,128)(2,1)S(1)} %get-tuple-element.23), channel_id=1, source_target_pairs={{0,2},{1,3},{2,0},{3,1},{4,6},{5,7},{6,4},{7,5},{8,10},{9,11},{10,... | collective-permute-start | bytes 638984 | tf_op jit(solution)/shard_map/ppermute | solution.py:392
  66.5 10.2 %collective-permute-start.7 = (bf16[64,1664]{1,0:T(8,128)(2,1)S(1)}, bf16[64,1664]{1,0:T(8,128)(2,1)S(1)}, u32[]{:S(2)}, u32[]{:S(2)}) collective-permute-start(bf16[64,1664]{1,0:T(8,128)(2,1)S(1)} %get-tuple-element.24), channel_id=1, source_target_pairs={{0,1},{1,2},{2,3},{3,0},{4,5},{5,6},{6,7},{7,4},{8,9},{9,10},{10,1... | collective-permute-start | bytes 638984 | tf_op jit(solution)/shard_map/ppermute | solution.py:393
  68.7 8.1 %collective-permute-start.8 = (bf16[64,1664]{1,0:T(8,128)(2,1)S(1)}, bf16[64,1664]{1,0:T(8,128)(2,1)S(1)}, u32[]{:S(2)}, u32[]{:S(2)}) collective-permute-start(bf16[64,1664]{1,0:T(8,128)(2,1)S(1)} %get-tuple-element.25), channel_id=1, source_target_pairs={{0,3},{1,0},{2,1},{3,2},{4,7},{5,4},{6,5},{7,6},{8,11},{9,8},{10,9... | collective-permute-start | bytes 638984 | tf_op jit(solution)/shard_map/ppermute | solution.py:394
  78.1 21.3 %all-to-all-start = ((bf16[32,4,1792]{2,1,0:T(4,128)(2,1)}), bf16[32,4,1792]{2,1,0:T(4,128)(2,1)S(1)}, u32[]{:S(2)}, u32[]{:S(2)}) async-start(bf16[32,4,1792]{2,1,0:T(4,128)(2,1)} %all_to_all.7), calls=%async_computation | async-start | bytes 917504 | tf_op jit(solution)/shard_map/all_to_all | solution.py:397
  118.1 5.7 %copy-start = (bf16[1664,4992]{1,0:T(8,128)(2,1)S(1)}, bf16[1664,4992]{1,0:T(8,128)(2,1)}, u32[]{:S(2)}) copy-start(bf16[1664,4992]{1,0:T(8,128)(2,1)} %reshape.70.weight_ref) | copy-start | bytes 49840132
Sparse Core Ops, SparseCore 0:
  10.4 78.8 all-gather.1

commit v2 on v1

v2 whole, which is shorter than its diff:
```python
import math

import jax
import jax.numpy as jnp
from jax import lax
from jax.experimental import pallas as pl
from jax.experimental.pallas import tpu as pltpu
from jax.sharding import PartitionSpec as P

HEAD_DIM = 104
EPSILON = 1e-06
MIB = 1 << 20


def normalise(values, gain, bias):
    mean_value = jnp.mean(values, axis=-1, keepdims=True)
    centred = values - mean_value
    spread = jnp.mean(centred * centred, axis=-1, keepdims=True)
    return centred * lax.rsqrt(spread + EPSILON) * gain + bias


def relative_offset(step):
    return jnp.where(step == 0, 2, jnp.where(step == 1, 1, jnp.where(step == 2, 3, 0)))


def gelu(value):
    return 0.5 * value * (1.0 + lax.erf(value * (1.0 / math.sqrt(2.0))))


def feed_tiles(rows, up_ref, up_bias_ref, down_ref, wait=None, tile=256):
    total = None
    for at in range(0, up_ref.shape[0], tile):
        if wait is not None:
            wait(at // tile)
        upward = lax.dot_general(
            rows,
            up_ref[at : at + tile],
            (((1,), (1,)), ((), ())),
            preferred_element_type=jnp.float32,
        )
        hidden = gelu(upward + up_bias_ref[:, at : at + tile]).astype(jnp.bfloat16)
        part = jnp.dot(hidden, down_ref[at : at + tile], preferred_element_type=jnp.float32)
        total = part if total is None else total + part
    return total


def first_kernel(
    lane_ref,
    rows_hbm,
    dest_ref,
    gain_ref,
    bias_ref,
    up_hbm,
    up_bias_ref,
    down_hbm,
    first_ref,
    second_ref,
    normed_ref,
    own_ref,
    rows_ref,
    up_ref,
    down_ref,
    far_ref,
    row_sems,
    up_sems,
    down_sems,
):
    lane = lane_ref[0]
    count = rows_hbm.shape[0] // 4
    part = count // 4
    tile = up_hbm.shape[0] // 4

    def copies(source, target, sems, size):
        return [
            pltpu.make_async_copy(
                source.at[pl.ds(i * size, size)], target.at[pl.ds(i * size, size)], sems.at[i]
            )
            for i in range(4)
        ]

    row_copies = copies(rows_hbm, rows_ref, row_sems, count)
    up_copies = copies(up_hbm, up_ref, up_sems, tile)
    down_copies = copies(down_hbm, down_ref, down_sems, tile)
    for copy in row_copies:
        copy.start()
    for i in range(4):
        up_copies[i].start()
        down_copies[i].start()
    index = lax.broadcasted_iota(jnp.int32, (count, count), 0)
    step = index // part
    wanted = 4 * (index - step * part) + ((lane + relative_offset(step)) & 3)
    for b in range(4):
        row_copies[b].wait()
        rows = rows_ref[b * count : (b + 1) * count]
        normed = normalise(rows.astype(jnp.float32), gain_ref[...], bias_ref[...])
        hits = jnp.where(dest_ref[b] == wanted, 1.0, 0.0).astype(jnp.bfloat16)
        moved = jnp.dot(
            hits, normed.astype(jnp.bfloat16), preferred_element_type=jnp.float32
        ).astype(jnp.bfloat16)
        far_ref[b * part : (b + 1) * part] = moved[:part]
        for k in range(3):
            normed_ref[k, b * part : (b + 1) * part] = moved[(k + 1) * part : (k + 2) * part]
        own_ref[b * part : (b + 1) * part] = jnp.dot(
            hits[3 * part :], rows, preferred_element_type=jnp.float32
        ).astype(jnp.bfloat16)

    def wait(i):
        up_copies[i].wait()
        down_copies[i].wait()

    total = feed_tiles(far_ref[...], up_ref, up_bias_ref, down_ref, wait, tile)
    half = count // 2
    first_ref[...] = total[:half].astype(jnp.bfloat16)
    second_ref[...] = total[half:].astype(jnp.bfloat16)


VMEM = pl.BlockSpec(memory_space=pltpu.VMEM)
SMEM = pl.BlockSpec(memory_space=pltpu.SMEM)
HBM = pl.BlockSpec(memory_space=pltpu.HBM)


def first(lane, residual_in, merge_dest, gain, bias, up_weight, up_bias, down_weight):
    group_rows, width = residual_in.shape
    count = group_rows // 4
    half = count // 2
    bf16 = jnp.bfloat16
    return pl.pallas_call(
        first_kernel,
        in_specs=[SMEM, HBM, VMEM, VMEM, VMEM, HBM, VMEM, HBM],
        out_specs=[VMEM] * 4,
        out_shape=[
            jax.ShapeDtypeStruct((half, width), bf16),
            jax.ShapeDtypeStruct((half, width), bf16),
            jax.ShapeDtypeStruct((3, count, width), bf16),
            jax.ShapeDtypeStruct((count, width), bf16),
        ],
        scratch_shapes=[
            pltpu.VMEM(residual_in.shape, bf16),
            pltpu.VMEM(up_weight.shape, bf16),
            pltpu.VMEM(down_weight.shape, bf16),
            pltpu.VMEM((count, width), bf16),
            pltpu.SemaphoreType.DMA((4,)),
            pltpu.SemaphoreType.DMA((4,)),
            pltpu.SemaphoreType.DMA((4,)),
        ],
        compiler_params=pltpu.CompilerParams(vmem_limit_bytes=32 * MIB),
        cost_estimate=FEED_COST,
        name="first",
    )(lane, residual_in, merge_dest.reshape(4, 1, count), gain, bias, up_weight, up_bias, down_weight)


def feed_kernel(rows_ref, up_ref, up_bias_ref, down_ref, first_ref, second_ref):
    total = feed_tiles(rows_ref[...], up_ref, up_bias_ref, down_ref)
    half = first_ref.shape[0]
    first_ref[...] = total[:half].astype(jnp.bfloat16)
    second_ref[...] = total[half:].astype(jnp.bfloat16)


def feed_own_kernel(
    rows_ref, up_ref, up_bias_ref, down_ref, residual_ref, down_bias_ref, out_ref
):
    total = feed_tiles(rows_ref[...], up_ref, up_bias_ref, down_ref)
    out_ref[...] = total + (residual_ref[...].astype(jnp.float32) + down_bias_ref[...])


FEED_COST = pl.CostEstimate(flops=7 << 28, bytes_accessed=1 << 22, transcendentals=0)


def feed(rows, step, up_weight, up_bias, down_weight, extra=None):
    _, count, width = rows.shape
    args = [rows, up_weight, up_bias, down_weight]
    if extra is None:
        half = count // 2
        out_shape = [jax.ShapeDtypeStruct((half, width), jnp.bfloat16)] * 2
        kernel = feed_kernel
    else:
        args += list(extra)
        out_shape = jax.ShapeDtypeStruct((count, width), jnp.float32)
        kernel = feed_own_kernel

    def wrapped(rows_ref, *refs):
        kernel(rows_ref.at[step], *refs)

    return pl.pallas_call(
        wrapped,
        in_specs=[VMEM] * len(args),
        out_specs=[VMEM] * 2 if extra is None else VMEM,
        out_shape=out_shape,
        compiler_params=pltpu.CompilerParams(vmem_limit_bytes=16 * MIB),
        cost_estimate=FEED_COST,
        name="feed",
    )(*args)


def project_kernel(
    lane_ref, base_ref, a1_ref, a2_ref, b1_ref, b2_ref, weight_ref, o0, o1, o2, own, total_ref
):
    half = a1_ref.shape[0]
    part = half // 2
    top = base_ref[:half] + a1_ref[...].astype(jnp.float32) + a2_ref[...].astype(jnp.float32)
    low = base_ref[half:] + b1_ref[...].astype(jnp.float32) + b2_ref[...].astype(jnp.float32)
    rows = jnp.concatenate([top, low], axis=0).astype(jnp.bfloat16)
    total_ref[...] = jnp.dot(rows, weight_ref[...], preferred_element_type=jnp.float32)
    lane = lane_ref[0]
    for offset, ref in ((2, o0), (1, o1), (3, o2), (0, own)):
        start = pl.multiple_of(((lane + offset) & 3) * part, part)
        ref[...] = total_ref[pl.ds(start, part)].astype(ref.dtype)


def project(lane, base, a1, a2, b1, b2, weight):
    count, width = base.shape
    part = count // 4
    vmem = pl.BlockSpec(memory_space=pltpu.VMEM)
    return pl.pallas_call(
        project_kernel,
        in_specs=[pl.BlockSpec(memory_space=pltpu.SMEM)] + [vmem] * 6,
        out_specs=[vmem] * 4,
        out_shape=[jax.ShapeDtypeStruct((part, width), jnp.bfloat16)] * 3
        + [jax.ShapeDtypeStruct((part, width), jnp.float32)],
        scratch_shapes=[pltpu.VMEM((count, width), jnp.float32)],
        compiler_params=pltpu.CompilerParams(vmem_limit_bytes=24 * MIB),
        cost_estimate=pl.CostEstimate(
            flops=2 * count * width * width,
            bytes_accessed=2 * width * width + 12 * count * width,
            transcendentals=0,
        ),
        name="project",
    )(lane, base, a1, a2, b1, b2, weight)


def turn(column):
    count = column.shape[0]
    same = lax.broadcasted_iota(jnp.int32, (count, count), 0) == lax.broadcasted_iota(
        jnp.int32, (count, count), 1
    )
    return jnp.sum(jnp.where(same, column, 0), axis=0, keepdims=True)


def route_kernel(
    lane_ref, own_ref, r0, r1, r2, counts_ref, owners_ref, dest_ref, seg_ref, out_ref
):
    lane = lane_ref[0]
    rows, width = own_ref.shape
    pieces = counts_ref.shape[1]
    slots = 2 * rows // pieces
    projected = (
        own_ref[...]
        + r0[...].astype(jnp.float32)
        + r1[...].astype(jnp.float32)
        + r2[...].astype(jnp.float32)
    ).astype(jnp.bfloat16)
    counts = counts_ref[...] // 4
    earlier = lax.broadcasted_iota(jnp.int32, (pieces, pieces), 1) < lax.broadcasted_iota(
        jnp.int32, (pieces, pieces), 0
    )
    starts = jnp.sum(jnp.where(earlier, counts, 0), axis=1, keepdims=True)
    upto = earlier | (
        lax.broadcasted_iota(jnp.int32, (pieces, pieces), 1)
        == lax.broadcasted_iota(jnp.int32, (pieces, pieces), 0)
    )
    ends = jnp.sum(jnp.where(upto, counts, 0), axis=1, keepdims=True)
    index = lax.broadcasted_iota(jnp.int32, (pieces, rows), 1)
    inside = (index >= starts) & (index < ends)
    owner_col = jnp.sum(
        jnp.where(
            lax.broadcasted_iota(jnp.int32, (pieces, pieces), 0)
            == lax.broadcasted_iota(jnp.int32, (pieces, pieces), 1),
            owners_ref[...],
            0,
        ),
        axis=1,
        keepdims=True,
    )
    target = jnp.sum(jnp.where(inside, owner_col * slots - starts, 0), axis=0, keepdims=True)
    target = target + lax.broadcasted_iota(jnp.int32, (1, rows), 1)
    out_rows = pieces * slots
    hits = lax.broadcasted_iota(jnp.int32, (out_rows, rows), 0) == target
    moved = jnp.dot(
        jnp.where(hits, 1.0, 0.0).astype(jnp.bfloat16),
        projected,
        preferred_element_type=jnp.float32,
    ).astype(jnp.bfloat16)
    dest = dest_ref[lane]
    seg = seg_ref[lane]
    tokens = dest.shape[1]
    first = dest == 4 * lax.broadcasted_iota(jnp.int32, (rows, tokens), 0)
    marks = turn(jnp.sum(jnp.where(first, seg, 0), axis=1, keepdims=True)) + 1
    tags = jnp.sum(jnp.where(hits, marks, 0), axis=1, keepdims=True)
    out_ref[:, :width] = moved
    out_ref[:, width:] = jnp.broadcast_to(
        tags.astype(jnp.float32), (out_rows, out_ref.shape[1] - width)
    ).astype(jnp.bfloat16)


def route(lane, own, others, lengths, owners, merge_dest, segment_ids):
    rows, width = own.shape
    pieces = lengths.shape[0]
    block = merge_dest.shape[0] // 4
    vmem = pl.BlockSpec(memory_space=pltpu.VMEM)
    return pl.pallas_call(
        route_kernel,
        in_specs=[pl.BlockSpec(memory_space=pltpu.SMEM)] + [vmem] * 8,
        out_specs=vmem,
        out_shape=jax.ShapeDtypeStruct((2 * rows, width + 128), jnp.bfloat16),
        compiler_params=pltpu.CompilerParams(vmem_limit_bytes=24 * MIB),
        name="route",
    )(
        lane,
        own,
        *others,
        lengths.reshape(1, pieces),
        owners.reshape(1, pieces),
        merge_dest.reshape(4, 1, block),
        segment_ids.reshape(4, 1, block),
    )


def pack_kernel(core_ref, weight_ref, keep_ref, send_ref):
    core = core_ref[0]
    parts, _, width = weight_ref.shape
    half = width // 2
    keep_ref[:, parts * half :] = jnp.zeros_like(keep_ref[:, parts * half :])
    send_ref[:, parts * half :] = jnp.zeros_like(send_ref[:, parts * half :])
    for part in range(parts):
        low = weight_ref[part, :, :half]
        high = weight_ref[part, :, half:]
        at = slice(part * half, (part + 1) * half)

        @pl.when(core == 0)
        def _():
            keep_ref[:, at] = low
            send_ref[:, at] = high

        @pl.when(core == 1)
        def _():
            keep_ref[:, at] = high
            send_ref[:, at] = low


def pack(core, weight):
    parts, depth, width = weight.shape
    columns = parts * width // 2 + 64
    return pl.pallas_call(
        pack_kernel,
        in_specs=[SMEM, VMEM],
        out_specs=[VMEM] * 2,
        out_shape=[jax.ShapeDtypeStruct((depth, columns), jnp.bfloat16)] * 2,
        compiler_params=pltpu.CompilerParams(vmem_limit_bytes=8 * MIB),
        name="pack",
    )(core, weight)


def pair_kernel(core_ref, own_ref, other_ref, *out_refs):
    core = core_ref[0]
    depth = own_ref.shape[0]
    size = out_refs[0].shape[2]
    index = lax.broadcasted_iota(jnp.int32, (2 * depth, depth), 0)
    column = lax.broadcasted_iota(jnp.int32, (2 * depth, depth), 1)
    own_hits = jnp.where(index == column + core * depth, 1.0, 0.0).astype(jnp.bfloat16)
    other_hits = jnp.where(index == column + (1 - core) * depth, 1.0, 0.0).astype(jnp.bfloat16)
    both = jnp.dot(own_hits, own_ref[...], preferred_element_type=jnp.float32) + jnp.dot(
        other_hits, other_ref[...], preferred_element_type=jnp.float32
    )
    both = both.astype(jnp.bfloat16)
    for i, ref in enumerate(out_refs):
        ref[0] = both[:, i * size : (i + 1) * size]


def pair(core, own, other, streams):
    depth, columns = own.shape
    return pl.pallas_call(
        pair_kernel,
        in_specs=[SMEM, VMEM, VMEM],
        out_specs=[VMEM] * streams,
        out_shape=[jax.ShapeDtypeStruct((1, 2 * depth, columns // streams), jnp.bfloat16)]
        * streams,
        compiler_params=pltpu.CompilerParams(vmem_limit_bytes=8 * MIB),
        name="pair",
    )(core, own, other)


ORDERS = ((1, 4, 3, 12), (4, 3, 12, 1), (3, 12, 1, 4), (12, 1, 4, 3))


def assemble(chip, streams, chips):
    _, depth, size = streams[0][0].shape

    def kernel(chip_ref, *refs):
        out_ref = refs[-1]
        chip_id = chip_ref[0]
        for s, order in enumerate(ORDERS):
            d1, d2, d3, d4 = order
            inner = (0, d1, d2, d2 ^ d1)
            for a, outer in enumerate((0, d3, d4, d4 ^ d3)):
                for i, mask in enumerate(inner):
                    out_ref[chip_id ^ (outer ^ mask), :, s * size : (s + 1) * size] = refs[
                        4 * s + a
                    ][i]

    flat = [array for stream in streams for array in stream]
    return pl.pallas_call(
        kernel,
        in_specs=[SMEM] + [VMEM] * len(flat),
        out_specs=VMEM,
        out_shape=jax.ShapeDtypeStruct((chips, depth, size * len(ORDERS)), jnp.bfloat16),
        compiler_params=pltpu.CompilerParams(vmem_limit_bytes=30 * MIB),
        cost_estimate=pl.CostEstimate(flops=0, bytes_accessed=1 << 24, transcendentals=0),
        name="assemble",
    )(chip, *flat)


def attention(heads_ref, base, tags, count, width, out_ref):
    tag_col = tags
    itself = lax.broadcasted_iota(jnp.int32, (count, count), 0) == lax.broadcasted_iota(
        jnp.int32, (count, count), 1
    )
    tag_row = jnp.sum(jnp.where(itself, tag_col, 0.0), axis=0, keepdims=True)
    allowed = ((tag_col == tag_row) & (tag_row > 0.5)) | itself
    live = tag_col > 0.5
    scale = 1.0 / math.sqrt(HEAD_DIM)
    rows = slice(base, base + count)
    for head in range(width // HEAD_DIM):
        at = head * HEAD_DIM
        query = heads_ref[rows, at : at + HEAD_DIM]
        keys = heads_ref[rows, width + at : width + at + HEAD_DIM]
        value = heads_ref[rows, 2 * width + at : 2 * width + at + HEAD_DIM]
        scores = (
            lax.dot_general(
                query, keys, (((1,), (1,)), ((), ())), preferred_element_type=jnp.float32
            )
            * scale
        )
        weights = jnp.where(allowed, jnp.exp(scores), 0.0)
        probs = (weights / jnp.sum(weights, axis=-1, keepdims=True)).astype(jnp.bfloat16)
        mixed = jnp.dot(probs, value, preferred_element_type=jnp.float32)
        out_ref[:, at : at + HEAD_DIM] = jnp.where(live, mixed, 0.0).astype(jnp.bfloat16)


def attend_kernel(
    core_ref,
    mine_ref,
    theirs_ref,
    gain_ref,
    bias_ref,
    weight_ref,
    merged_ref,
    other_ref,
    heads_out_ref,
    tags_ref,
    heads_ref,
):
    core = core_ref[0]
    count, width = merged_ref.shape
    target = lax.broadcasted_iota(jnp.int32, (count, count), 0)
    source = lax.broadcasted_iota(jnp.int32, (count, count), 1)
    from_mine = ((target >> 2) & 1) == core

    def one_hot(hits):
        return jnp.where(hits, 1.0, 0.0).astype(jnp.bfloat16)

    def gather(first_hits, second_hits):
        return jnp.dot(
            one_hot(first_hits), mine_ref[...], preferred_element_type=jnp.float32
        ) + jnp.dot(one_hot(second_hits), theirs_ref[...], preferred_element_type=jnp.float32)

    same = target == source
    swapped = (target ^ 4) == source
    here = gather(from_mine & same, ~from_mine & swapped)
    there = gather(from_mine & swapped, ~from_mine & same)
    merged_ref[...] = here[:, :width].astype(jnp.bfloat16)
    both = jnp.concatenate([there, here], axis=0)
    normed = normalise(both[:, :width], gain_ref[...], bias_ref[...]).astype(jnp.bfloat16)
    heads_ref[...] = jnp.dot(normed, weight_ref[...], preferred_element_type=jnp.float32).astype(
        jnp.bfloat16
    )
    heads_out_ref[...] = heads_ref[count:]
    tags_ref[...] = here[:, width:]
    attention(heads_ref, 0, there[:, width : width + 1], count, width // 2, other_ref)


def attend_own_kernel(heads_ref, tags_ref, out_ref):
    attention(heads_ref, 0, tags_ref[:, :1], *out_ref.shape, out_ref)


def finish_kernel(core_ref, mine_ref, theirs_ref, out_ref):
    core = core_ref[0]
    half = mine_ref.shape[1]

    @pl.when(core == 0)
    def _():
        out_ref[:, :half] = mine_ref[...]
        out_ref[:, half:] = theirs_ref[...]

    @pl.when(core == 1)
    def _():
        out_ref[:, :half] = theirs_ref[...]
        out_ref[:, half:] = mine_ref[...]


def attend(core, mine, theirs, gain, bias, weight, sibling):
    count = mine.shape[0]
    width, columns = weight.shape
    bf16 = jnp.bfloat16
    merged, other, heads, tags = pl.pallas_call(
        attend_kernel,
        in_specs=[SMEM] + [VMEM] * 5,
        out_specs=[VMEM] * 4,
        out_shape=[
            jax.ShapeDtypeStruct((count, width), bf16),
            jax.ShapeDtypeStruct((count, width // 2), bf16),
            jax.ShapeDtypeStruct((count, columns), bf16),
            jax.ShapeDtypeStruct((count, mine.shape[1] - width), jnp.float32),
        ],
        scratch_shapes=[pltpu.VMEM((2 * count, columns), bf16)],
        compiler_params=pltpu.CompilerParams(vmem_limit_bytes=24 * MIB),
        name="attend",
    )(core, mine, theirs, gain, bias, weight)
    other = lax.ppermute(other, "req", sibling)
    own = pl.pallas_call(
        attend_own_kernel,
        in_specs=[VMEM] * 2,
        out_specs=VMEM,
        out_shape=jax.ShapeDtypeStruct((count, width // 2), bf16),
        compiler_params=pltpu.CompilerParams(vmem_limit_bytes=12 * MIB),
        cost_estimate=pl.CostEstimate(flops=1 << 30, bytes_accessed=1 << 20, transcendentals=0),
        name="attend_own",
    )(heads, tags)
    mixed = pl.pallas_call(
        finish_kernel,
        in_specs=[SMEM, VMEM, VMEM],
        out_specs=VMEM,
        out_shape=jax.ShapeDtypeStruct((count, width), bf16),
        compiler_params=pltpu.CompilerParams(vmem_limit_bytes=4 * MIB),
        name="finish",
    )(core, own, other)
    return merged, mixed


def body(
    residual_in,
    lengths,
    owners,
    merge_dest,
    segment_ids,
    norm2_gain,
    norm2_bias,
    up_weight,
    up_bias,
    down_weight,
    down_bias,
    proj_weight,
    norm3_gain,
    norm3_bias,
    next_weight,
):
    width = residual_in.shape[1]
    lanes = lax.axis_size("mlp")
    lane = lax.axis_index("mlp").astype(jnp.int32).reshape(1)
    onward = [(i, (i + 1) % lanes) for i in range(lanes)]
    back = [(i, (i - 1) % lanes) for i in range(lanes)]
    across = [(i, (i + 2) % lanes) for i in range(lanes)]

    def row(vector):
        return vector.reshape(1, -1)

    count = residual_in.shape[0] // lanes
    bias_up = row(up_bias)
    place = lax.axis_index("req").astype(jnp.int32)
    core = (place & 1).reshape(1)
    chip = (place >> 1).reshape(1)
    senders = lax.axis_size("req")
    sibling = [(i, i ^ 1) for i in range(senders)]

    def swap(array, mask):
        return lax.ppermute(array, "req", [(i, i ^ (2 * mask)) for i in range(senders)])

    keep, send = pack(core, next_weight.transpose(1, 0, 2))
    chunks = pair(core, keep, lax.ppermute(send, "req", sibling), len(ORDERS))
    got1 = [swap(chunks[s], order[0]) for s, order in enumerate(ORDERS)]
    far_a, far_b, normed, own_rows = first(
        lane,
        residual_in,
        merge_dest,
        row(norm2_gain),
        row(norm2_bias),
        up_weight,
        bias_up,
        down_weight,
    )
    got2 = [
        (swap(chunks[s], order[1]), swap(got1[s], order[1])) for s, order in enumerate(ORDERS)
    ]
    quads = [
        jnp.concatenate([chunks[s], got1[s], got2[s][0], got2[s][1]], axis=0)
        for s in range(len(ORDERS))
    ]
    got3 = [swap(quads[s], order[2]) for s, order in enumerate(ORDERS)]
    got4 = [
        (swap(quads[s], order[3]), swap(got3[s], order[3])) for s, order in enumerate(ORDERS)
    ]
    far_a = lax.ppermute(far_a, "mlp", onward)
    far_b = lax.ppermute(far_b, "mlp", back)
    next_a, next_b = feed(normed, 0, up_weight, bias_up, down_weight)
    b1 = lax.ppermute(next_b, "mlp", onward)
    prev_a, prev_b = feed(normed, 1, up_weight, bias_up, down_weight)
    a2 = lax.ppermute(prev_a, "mlp", back)

    def join(first, second):
        return (first.astype(jnp.float32) + second.astype(jnp.float32)).astype(jnp.bfloat16)

    a1 = lax.ppermute(join(far_a, next_a), "mlp", onward)
    b2 = lax.ppermute(join(far_b, prev_b), "mlp", back)
    base = feed(
        normed,
        2,
        up_weight,
        bias_up,
        down_weight,
        (own_rows, row(down_bias)),
    )
    p0, p1, p2, own = project(lane, base, a1, a2, b1, b2, proj_weight)
    others = (
        lax.ppermute(p0, "mlp", across),
        lax.ppermute(p1, "mlp", onward),
        lax.ppermute(p2, "mlp", back),
    )
    outgoing = route(lane, own, others, lengths, owners, merge_dest, segment_ids)
    groups = [[2 * i + c for i in range(senders // 2)] for c in range(2)]
    mine = lax.all_to_all(
        outgoing, "req", split_axis=0, concat_axis=0, axis_index_groups=groups, tiled=True
    )
    theirs = lax.ppermute(mine, "req", sibling)
    full = assemble(
        chip,
        [
            (quads[s], got3[s], got4[s][0], got4[s][1])
            for s in range(len(ORDERS))
        ],
        senders // 2,
    )
    return attend(
        core,
        mine,
        theirs,
        row(norm3_gain),
        row(norm3_bias),
        full.reshape(width, -1),
        sibling,
    )


def solution(mesh):
    return jax.shard_map(
        body,
        mesh=mesh,
        in_specs=(
            P("req", None),
            P(("req", "mlp")),
            P(("req", "mlp")),
            P("req"),
            P("req"),
            P(),
            P(),
            P("mlp", None),
            P("mlp"),
            P("mlp", None),
            P(),
            P("mlp", None),
            P(),
            P(),
            P("req", None, None),
        ),
        out_specs=(P(("req", "mlp"), None), P(("req", "mlp"), None)),
        check_vma=False,
    )
```

time: 139 us -> 145 us (1.043)
  starting transfers between devices: 24.8 us -> 75.4 us
  local copies, waits for them, and re-layouts: 32 us -> 12.2 us
  between operations: 14.4 us -> 1.08 us
  waiting for transfers between devices: 30.3 us -> 19.2 us
    ppermute x0 -> x27, starting transfers between devices: none -> 60.4 us  [the longest x24 34.5 us: swap(): lax.ppermute(array, 'req', [(i, i ^ 2 * mask) for i in range(senders)])]
    reshape x1 -> x0, local copies, waits for them, and re-layouts: 18.6 us -> none  [body(): gathered.reshape(-1, padded, 3 * width)[:, :depth].reshape(width, 3 * width)]
    ppermute x0 -> x27, waiting for transfers between devices: none -> 11.1 us  [the longest x24 11.1 us: swap(): lax.ppermute(array, 'req', [(i, i ^ 2 * mask) for i in range(senders)])]
    ppermute x1, waiting for transfers between devices: 9.7 us -> 0.01 us  [body(): far_b = lax.ppermute(far_b, 'mlp', back)]
    all_to_all x1, waiting for transfers between devices: 10.8 us -> 5.19 us  [body(): lax.all_to_all(outgoing, 'req', split_axis=0, concat_axis=0, axis_index_g...]
    all_to_all x1, starting transfers between devices: 10.4 us -> 4.98 us  [body(): lax.all_to_all(outgoing, 'req', split_axis=0, concat_axis=0, axis_index_g...]
    ppermute x1, waiting for transfers between devices: 5.73 us -> 2.17 us  [body(): lax.ppermute(p1, 'mlp', onward)]
    ppermute x1, starting transfers between devices: 3.22 us -> 0.43 us  [body(): b2 = lax.ppermute(join(far_b, prev_b), 'mlp', back)]
  transfers between devices with their start and end apart: 11 -> 37, of which waited for: 6 -> 10; matrix products, arithmetic and copies ran while one was open for 0% -> 1% of each run, Pallas kernels for 21% -> 19%
where the time goes in v2:
time: 145 us; the launch traced here: 144 us
  starting transfers between devices  75.4 us (52%)
  Pallas kernels  35.9 us (25%)
  waiting for transfers between devices  19.2 us (13%)
  local copies, waits for them, and re-layouts  12.2 us (8%)
    ppermute x24, starting transfers between devices, swap(): lax.ppermute(array, 'req', [(i, i ^ 2 * mask) for i in range(senders)])  34.5 us
    ppermute x1, starting transfers between devices, body(): theirs = lax.ppermute(mine, 'req', sibling)  15.9 us
    ppermute x24, waiting for transfers between devices, swap(): lax.ppermute(array, 'req', [(i, i ^ 2 * mask) for i in range(senders)])  11.1 us
    unnamed x50, local copies, waits for them, and re-layouts  10.7 us
    pallas_call x1, Pallas kernels, first(): pl.pallas_call(first_kernel, in_specs=[SMEM, HBM, VMEM, VMEM, VMEM, HBM,...  9.69 us
    pallas_call x3, Pallas kernels, feed(): pl.pallas_call(wrapped, in_specs=[VMEM] * len(args), out_specs=[VMEM] * 2...  8.8 us
    ppermute x1, starting transfers between devices, attend(): other = lax.ppermute(other, 'req', sibling)  8.46 us
    pallas_call x1, Pallas kernels, attend(): pl.pallas_call(attend_kernel, in_specs=[SMEM] + [VMEM] * 5, out_specs=[VM...  7.1 us
  transfers between devices with their start and end apart: 37, of which 10 were waited for; matrix products, arithmetic and copies ran while one was open for 1% of the time, Pallas kernels for 19%

profile of v2, /device:TPU:1, one launch (start us, length us, event | category | flops | bytes accessed | tf_op | source)
XLA Modules:
  0.0 143.9 jit_solution(5160399672434080754)
XLA Ops:
  0.6 1.0 copy-done.3
  2.0 1.5 %collective-permute-start.10 = (bf16[52,2560]{1,0:T(8,128)(2,1)S(1)}, bf16[52,2560]{1,0:T(8,128)(2,1)S(1)}, u32[]{:S(2)}, u32[]{:S(2)}) collective-permute-start(bf16[52,2560]{1,0:T(8,128)(2,1)S(1)} %get-tuple-element.37), channel_id=1, source_target_pairs={{0,4},{4,0},{8,12},{12,8},{16,20},{20,16},{24,28},{28,24},{32,36},... | collective-permute-start | bytes 798728 | tf_op jit(solution)/shard_map/ppermute | solution.py:578
  4.9 2.0 %copy-done = bf16[1024,1664]{1,0:T(8,128)(2,1)S(1)} copy-done((bf16[1024,1664]{1,0:T(8,128)(2,1)S(1)}, bf16[1024,1664]{1,0:T(8,128)(2,1)}, u32[]{:S(2)}) %copy-start) | copy-done | bytes 3407896
  6.9 2.0 %copy-done.1 = bf16[1024,1664]{1,0:T(8,128)(2,1)S(1)} copy-done((bf16[1024,1664]{1,0:T(8,128)(2,1)S(1)}, bf16[1024,1664]{1,0:T(8,128)(2,1)}, u32[]{:S(2)}) %copy-start.1) | copy-done | bytes 3407896
  8.8 2.0 %copy-done.2 = bf16[1024,1664]{1,0:T(8,128)(2,1)S(1)} copy-done((bf16[1024,1664]{1,0:T(8,128)(2,1)S(1)}, bf16[1024,1664]{1,0:T(8,128)(2,1)}, u32[]{:S(2)}) %copy-start.2) | copy-done | bytes 3407896
  12.2 9.7 %first.1 = (bf16[128,1664]{1,0:T(8,128)(2,1)S(1)}, bf16[128,1664]{1,0:T(8,128)(2,1)S(1)}, bf16[3,256,1664]{2,1,0:T(8,128)(2,1)S(1)}, bf16[256,1664]{1,0:T(8,128)(2,1)S(1)}) custom-call(s32[1]{0:T(128)} %bitcast.1.lane_ref, bf16[1024,1664]{1,0:T(8,128)(2,1)S(1)} %copy-done.2, s32[4,1,256]{2,1,0:T(1,128)S(1)} %bitcast.22, f32[1,1664]{1,0:T(1,128)S(1)} %reshape.52.gain_ref, ...), custom_call_target="tpu_custom_call" | custom-call | flops 1879048192 | bytes 4194304 | tf_op jit(solution)/shard_map/first/pallas_call | solution.py:127
  21.9 2.9 %collective-permute-start.4 = (bf16[128,1664]{1,0:T(8,128)(2,1)S(1)}, bf16[128,1664]{1,0:T(8,128)(2,1)S(1)}, u32[]{:S(2)}, u32[]{:S(2)}) collective-permute-start(bf16[128,1664]{1,0:T(8,128)(2,1)S(1)} %get-tuple-element.30), channel_id=1, source_target_pairs={{0,3},{1,0},{2,1},{3,2},{4,7},{5,4},{6,5},{7,6},{8,11},{9,8},{10,9... | collective-permute-start | bytes 1277960 | tf_op jit(solution)/shard_map/ppermute | solution.py:602
  24.8 2.9 %feed.5 = (bf16[128,1664]{1,0:T(8,128)(2,1)S(1)}, bf16[128,1664]{1,0:T(8,128)(2,1)S(1)}) custom-call(bf16[3,256,1664]{2,1,0:T(8,128)(2,1)S(1)} %get-tuple-element.24.rows_ref, bf16[1024,1664]{1,0:T(8,128)(2,1)S(1)} %copy-done, f32[1,1024]{1,0:T(1,128)S(1)} %bitcast.19, bf16[1024,1664]{1,0:T(8,128)(2,1)S(1)} %copy-done.1), custom_call_target="tpu_custom_call" | custom-call | flops 1879048192 | bytes 4194304 | tf_op jit(solution)/shard_map/feed/pallas_call | solution.py:184
  27.7 2.9 %collective-permute-start.2 = (bf16[128,1664]{1,0:T(8,128)(2,1)S(1)}, bf16[128,1664]{1,0:T(8,128)(2,1)S(1)}, u32[]{:S(2)}, u32[]{:S(2)}) collective-permute-start(bf16[128,1664]{1,0:T(8,128)(2,1)S(1)} %get-tuple-element.28), channel_id=1, source_target_pairs={{0,3},{1,0},{2,1},{3,2},{4,7},{5,4},{6,5},{7,6},{8,11},{9,8},{10,9... | collective-permute-start | bytes 1277960 | tf_op jit(solution)/shard_map/ppermute | solution.py:606
  30.7 2.9 %feed.4 = (bf16[128,1664]{1,0:T(8,128)(2,1)S(1)}, bf16[128,1664]{1,0:T(8,128)(2,1)S(1)}) custom-call(bf16[3,256,1664]{2,1,0:T(8,128)(2,1)S(1)} %get-tuple-element.24.rows_ref, bf16[1024,1664]{1,0:T(8,128)(2,1)S(1)} %copy-done, f32[1,1024]{1,0:T(1,128)S(1)} %bitcast.20, bf16[1024,1664]{1,0:T(8,128)(2,1)S(1)} %copy-done.1), custom_call_target="tpu_custom_call" | custom-call | flops 1879048192 | bytes 4194304 | tf_op jit(solution)/shard_map/feed/pallas_call | solution.py:184
  34.1 1.3 collective-permute-start.11
  35.4 1.6 %collective-permute-start.12 = (bf16[1,104,640]{2,1,0:T(8,128)(2,1)S(1)}, bf16[1,104,640]{2,1,0:T(8,128)(2,1)S(1)}, u32[]{:S(2)}, u32[]{:S(2)}) collective-permute-start(bf16[1,104,640]{2,1,0:T(8,128)(2,1)S(1)} %get-tuple-element.38), channel_id=1, source_target_pairs={{0,32},{4,36},{8,40},{12,44},{16,48},{20,52},{24,56},{28,60},{32,0... | collective-permute-start | bytes 399368 | tf_op jit(solution)/shard_map/ppermute | solution.py:575
  37.1 1.3 collective-permute-done.11
  38.3 1.6 %collective-permute-start.17 = (bf16[1,104,640]{2,1,0:T(8,128)(2,1)S(1)}, bf16[1,104,640]{2,1,0:T(8,128)(2,1)S(1)}, u32[]{:S(2)}, u32[]{:S(2)}) collective-permute-start(bf16[1,104,640]{2,1,0:T(8,128)(2,1)S(1)} %get-tuple-element.39), channel_id=1, source_target_pairs={{0,32},{4,36},{8,40},{12,44},{16,48},{20,52},{24,56},{28,60},{32,0... | collective-permute-start | bytes 399368 | tf_op jit(solution)/shard_map/ppermute | solution.py:575
  40.0 2.6 %collective-permute-start.18 = (bf16[1,104,640]{2,1,0:T(8,128)(2,1)S(1)}, bf16[1,104,640]{2,1,0:T(8,128)(2,1)S(1)}, u32[]{:S(2)}, u32[]{:S(2)}) collective-permute-start(bf16[1,104,640]{2,1,0:T(8,128)(2,1)S(1)} %get-tuple-element.39), channel_id=1, source_target_pairs={{0,24},{4,28},{8,16},{12,20},{16,8},{20,12},{24,0},{28,4},{32,56},... | collective-permute-start | bytes 399368 | tf_op jit(solution)/shard_map/ppermute | solution.py:575
  42.6 2.5 %collective-permute-start.23 = (bf16[1,104,640]{2,1,0:T(8,128)(2,1)S(1)}, bf16[1,104,640]{2,1,0:T(8,128)(2,1)S(1)}, u32[]{:S(2)}, u32[]{:S(2)}) collective-permute-start(bf16[1,104,640]{2,1,0:T(8,128)(2,1)S(1)} %get-tuple-element.40), channel_id=1, source_target_pairs={{0,24},{4,28},{8,16},{12,20},{16,8},{20,12},{24,0},{28,4},{32,56},... | collective-permute-start | bytes 399368 | tf_op jit(solution)/shard_map/ppermute | solution.py:575
  45.2 3.7 %collective-permute-start.24 = (bf16[1,104,640]{2,1,0:T(8,128)(2,1)S(1)}, bf16[1,104,640]{2,1,0:T(8,128)(2,1)S(1)}, u32[]{:S(2)}, u32[]{:S(2)}) collective-permute-start(bf16[1,104,640]{2,1,0:T(8,128)(2,1)S(1)} %get-tuple-element.40), channel_id=1, source_target_pairs={{0,96},{4,100},{8,104},{12,108},{16,112},{20,116},{24,120},{28,124... | collective-permute-start | bytes 399368 | tf_op jit(solution)/shard_map/ppermute | solution.py:575
  49.3 1.9 %collective-permute-done.24 = bf16[1,104,640]{2,1,0:T(8,128)(2,1)S(1)} collective-permute-done((bf16[1,104,640]{2,1,0:T(8,128)(2,1)S(1)}, bf16[1,104,640]{2,1,0:T(8,128)(2,1)S(1)}, u32[]{:S(2)}, u32[]{:S(2)}) %collective-permute-start.24) | collective-permute-done | bytes 133152 | tf_op jit(solution)/shard_map/ppermute | solution.py:575
  51.2 3.0 %collective-permute-start.29 = (bf16[1,104,640]{2,1,0:T(8,128)(2,1)S(1)}, bf16[1,104,640]{2,1,0:T(8,128)(2,1)S(1)}, u32[]{:S(2)}, u32[]{:S(2)}) collective-permute-start(bf16[1,104,640]{2,1,0:T(8,128)(2,1)S(1)} %get-tuple-element.41), channel_id=1, source_target_pairs={{0,96},{4,100},{8,104},{12,108},{16,112},{20,116},{24,120},{28,124... | collective-permute-start | bytes 399368 | tf_op jit(solution)/shard_map/ppermute | solution.py:575
  54.4 1.1 collective-permute-start.19
  55.6 0.9 collective-permute-done.29
  56.6 3.0 %collective-permute-start.25 = (bf16[1,104,640]{2,1,0:T(8,128)(2,1)S(1)}, bf16[1,104,640]{2,1,0:T(8,128)(2,1)S(1)}, u32[]{:S(2)}, u32[]{:S(2)}) collective-permute-start(bf16[1,104,640]{2,1,0:T(8,128)(2,1)S(1)} %collective-permute-done.23), channel_id=1, source_target_pairs={{0,96},{4,100},{8,104},{12,108},{16,112},{20,116},{24,120},{28,124... | collective-permute-start | bytes 399368 | tf_op jit(solution)/shard_map/ppermute | solution.py:575
  60.0 1.0 collective-permute-start.1
  61.1 1.7 %collective-permute-done.25 = bf16[1,104,640]{2,1,0:T(8,128)(2,1)S(1)} collective-permute-done((bf16[1,104,640]{2,1,0:T(8,128)(2,1)S(1)}, bf16[1,104,640]{2,1,0:T(8,128)(2,1)S(1)}, u32[]{:S(2)}, u32[]{:S(2)}) %collective-permute-start.25) | collective-permute-done | bytes 133152 | tf_op jit(solution)/shard_map/ppermute | solution.py:575
  62.8 2.8 %collective-permute-start.14 = (bf16[4,104,640]{2,1,0:T(8,128)(2,1)S(1)}, bf16[4,104,640]{2,1,0:T(8,128)(2,1)S(1)}, u32[]{:S(2)}, u32[]{:S(2)}) collective-permute-start(bf16[4,104,640]{2,1,0:T(8,128)(2,1)S(1)} %constant_dynamic-update-slice_fusion.refs_0_), channel_id=1, source_target_pairs={{0,24},{4,28},{8,16},{12,20},{16,8},{20,12},{24,0},{28,4},{32,56},... | collective-permute-start | bytes 1597448 | tf_op jit(solution)/shard_map/ppermute | solution.py:575
  65.6 1.5 %collective-permute-start.20 = (bf16[4,104,640]{2,1,0:T(8,128)(2,1)S(1)}, bf16[4,104,640]{2,1,0:T(8,128)(2,1)S(1)}, u32[]{:S(2)}, u32[]{:S(2)}) collective-permute-start(bf16[4,104,640]{2,1,0:T(8,128)(2,1)S(1)} %constant_dynamic-update-slice_fusion.4.refs_4_), channel_id=1, source_target_pairs={{0,96},{4,100},{8,104},{12,108},{16,112},{20,116},{24,120},{28,124... | collective-permute-start | bytes 1597448 | tf_op jit(solution)/shard_map/ppermute | solution.py:575
  67.2 2.9 %feed.3.base_ref = f32[256,1664]{1,0:T(8,128)S(1)} custom-call(bf16[3,256,1664]{2,1,0:T(8,128)(2,1)S(1)} %get-tuple-element.24.rows_ref, bf16[1024,1664]{1,0:T(8,128)(2,1)S(1)} %copy-done, f32[1,1024]{1,0:T(1,128)S(1)} %bitcast.21, bf16[1024,1664]{1,0:T(8,128)(2,1)S(1)} %copy-done.1, bf16[256,1664]{1,0:T(8,128)(2,1)S(1)} %get-tuple-element.25.refs_3_, ...), custom_call_target="tpu_custom_call" | custom-call | flops 1879048192 | bytes 4194304 | tf_op jit(solution)/shard_map/feed/pallas_call | solution.py:184
  70.1 1.5 %collective-permute-start.30 = (bf16[1,104,640]{2,1,0:T(8,128)(2,1)S(1)}, bf16[1,104,640]{2,1,0:T(8,128)(2,1)S(1)}, u32[]{:S(2)}, u32[]{:S(2)}) collective-permute-start(bf16[1,104,640]{2,1,0:T(8,128)(2,1)S(1)} %get-tuple-element.41), channel_id=1, source_target_pairs={{0,8},{4,12},{8,0},{12,4},{16,24},{20,28},{24,16},{28,20},{32,40},... | collective-permute-start | bytes 399368 | tf_op jit(solution)/shard_map/ppermute | solution.py:575
  71.9 2.2 %project.1 = (bf16[64,1664]{1,0:T(8,128)(2,1)S(1)}, bf16[64,1664]{1,0:T(8,128)(2,1)S(1)}, bf16[64,1664]{1,0:T(8,128)(2,1)S(1)}, f32[64,1664]{1,0:T(8,128)S(1)}) custom-call(s32[1]{0:T(128)} %bitcast.1.lane_ref, f32[256,1664]{1,0:T(8,128)S(1)} %feed.3.base_ref, bf16[128,1664]{1,0:T(8,128)(2,1)S(1)} %collective-permute-done.1.a1_ref, ...), custom_call_target="tpu_custom_call" | custom-call | flops 1417674752 | bytes 10649600 | tf_op jit(solution)/shard_map/project/pallas_call | solution.py:214
  74.0 3.0 %collective-permute-done.30 = bf16[1,104,640]{2,1,0:T(8,128)(2,1)S(1)} collective-permute-done((bf16[1,104,640]{2,1,0:T(8,128)(2,1)S(1)}, bf16[1,104,640]{2,1,0:T(8,128)(2,1)S(1)}, u32[]{:S(2)}, u32[]{:S(2)}) %collective-permute-start.30) | collective-permute-done | bytes 133152 | tf_op jit(solution)/shard_map/ppermute | solution.py:575
  77.0 1.8 %collective-permute-done.31 = bf16[1,104,640]{2,1,0:T(8,128)(2,1)S(1)} collective-permute-done((bf16[1,104,640]{2,1,0:T(8,128)(2,1)S(1)}, bf16[1,104,640]{2,1,0:T(8,128)(2,1)S(1)}, u32[]{:S(2)}, u32[]{:S(2)}) %collective-permute-start.31) | collective-permute-done | bytes 133152 | tf_op jit(solution)/shard_map/ppermute | solution.py:575
  78.8 2.7 %collective-permute-start.8 = (bf16[64,1664]{1,0:T(8,128)(2,1)S(1)}, bf16[64,1664]{1,0:T(8,128)(2,1)S(1)}, u32[]{:S(2)}, u32[]{:S(2)}) collective-permute-start(bf16[64,1664]{1,0:T(8,128)(2,1)S(1)} %get-tuple-element.35), channel_id=1, source_target_pairs={{0,3},{1,0},{2,1},{3,2},{4,7},{5,4},{6,5},{7,6},{8,11},{9,8},{10,9... | collective-permute-start | bytes 638984 | tf_op jit(solution)/shard_map/ppermute | solution.py:625
  81.7 0.9 collective-permute-start.15
  83.3 2.2 %collective-permute-done.7.r1 = bf16[64,1664]{1,0:T(8,128)(2,1)S(1)} collective-permute-done((bf16[64,1664]{1,0:T(8,128)(2,1)S(1)}, bf16[64,1664]{1,0:T(8,128)(2,1)S(1)}, u32[]{:S(2)}, u32[]{:S(2)}) %collective-permute-start.7) | collective-permute-done | bytes 213024 | tf_op jit(solution)/shard_map/ppermute | solution.py:624
  85.5 1.3 collective-permute-start.33
  86.8 1.1 route.1
  87.9 5.0 %all-to-all-start = ((bf16[16,8,1792]{2,1,0:T(8,128)(2,1)}), bf16[16,8,1792]{2,1,0:T(8,128)(2,1)S(1)}, u32[]{:S(2)}, u32[]{:S(2)}) async-start(bf16[16,8,1792]{2,1,0:T(8,128)(2,1)} %bitcast.7), calls=%async_computation | async-start | bytes 917504 | tf_op jit(solution)/shard_map/all_to_all | solution.py:629
  92.9 2.7 %collective-permute-start.16 = (bf16[4,104,640]{2,1,0:T(8,128)(2,1)S(1)}, bf16[4,104,640]{2,1,0:T(8,128)(2,1)}, u32[]{:S(2)}, u32[]{:S(2)}) collective-permute-start(bf16[4,104,640]{2,1,0:T(8,128)(2,1)S(1)} %collective-permute-done.14.refs_1_), channel_id=1, source_target_pairs={{0,96},{4,100},{8,104},{12,108},{16,112},{20,116},{24,120},{28,124... | collective-permute-start | bytes 1597448 | tf_op jit(solution)/shard_map/ppermute | solution.py:575
  95.6 1.2 collective-permute-start.22
  96.8 2.0 %collective-permute-start.34 = (bf16[4,104,640]{2,1,0:T(8,128)(2,1)}, bf16[4,104,640]{2,1,0:T(8,128)(2,1)}, u32[]{:S(2)}, u32[]{:S(2)}) collective-permute-start(bf16[4,104,640]{2,1,0:T(8,128)(2,1)} %collective-permute-done.32.refs_13_), channel_id=1, source_target_pairs={{0,24},{4,28},{8,16},{12,20},{16,8},{20,12},{24,0},{28,4},{32,56},... | collective-permute-start | bytes 1597448 | tf_op jit(solution)/shard_map/ppermute | solution.py:575
  98.8 5.2 %all-to-all-done = bf16[16,8,1792]{2,1,0:T(8,128)(2,1)S(1)} async-done(((bf16[16,8,1792]{2,1,0:T(8,128)(2,1)}), bf16[16,8,1792]{2,1,0:T(8,128)(2,1)S(1)}, u32[]{:S(2)}, u32[]{:S(2)}) %all-to-all-start) | async-done | bytes 458784 | tf_op jit(solution)/shard_map/all_to_all | solution.py:629
  104.0 15.9 %collective-permute-start.9 = (bf16[128,1792]{1,0:T(8,128)(2,1)S(1)}, bf16[128,1792]{1,0:T(8,128)(2,1)}, u32[]{:S(2)}, u32[]{:S(2)}) collective-permute-start(bf16[128,1792]{1,0:T(8,128)(2,1)S(1)} %bitcast.15), channel_id=1, source_target_pairs={{0,4},{4,0},{8,12},{12,8},{16,20},{20,16},{24,28},{28,24},{32,36},... | collective-permute-start | bytes 1376264 | tf_op jit(solution)/shard_map/ppermute | solution.py:632
  120.0 1.0 copy-done.5
  121.0 1.0 copy-done.7
  122.1 3.0 %assemble.1 = bf16[16,104,2560]{2,1,0:T(8,128)(2,1)S(1)} custom-call(s32[1]{0:T(128)} %bitcast.9.chip_ref, bf16[4,104,640]{2,1,0:T(8,128)(2,1)S(1)} %constant_dynamic-update-slice_fusion.refs_0_, bf16[4,104,640]{2,1,0:T(8,128)(2,1)S(1)} %collective-permute-done.14.refs_1_, bf16[4,104,640]{2,1,0:T(8,128)(2,1)} %collective-permute-done.15.refs_2_, ...), custom_call_target="tpu_custom_call" | custom-call | bytes 16777216 | tf_op jit(solution)/shard_map/assemble/pallas_call | solution.py:401
  125.1 7.1 %attend.1 = (bf16[128,1664]{1,0:T(8,128)(2,1)}, bf16[128,832]{1,0:T(8,128)(2,1)S(1)}, bf16[128,2560]{1,0:T(8,128)(2,1)S(1)}, f32[128,128]{1,0:T(8,128)S(1)}) custom-call(s32[1]{0:T(128)} %bitcast.core_ref, bf16[128,1792]{1,0:T(8,128)(2,1)S(1)} %bitcast.16, bf16[128,1792]{1,0:T(8,128)(2,1)} %collective-permute-done.9.theirs_ref, ...), custom_call_target="tpu_custom_call" | custom-call | tf_op jit(solution)/shard_map/attend/pallas_call | solution.py:504
  132.2 8.5 %collective-permute-start.35 = (bf16[128,832]{1,0:T(8,128)(2,1)S(1)}, bf16[128,832]{1,0:T(8,128)(2,1)S(1)}, u32[]{:S(2)}, u32[]{:S(2)}) collective-permute-start(bf16[128,832]{1,0:T(8,128)(2,1)S(1)} %get-tuple-element.45), channel_id=1, source_target_pairs={{0,4},{4,0},{8,12},{12,8},{16,20},{20,16},{24,28},{28,24},{32,36},... | collective-permute-start | bytes 638984 | tf_op jit(solution)/shard_map/ppermute | solution.py:518
  140.7 2.4 %attend_own.1.mine_ref = bf16[128,832]{1,0:T(8,128)(2,1)S(1)} custom-call(bf16[128,2560]{1,0:T(8,128)(2,1)S(1)} %get-tuple-element.43.heads_ref, f32[128,128]{1,0:T(8,128)S(1)} %get-tuple-element.44.tags_ref), custom_call_target="tpu_custom_call" | custom-call | flops 1073741824 | bytes 1048576 | tf_op jit(solution)/shard_map/attend_own/pallas_call | solution.py:519
  (100 shorter events, 7.1 us)
Async XLA Ops:
  2.0 31.6 %collective-permute-start.10 = (bf16[52,2560]{1,0:T(8,128)(2,1)S(1)}, bf16[52,2560]{1,0:T(8,128)(2,1)S(1)}, u32[]{:S(2)}, u32[]{:S(2)}) collective-permute-start(bf16[52,2560]{1,0:T(8,128)(2,1)S(1)} %get-tuple-element.37), channel_id=1, source_target_pairs={{0,4},{4,0},{8,12},{12,8},{16,20},{20,16},{24,28},{28,24},{32,36},... | collective-permute-start | bytes 798728 | tf_op jit(solution)/shard_map/ppermute | solution.py:578
  21.9 32.3 %collective-permute-start.4 = (bf16[128,1664]{1,0:T(8,128)(2,1)S(1)}, bf16[128,1664]{1,0:T(8,128)(2,1)S(1)}, u32[]{:S(2)}, u32[]{:S(2)}) collective-permute-start(bf16[128,1664]{1,0:T(8,128)(2,1)S(1)} %get-tuple-element.30), channel_id=1, source_target_pairs={{0,3},{1,0},{2,1},{3,2},{4,7},{5,4},{6,5},{7,6},{8,11},{9,8},{10,9... | collective-permute-start | bytes 1277960 | tf_op jit(solution)/shard_map/ppermute | solution.py:602
  24.8 29.6 %collective-permute-start = (bf16[128,1664]{1,0:T(8,128)(2,1)S(1)}, bf16[128,1664]{1,0:T(8,128)(2,1)S(1)}, u32[]{:S(2)}, u32[]{:S(2)}) collective-permute-start(bf16[128,1664]{1,0:T(8,128)(2,1)S(1)} %get-tuple-element.26), channel_id=1, source_target_pairs={{0,1},{1,2},{2,3},{3,0},{4,5},{5,6},{6,7},{7,4},{8,9},{9,10},{10,1... | collective-permute-start | bytes 1277960 | tf_op jit(solution)/shard_map/ppermute | solution.py:601
  24.8 5.9 %copy-start.15 = (f32[1664]{0:T(1024)S(1)}, f32[1664]{0:T(1024)}, u32[]{:S(2)}) copy-start(f32[1664]{0:T(1024)} %param.25) | copy-start | bytes 19972
  27.7 37.9 %collective-permute-start.2 = (bf16[128,1664]{1,0:T(8,128)(2,1)S(1)}, bf16[128,1664]{1,0:T(8,128)(2,1)S(1)}, u32[]{:S(2)}, u32[]{:S(2)}) collective-permute-start(bf16[128,1664]{1,0:T(8,128)(2,1)S(1)} %get-tuple-element.28), channel_id=1, source_target_pairs={{0,3},{1,0},{2,1},{3,2},{4,7},{5,4},{6,5},{7,6},{8,11},{9,8},{10,9... | collective-permute-start | bytes 1277960 | tf_op jit(solution)/shard_map/ppermute | solution.py:606
  33.6 33.6 %copy-start.9 = (f32[1024]{0:T(1024)S(1)}, f32[1024]{0:T(1024)}, u32[]{:S(2)}) copy-start(f32[1024]{0:T(1024)} %param.23) | copy-start | bytes 12292
  34.1 4.3 %collective-permute-start.11 = (bf16[1,104,640]{2,1,0:T(8,128)(2,1)S(1)}, bf16[1,104,640]{2,1,0:T(8,128)(2,1)S(1)}, u32[]{:S(2)}, u32[]{:S(2)}) collective-permute-start(bf16[1,104,640]{2,1,0:T(8,128)(2,1)S(1)} %get-tuple-element.38), channel_id=1, source_target_pairs={{0,8},{4,12},{8,0},{12,4},{16,24},{20,28},{24,16},{28,20},{32,40},... | collective-permute-start | bytes 399368 | tf_op jit(solution)/shard_map/ppermute | solution.py:575
  35.4 4.6 %collective-permute-start.12 = (bf16[1,104,640]{2,1,0:T(8,128)(2,1)S(1)}, bf16[1,104,640]{2,1,0:T(8,128)(2,1)S(1)}, u32[]{:S(2)}, u32[]{:S(2)}) collective-permute-start(bf16[1,104,640]{2,1,0:T(8,128)(2,1)S(1)} %get-tuple-element.38), channel_id=1, source_target_pairs={{0,32},{4,36},{8,40},{12,44},{16,48},{20,52},{24,56},{28,60},{32,0... | collective-permute-start | bytes 399368 | tf_op jit(solution)/shard_map/ppermute | solution.py:575
  38.3 4.3 %collective-permute-start.17 = (bf16[1,104,640]{2,1,0:T(8,128)(2,1)S(1)}, bf16[1,104,640]{2,1,0:T(8,128)(2,1)S(1)}, u32[]{:S(2)}, u32[]{:S(2)}) collective-permute-start(bf16[1,104,640]{2,1,0:T(8,128)(2,1)S(1)} %get-tuple-element.39), channel_id=1, source_target_pairs={{0,32},{4,36},{8,40},{12,44},{16,48},{20,52},{24,56},{28,60},{32,0... | collective-permute-start | bytes 399368 | tf_op jit(solution)/shard_map/ppermute | solution.py:575
  40.0 5.2 %collective-permute-start.18 = (bf16[1,104,640]{2,1,0:T(8,128)(2,1)S(1)}, bf16[1,104,640]{2,1,0:T(8,128)(2,1)S(1)}, u32[]{:S(2)}, u32[]{:S(2)}) collective-permute-start(bf16[1,104,640]{2,1,0:T(8,128)(2,1)S(1)} %get-tuple-element.39), channel_id=1, source_target_pairs={{0,24},{4,28},{8,16},{12,20},{16,8},{20,12},{24,0},{28,4},{32,56},... | collective-permute-start | bytes 399368 | tf_op jit(solution)/shard_map/ppermute | solution.py:575
  42.6 6.6 %collective-permute-start.23 = (bf16[1,104,640]{2,1,0:T(8,128)(2,1)S(1)}, bf16[1,104,640]{2,1,0:T(8,128)(2,1)S(1)}, u32[]{:S(2)}, u32[]{:S(2)}) collective-permute-start(bf16[1,104,640]{2,1,0:T(8,128)(2,1)S(1)} %get-tuple-element.40), channel_id=1, source_target_pairs={{0,24},{4,28},{8,16},{12,20},{16,8},{20,12},{24,0},{28,4},{32,56},... | collective-permute-start | bytes 399368 | tf_op jit(solution)/shard_map/ppermute | solution.py:575
  45.2 6.0 %collective-permute-start.24 = (bf16[1,104,640]{2,1,0:T(8,128)(2,1)S(1)}, bf16[1,104,640]{2,1,0:T(8,128)(2,1)S(1)}, u32[]{:S(2)}, u32[]{:S(2)}) collective-permute-start(bf16[1,104,640]{2,1,0:T(8,128)(2,1)S(1)} %get-tuple-element.40), channel_id=1, source_target_pairs={{0,96},{4,100},{8,104},{12,108},{16,112},{20,116},{24,120},{28,124... | collective-permute-start | bytes 399368 | tf_op jit(solution)/shard_map/ppermute | solution.py:575
  49.2 17.9 %collective-permute-start.3 = (bf16[128,1664]{1,0:T(8,128)(2,1)S(1)}, bf16[128,1664]{1,0:T(8,128)(2,1)S(1)}, u32[]{:S(2)}, u32[]{:S(2)}) collective-permute-start(bf16[128,1664]{1,0:T(8,128)(2,1)S(1)} %get-tuple-element.29), channel_id=1, source_target_pairs={{0,1},{1,2},{2,3},{3,0},{4,5},{5,6},{6,7},{7,4},{8,9},{9,10},{10,1... | collective-permute-start | bytes 1277960 | tf_op jit(solution)/shard_map/ppermute | solution.py:604
  51.2 5.4 %collective-permute-start.29 = (bf16[1,104,640]{2,1,0:T(8,128)(2,1)S(1)}, bf16[1,104,640]{2,1,0:T(8,128)(2,1)S(1)}, u32[]{:S(2)}, u32[]{:S(2)}) collective-permute-start(bf16[1,104,640]{2,1,0:T(8,128)(2,1)S(1)} %get-tuple-element.41), channel_id=1, source_target_pairs={{0,96},{4,100},{8,104},{12,108},{16,112},{20,116},{24,120},{28,124... | collective-permute-start | bytes 399368 | tf_op jit(solution)/shard_map/ppermute | solution.py:575
  54.2 5.4 %collective-permute-start.13 = (bf16[1,104,640]{2,1,0:T(8,128)(2,1)S(1)}, bf16[1,104,640]{2,1,0:T(8,128)(2,1)S(1)}, u32[]{:S(2)}, u32[]{:S(2)}) collective-permute-start(bf16[1,104,640]{2,1,0:T(8,128)(2,1)S(1)} %collective-permute-done.11), channel_id=1, source_target_pairs={{0,32},{4,36},{8,40},{12,44},{16,48},{20,52},{24,56},{28,60},{32,0... | collective-permute-start | bytes 399368 | tf_op jit(solution)/shard_map/ppermute | solution.py:575
  54.4 5.6 %collective-permute-start.19 = (bf16[1,104,640]{2,1,0:T(8,128)(2,1)S(1)}, bf16[1,104,640]{2,1,0:T(8,128)(2,1)S(1)}, u32[]{:S(2)}, u32[]{:S(2)}) collective-permute-start(bf16[1,104,640]{2,1,0:T(8,128)(2,1)S(1)} %collective-permute-done.17), channel_id=1, source_target_pairs={{0,24},{4,28},{8,16},{12,20},{16,8},{20,12},{24,0},{28,4},{32,56},... | collective-permute-start | bytes 399368 | tf_op jit(solution)/shard_map/ppermute | solution.py:575
  56.6 6.2 %collective-permute-start.25 = (bf16[1,104,640]{2,1,0:T(8,128)(2,1)S(1)}, bf16[1,104,640]{2,1,0:T(8,128)(2,1)S(1)}, u32[]{:S(2)}, u32[]{:S(2)}) collective-permute-start(bf16[1,104,640]{2,1,0:T(8,128)(2,1)S(1)} %collective-permute-done.23), channel_id=1, source_target_pairs={{0,96},{4,100},{8,104},{12,108},{16,112},{20,116},{24,120},{28,124... | collective-permute-start | bytes 399368 | tf_op jit(solution)/shard_map/ppermute | solution.py:575
  59.6 10.5 %collective-permute-start.5 = (bf16[128,1664]{1,0:T(8,128)(2,1)S(1)}, bf16[128,1664]{1,0:T(8,128)(2,1)S(1)}, u32[]{:S(2)}, u32[]{:S(2)}) collective-permute-start(bf16[128,1664]{1,0:T(8,128)(2,1)S(1)} %add_convert_fusion), channel_id=1, source_target_pairs={{0,3},{1,0},{2,1},{3,2},{4,7},{5,4},{6,5},{7,6},{8,11},{9,8},{10,9... | collective-permute-start | bytes 1277960 | tf_op jit(solution)/shard_map/ppermute | solution.py:612
  60.0 11.6 %collective-permute-start.1 = (bf16[128,1664]{1,0:T(8,128)(2,1)S(1)}, bf16[128,1664]{1,0:T(8,128)(2,1)S(1)}, u32[]{:S(2)}, u32[]{:S(2)}) collective-permute-start(bf16[128,1664]{1,0:T(8,128)(2,1)S(1)} %add_convert_fusion.1), channel_id=1, source_target_pairs={{0,1},{1,2},{2,3},{3,0},{4,5},{5,6},{6,7},{7,4},{8,9},{9,10},{10,1... | collective-permute-start | bytes 1277960 | tf_op jit(solution)/shard_map/ppermute | solution.py:611
  62.8 16.0 %collective-permute-start.14 = (bf16[4,104,640]{2,1,0:T(8,128)(2,1)S(1)}, bf16[4,104,640]{2,1,0:T(8,128)(2,1)S(1)}, u32[]{:S(2)}, u32[]{:S(2)}) collective-permute-start(bf16[4,104,640]{2,1,0:T(8,128)(2,1)S(1)} %constant_dynamic-update-slice_fusion.refs_0_), channel_id=1, source_target_pairs={{0,24},{4,28},{8,16},{12,20},{16,8},{20,12},{24,0},{28,4},{32,56},... | collective-permute-start | bytes 1597448 | tf_op jit(solution)/shard_map/ppermute | solution.py:575
  65.6 15.9 %collective-permute-start.20 = (bf16[4,104,640]{2,1,0:T(8,128)(2,1)S(1)}, bf16[4,104,640]{2,1,0:T(8,128)(2,1)S(1)}, u32[]{:S(2)}, u32[]{:S(2)}) collective-permute-start(bf16[4,104,640]{2,1,0:T(8,128)(2,1)S(1)} %constant_dynamic-update-slice_fusion.4.refs_4_), channel_id=1, source_target_pairs={{0,96},{4,100},{8,104},{12,108},{16,112},{20,116},{24,120},{28,124... | collective-permute-start | bytes 1597448 | tf_op jit(solution)/shard_map/ppermute | solution.py:575
  67.2 14.5 %collective-permute-start.26 = (bf16[4,104,640]{2,1,0:T(8,128)(2,1)S(1)}, bf16[4,104,640]{2,1,0:T(8,128)(2,1)S(1)}, u32[]{:S(2)}, u32[]{:S(2)}) collective-permute-start(bf16[4,104,640]{2,1,0:T(8,128)(2,1)S(1)} %constant_dynamic-update-slice_fusion.8.refs_8_), channel_id=1, source_target_pairs={{0,8},{4,12},{8,0},{12,4},{16,24},{20,28},{24,16},{28,20},{32,40},... | collective-permute-start | bytes 1597448 | tf_op jit(solution)/shard_map/ppermute | solution.py:575
  67.2 4.6 %slice-start = ((s8[5537792]{0:T(1024)(128)(4,1)}), s8[4194304]{0:T(1024)(128)(4,1)S(1)}, s32[]{:S(2)}) async-start(s8[5537792]{0:T(1024)(128)(4,1)} %bitcast.13), calls=%async_computation.1 | async-start | bytes 8388608
  67.2 4.6 %slice-start.1 = ((s8[5537792]{0:T(1024)(128)(4,1)}), s8[1343488]{0:T(1024)(128)(4,1)S(1)}, s32[]{:S(2)}) async-start(s8[5537792]{0:T(1024)(128)(4,1)} %bitcast.13), calls=%async_computation.2 | async-start | bytes 2686976
  70.1 6.9 %collective-permute-start.30 = (bf16[1,104,640]{2,1,0:T(8,128)(2,1)S(1)}, bf16[1,104,640]{2,1,0:T(8,128)(2,1)S(1)}, u32[]{:S(2)}, u32[]{:S(2)}) collective-permute-start(bf16[1,104,640]{2,1,0:T(8,128)(2,1)S(1)} %get-tuple-element.41), channel_id=1, source_target_pairs={{0,8},{4,12},{8,0},{12,4},{16,24},{20,28},{24,16},{28,20},{32,40},... | collective-permute-start | bytes 399368 | tf_op jit(solution)/shard_map/ppermute | solution.py:575
  71.7 7.1 %collective-permute-start.31 = (bf16[1,104,640]{2,1,0:T(8,128)(2,1)S(1)}, bf16[1,104,640]{2,1,0:T(8,128)(2,1)S(1)}, u32[]{:S(2)}, u32[]{:S(2)}) collective-permute-start(bf16[1,104,640]{2,1,0:T(8,128)(2,1)S(1)} %collective-permute-done.29), channel_id=1, source_target_pairs={{0,8},{4,12},{8,0},{12,4},{16,24},{20,28},{24,16},{28,20},{32,40},... | collective-permute-start | bytes 399368 | tf_op jit(solution)/shard_map/ppermute | solution.py:575
  71.8 15.0 %copy-start.11 = (s32[1024]{0:T(1024)S(1)}, s32[1024]{0:T(1024)}, u32[]{:S(2)}) copy-start(s32[1024]{0:T(1024)} %param.18) | copy-start | bytes 12292
  71.8 15.0 %copy-start.12 = (s32[1024]{0:T(1024)S(1)}, s32[1024]{0:T(1024)}, u32[]{:S(2)}) copy-start(s32[1024]{0:T(1024)} %param.19) | copy-start | bytes 12292
  71.8 15.0 %copy-start.13 = (s32[32]{0:T(128)S(1)}, s32[32]{0:T(128)}, u32[]{:S(2)}) copy-start(s32[32]{0:T(128)} %param.16) | copy-start | bytes 388
  71.8 14.9 %copy-start.14 = (s32[32]{0:T(128)S(1)}, s32[32]{0:T(128)}, u32[]{:S(2)}) copy-start(s32[32]{0:T(128)} %param.17) | copy-start | bytes 388
  71.9 48.1 %copy-start.16 = (f32[1664]{0:T(1024)S(1)}, f32[1664]{0:T(1024)}, u32[]{:S(2)}) copy-start(f32[1664]{0:T(1024)} %param.27) | copy-start | bytes 19972
  71.9 48.1 %copy-start.17 = (f32[1664]{0:T(1024)S(1)}, f32[1664]{0:T(1024)}, u32[]{:S(2)}) copy-start(f32[1664]{0:T(1024)} %param.28) | copy-start | bytes 19972
  77.0 6.3 %collective-permute-start.6 = (bf16[64,1664]{1,0:T(8,128)(2,1)S(1)}, bf16[64,1664]{1,0:T(8,128)(2,1)S(1)}, u32[]{:S(2)}, u32[]{:S(2)}) collective-permute-start(bf16[64,1664]{1,0:T(8,128)(2,1)S(1)} %get-tuple-element.33), channel_id=1, source_target_pairs={{0,2},{1,3},{2,0},{3,1},{4,6},{5,7},{6,4},{7,5},{8,10},{9,11},{10,... | collective-permute-start | bytes 638984 | tf_op jit(solution)/shard_map/ppermute | solution.py:623
  78.8 6.7 %collective-permute-start.7 = (bf16[64,1664]{1,0:T(8,128)(2,1)S(1)}, bf16[64,1664]{1,0:T(8,128)(2,1)S(1)}, u32[]{:S(2)}, u32[]{:S(2)}) collective-permute-start(bf16[64,1664]{1,0:T(8,128)(2,1)S(1)} %get-tuple-element.34), channel_id=1, source_target_pairs={{0,1},{1,2},{2,3},{3,0},{4,5},{5,6},{6,7},{7,4},{8,9},{9,10},{10,1... | collective-permute-start | bytes 638984 | tf_op jit(solution)/shard_map/ppermute | solution.py:624
  78.8 6.7 %collective-permute-start.8 = (bf16[64,1664]{1,0:T(8,128)(2,1)S(1)}, bf16[64,1664]{1,0:T(8,128)(2,1)S(1)}, u32[]{:S(2)}, u32[]{:S(2)}) collective-permute-start(bf16[64,1664]{1,0:T(8,128)(2,1)S(1)} %get-tuple-element.35), channel_id=1, source_target_pairs={{0,3},{1,0},{2,1},{3,2},{4,7},{5,4},{6,5},{7,6},{8,11},{9,8},{10,9... | collective-permute-start | bytes 638984 | tf_op jit(solution)/shard_map/ppermute | solution.py:625
  81.5 3.9 %copy-start.4 = (bf16[4,104,640]{2,1,0:T(8,128)(2,1)}, bf16[4,104,640]{2,1,0:T(8,128)(2,1)S(1)}, u32[]{:S(2)}) copy-start(bf16[4,104,640]{2,1,0:T(8,128)(2,1)S(1)} %collective-permute-done.20.refs_5_) | copy-start | bytes 1597444
  81.6 11.4 %collective-permute-start.32 = (bf16[4,104,640]{2,1,0:T(8,128)(2,1)S(1)}, bf16[4,104,640]{2,1,0:T(8,128)(2,1)}, u32[]{:S(2)}, u32[]{:S(2)}) collective-permute-start(bf16[4,104,640]{2,1,0:T(8,128)(2,1)S(1)} %constant_dynamic-update-slice_fusion.12.refs_12_), channel_id=1, source_target_pairs={{0,32},{4,36},{8,40},{12,44},{16,48},{20,52},{24,56},{28,60},{32,0... | collective-permute-start | bytes 1597448 | tf_op jit(solution)/shard_map/ppermute | solution.py:575
  81.7 13.9 %collective-permute-start.15 = (bf16[4,104,640]{2,1,0:T(8,128)(2,1)S(1)}, bf16[4,104,640]{2,1,0:T(8,128)(2,1)}, u32[]{:S(2)}, u32[]{:S(2)}) collective-permute-start(bf16[4,104,640]{2,1,0:T(8,128)(2,1)S(1)} %constant_dynamic-update-slice_fusion.refs_0_), channel_id=1, source_target_pairs={{0,96},{4,100},{8,104},{12,108},{16,112},{20,116},{24,120},{28,124... | collective-permute-start | bytes 1597448 | tf_op jit(solution)/shard_map/ppermute | solution.py:575
  83.3 13.5 %collective-permute-start.21 = (bf16[4,104,640]{2,1,0:T(8,128)(2,1)S(1)}, bf16[4,104,640]{2,1,0:T(8,128)(2,1)}, u32[]{:S(2)}, u32[]{:S(2)}) collective-permute-start(bf16[4,104,640]{2,1,0:T(8,128)(2,1)S(1)} %constant_dynamic-update-slice_fusion.4.refs_4_), channel_id=1, source_target_pairs={{0,8},{4,12},{8,0},{12,4},{16,24},{20,28},{24,16},{28,20},{32,40},... | collective-permute-start | bytes 1597448 | tf_op jit(solution)/shard_map/ppermute | solution.py:575
  85.5 11.3 %collective-permute-start.27 = (bf16[4,104,640]{2,1,0:T(8,128)(2,1)S(1)}, bf16[4,104,640]{2,1,0:T(8,128)(2,1)}, u32[]{:S(2)}, u32[]{:S(2)}) collective-permute-start(bf16[4,104,640]{2,1,0:T(8,128)(2,1)S(1)} %constant_dynamic-update-slice_fusion.8.refs_8_), channel_id=1, source_target_pairs={{0,32},{4,36},{8,40},{12,44},{16,48},{20,52},{24,56},{28,60},{32,0... | collective-permute-start | bytes 1597448 | tf_op jit(solution)/shard_map/ppermute | solution.py:575
  85.5 13.3 %collective-permute-start.33 = (bf16[4,104,640]{2,1,0:T(8,128)(2,1)S(1)}, bf16[4,104,640]{2,1,0:T(8,128)(2,1)}, u32[]{:S(2)}, u32[]{:S(2)}) collective-permute-start(bf16[4,104,640]{2,1,0:T(8,128)(2,1)S(1)} %constant_dynamic-update-slice_fusion.12.refs_12_), channel_id=1, source_target_pairs={{0,24},{4,28},{8,16},{12,20},{16,8},{20,12},{24,0},{28,4},{32,56},... | collective-permute-start | bytes 1597448 | tf_op jit(solution)/shard_map/ppermute | solution.py:575
  87.9 16.0 %all-to-all-start = ((bf16[16,8,1792]{2,1,0:T(8,128)(2,1)}), bf16[16,8,1792]{2,1,0:T(8,128)(2,1)S(1)}, u32[]{:S(2)}, u32[]{:S(2)}) async-start(bf16[16,8,1792]{2,1,0:T(8,128)(2,1)} %bitcast.7), calls=%async_computation | async-start | bytes 917504 | tf_op jit(solution)/shard_map/all_to_all | solution.py:629
  92.9 27.0 %collective-permute-start.16 = (bf16[4,104,640]{2,1,0:T(8,128)(2,1)S(1)}, bf16[4,104,640]{2,1,0:T(8,128)(2,1)}, u32[]{:S(2)}, u32[]{:S(2)}) collective-permute-start(bf16[4,104,640]{2,1,0:T(8,128)(2,1)S(1)} %collective-permute-done.14.refs_1_), channel_id=1, source_target_pairs={{0,96},{4,100},{8,104},{12,108},{16,112},{20,116},{24,120},{28,124... | collective-permute-start | bytes 1597448 | tf_op jit(solution)/shard_map/ppermute | solution.py:575
  95.6 24.4 %collective-permute-start.22 = (bf16[4,104,640]{2,1,0:T(8,128)(2,1)}, bf16[4,104,640]{2,1,0:T(8,128)(2,1)}, u32[]{:S(2)}, u32[]{:S(2)}) collective-permute-start(bf16[4,104,640]{2,1,0:T(8,128)(2,1)} %copy-done.4), channel_id=1, source_target_pairs={{0,8},{4,12},{8,0},{12,4},{16,24},{20,28},{24,16},{28,20},{32,40},... | collective-permute-start | bytes 1597448 | tf_op jit(solution)/shard_map/ppermute | solution.py:575
  96.8 23.2 %collective-permute-start.28 = (bf16[4,104,640]{2,1,0:T(8,128)(2,1)}, bf16[4,104,640]{2,1,0:T(8,128)(2,1)}, u32[]{:S(2)}, u32[]{:S(2)}) collective-permute-start(bf16[4,104,640]{2,1,0:T(8,128)(2,1)} %copy-done.6), channel_id=1, source_target_pairs={{0,32},{4,36},{8,40},{12,44},{16,48},{20,52},{24,56},{28,60},{32,0... | collective-permute-start | bytes 1597448 | tf_op jit(solution)/shard_map/ppermute | solution.py:575
  96.8 23.2 %collective-permute-start.34 = (bf16[4,104,640]{2,1,0:T(8,128)(2,1)}, bf16[4,104,640]{2,1,0:T(8,128)(2,1)}, u32[]{:S(2)}, u32[]{:S(2)}) collective-permute-start(bf16[4,104,640]{2,1,0:T(8,128)(2,1)} %collective-permute-done.32.refs_13_), channel_id=1, source_target_pairs={{0,24},{4,28},{8,16},{12,20},{16,8},{20,12},{24,0},{28,4},{32,56},... | collective-permute-start | bytes 1597448 | tf_op jit(solution)/shard_map/ppermute | solution.py:575
  104.0 21.1 %collective-permute-start.9 = (bf16[128,1792]{1,0:T(8,128)(2,1)S(1)}, bf16[128,1792]{1,0:T(8,128)(2,1)}, u32[]{:S(2)}, u32[]{:S(2)}) collective-permute-start(bf16[128,1792]{1,0:T(8,128)(2,1)S(1)} %bitcast.15), channel_id=1, source_target_pairs={{0,4},{4,0},{8,12},{12,8},{16,20},{20,16},{24,28},{28,24},{32,36},... | collective-permute-start | bytes 1376264 | tf_op jit(solution)/shard_map/ppermute | solution.py:632
  132.2 10.8 %collective-permute-start.35 = (bf16[128,832]{1,0:T(8,128)(2,1)S(1)}, bf16[128,832]{1,0:T(8,128)(2,1)S(1)}, u32[]{:S(2)}, u32[]{:S(2)}) collective-permute-start(bf16[128,832]{1,0:T(8,128)(2,1)S(1)} %get-tuple-element.45), channel_id=1, source_target_pairs={{0,4},{4,0},{8,12},{12,8},{16,20},{20,16},{24,28},{28,24},{32,36},... | collective-permute-start | bytes 638984 | tf_op jit(solution)/shard_map/ppermute | solution.py:518
  (9 other events, 14.2 us)

commit v3 on v2

--- a/solution.py
+++ b/solution.py
@@ -27,11 +27,9 @@
     return 0.5 * value * (1.0 + lax.erf(value * (1.0 / math.sqrt(2.0))))
 
 
-def feed_tiles(rows, up_ref, up_bias_ref, down_ref, wait=None, tile=256):
+def feed_tiles(rows, up_ref, up_bias_ref, down_ref, tile=256):
     total = None
     for at in range(0, up_ref.shape[0], tile):
-        if wait is not None:
-            wait(at // tile)
         upward = lax.dot_general(
             rows,
             up_ref[at : at + tile],
@@ -44,48 +42,39 @@
     return total
 
 
-def first_kernel(
+def arrange_kernel(
     lane_ref,
     rows_hbm,
     dest_ref,
     gain_ref,
     bias_ref,
     up_hbm,
-    up_bias_ref,
     down_hbm,
-    first_ref,
-    second_ref,
     normed_ref,
     own_ref,
-    rows_ref,
     up_ref,
     down_ref,
-    far_ref,
+    rows_ref,
     row_sems,
-    up_sems,
-    down_sems,
+    sems,
 ):
     lane = lane_ref[0]
     count = rows_hbm.shape[0] // 4
     part = count // 4
-    tile = up_hbm.shape[0] // 4
-
-    def copies(source, target, sems, size):
-        return [
-            pltpu.make_async_copy(
-                source.at[pl.ds(i * size, size)], target.at[pl.ds(i * size, size)], sems.at[i]
-            )
-            for i in range(4)
-        ]
-
-    row_copies = copies(rows_hbm, rows_ref, row_sems, count)
-    up_copies = copies(up_hbm, up_ref, up_sems, tile)
-    down_copies = copies(down_hbm, down_ref, down_sems, tile)
+    row_copies = [
+        pltpu.make_async_copy(
+            rows_hbm.at[pl.ds(i * count, count)],
+            rows_ref.at[pl.ds(i * count, count)],
+            row_sems.at[i],
+        )
+        for i in range(4)
+    ]
+    up_copy = pltpu.make_async_copy(up_hbm, up_ref, sems.at[0])
+    down_copy = pltpu.make_async_copy(down_hbm, down_ref, sems.at[1])
     for copy in row_copies:
         copy.start()
-    for i in range(4):
-        up_copies[i].start()
-        down_copies[i].start()
+    up_copy.start()
+    down_copy.start()
     index = lax.broadcasted_iota(jnp.int32, (count, count), 0)
     step = index // part
     wanted = 4 * (index - step * part) + ((lane + relative_offset(step)) & 3)
@@ -97,21 +86,13 @@
         moved = jnp.dot(
             hits, normed.astype(jnp.bfloat16), preferred_element_type=jnp.float32
         ).astype(jnp.bfloat16)
-        far_ref[b * part : (b + 1) * part] = moved[:part]
-        for k in range(3):
-            normed_ref[k, b * part : (b + 1) * part] = moved[(k + 1) * part : (k + 2) * part]
+        for k in range(4):
+            normed_ref[k, b * part : (b + 1) * part] = moved[k * part : (k + 1) * part]
         own_ref[b * part : (b + 1) * part] = jnp.dot(
             hits[3 * part :], rows, preferred_element_type=jnp.float32
         ).astype(jnp.bfloat16)
-
-    def wait(i):
-        up_copies[i].wait()
-        down_copies[i].wait()
-
-    total = feed_tiles(far_ref[...], up_ref, up_bias_ref, down_ref, wait, tile)
-    half = count // 2
-    first_ref[...] = total[:half].astype(jnp.bfloat16)
-    second_ref[...] = total[half:].astype(jnp.bfloat16)
+    up_copy.wait()
+    down_copy.wait()
 
 
 VMEM = pl.BlockSpec(memory_space=pltpu.VMEM)
@@ -119,41 +100,48 @@
 HBM = pl.BlockSpec(memory_space=pltpu.HBM)
 
 
-def first(lane, residual_in, merge_dest, gain, bias, up_weight, up_bias, down_weight):
+def in_hbm(array):
+    return pltpu.with_memory_space_constraint(array, pltpu.HBM)
+
+
+def arrange(lane, residual_in, merge_dest, gain, bias, up_weight, down_weight):
     group_rows, width = residual_in.shape
     count = group_rows // 4
-    half = count // 2
     bf16 = jnp.bfloat16
     return pl.pallas_call(
-        first_kernel,
-        in_specs=[SMEM, HBM, VMEM, VMEM, VMEM, HBM, VMEM, HBM],
+        arrange_kernel,
+        in_specs=[SMEM, HBM, VMEM, VMEM, VMEM, HBM, HBM],
         out_specs=[VMEM] * 4,
         out_shape=[
-            jax.ShapeDtypeStruct((half, width), bf16),
-            jax.ShapeDtypeStruct((half, width), bf16),
-            jax.ShapeDtypeStruct((3, count, width), bf16),
-            jax.ShapeDtypeStruct((count, width), bf16),
+            pltpu.VMEM((4, count, width), bf16),
+            pltpu.VMEM((count, width), bf16),
+            pltpu.VMEM(up_weight.shape, bf16),
+            pltpu.VMEM(down_weight.shape, bf16),
         ],
         scratch_shapes=[
             pltpu.VMEM(residual_in.shape, bf16),
-            pltpu.VMEM(up_weight.shape, bf16),
-            pltpu.VMEM(down_weight.shape, bf16),
-            pltpu.VMEM((count, width), bf16),
             pltpu.SemaphoreType.DMA((4,)),
-            pltpu.SemaphoreType.DMA((4,)),
-            pltpu.SemaphoreType.DMA((4,)),
+            pltpu.SemaphoreType.DMA((2,)),
         ],
-        compiler_params=pltpu.CompilerParams(vmem_limit_bytes=32 * MIB),
+        compiler_params=pltpu.CompilerParams(vmem_limit_bytes=16 * MIB),
         cost_estimate=FEED_COST,
-        name="first",
-    )(lane, residual_in, merge_dest.reshape(4, 1, count), gain, bias, up_weight, up_bias, down_weight)
-
-
-def feed_kernel(rows_ref, up_ref, up_bias_ref, down_ref, first_ref, second_ref):
+        name="arrange",
+    )(
+        lane,
+        in_hbm(residual_in),
+        merge_dest.reshape(4, 1, count),
+        gain,
+        bias,
+        in_hbm(up_weight),
+        in_hbm(down_weight),
+    )
+
+
+def feed_kernel(rows_ref, up_ref, up_bias_ref, down_ref, *out_refs):
     total = feed_tiles(rows_ref[...], up_ref, up_bias_ref, down_ref)
-    half = first_ref.shape[0]
-    first_ref[...] = total[:half].astype(jnp.bfloat16)
-    second_ref[...] = total[half:].astype(jnp.bfloat16)
+    size = out_refs[0].shape[0]
+    for i, ref in enumerate(out_refs):
+        ref[...] = total[i * size : (i + 1) * size].astype(jnp.bfloat16)
 
 
 def feed_own_kernel(
@@ -163,15 +151,14 @@
     out_ref[...] = total + (residual_ref[...].astype(jnp.float32) + down_bias_ref[...])
 
 
-FEED_COST = pl.CostEstimate(flops=7 << 28, bytes_accessed=1 << 22, transcendentals=0)
-
-
-def feed(rows, step, up_weight, up_bias, down_weight, extra=None):
+FEED_COST = pl.CostEstimate(flops=1 << 20, bytes_accessed=1 << 16, transcendentals=0)
+
+
+def feed(rows, step, up_weight, up_bias, down_weight, extra=None, pieces=1):
     _, count, width = rows.shape
     args = [rows, up_weight, up_bias, down_weight]
     if extra is None:
-        half = count // 2
-        out_shape = [jax.ShapeDtypeStruct((half, width), jnp.bfloat16)] * 2
+        out_shape = [jax.ShapeDtypeStruct((count // pieces, width), jnp.bfloat16)] * pieces
         kernel = feed_kernel
     else:
         args += list(extra)
@@ -184,7 +171,7 @@
     return pl.pallas_call(
         wrapped,
         in_specs=[VMEM] * len(args),
-        out_specs=[VMEM] * 2 if extra is None else VMEM,
+        out_specs=[VMEM] * pieces if extra is None else VMEM,
         out_shape=out_shape,
         compiler_params=pltpu.CompilerParams(vmem_limit_bytes=16 * MIB),
         cost_estimate=FEED_COST,
@@ -193,39 +180,58 @@
 
 
 def project_kernel(
-    lane_ref, base_ref, a1_ref, a2_ref, b1_ref, b2_ref, weight_ref, o0, o1, o2, own, total_ref
+    lane_ref,
+    base_ref,
+    onward_top,
+    onward_low,
+    back_top,
+    back_low,
+    weight_ref,
+    fa,
+    fb,
+    following,
+    previous,
+    own,
+    total_ref,
 ):
-    half = a1_ref.shape[0]
-    part = half // 2
-    top = base_ref[:half] + a1_ref[...].astype(jnp.float32) + a2_ref[...].astype(jnp.float32)
-    low = base_ref[half:] + b1_ref[...].astype(jnp.float32) + b2_ref[...].astype(jnp.float32)
-    rows = jnp.concatenate([top, low], axis=0).astype(jnp.bfloat16)
-    total_ref[...] = jnp.dot(rows, weight_ref[...], preferred_element_type=jnp.float32)
+    split = onward_top.shape[0]
+    top = base_ref[:split] + onward_top[...].astype(jnp.float32) + back_top[...].astype(jnp.float32)
+    low = base_ref[split:] + onward_low[...].astype(jnp.float32) + back_low[...].astype(jnp.float32)
+    rows = jnp.concatenate([top, low], axis=0)
+    total_ref[...] = jnp.dot(
+        rows.astype(jnp.bfloat16), weight_ref[...], preferred_element_type=jnp.float32
+    )
     lane = lane_ref[0]
-    for offset, ref in ((2, o0), (1, o1), (3, o2), (0, own)):
-        start = pl.multiple_of(((lane + offset) & 3) * part, part)
-        ref[...] = total_ref[pl.ds(start, part)].astype(ref.dtype)
-
-
-def project(lane, base, a1, a2, b1, b2, weight):
+    half = fa.shape[0]
+    part = 2 * half
+
+    def block(offset, at, size):
+        start = pl.multiple_of(((lane + offset) & 3) * part + at, half)
+        return total_ref[pl.ds(start, size)]
+
+    fa[...] = block(2, 0, half).astype(jnp.bfloat16)
+    fb[...] = block(2, half, half).astype(jnp.bfloat16)
+    following[...] = block(1, 0, part).astype(jnp.bfloat16)
+    previous[...] = block(3, 0, part).astype(jnp.bfloat16)
+    own[...] = block(0, 0, part)
+
+
+def project(lane, base, halves, weight):
     count, width = base.shape
     part = count // 4
-    vmem = pl.BlockSpec(memory_space=pltpu.VMEM)
+    bf16 = jnp.bfloat16
     return pl.pallas_call(
         project_kernel,
-        in_specs=[pl.BlockSpec(memory_space=pltpu.SMEM)] + [vmem] * 6,
-        out_specs=[vmem] * 4,
-        out_shape=[jax.ShapeDtypeStruct((part, width), jnp.bfloat16)] * 3
+        in_specs=[SMEM] + [VMEM] * 6,
+        out_specs=[VMEM] * 5,
+        out_shape=[jax.ShapeDtypeStruct((part // 2, width), bf16)] * 2
+        + [jax.ShapeDtypeStruct((part, width), bf16)] * 2
         + [jax.ShapeDtypeStruct((part, width), jnp.float32)],
         scratch_shapes=[pltpu.VMEM((count, width), jnp.float32)],
-        compiler_params=pltpu.CompilerParams(vmem_limit_bytes=24 * MIB),
-        cost_estimate=pl.CostEstimate(
-            flops=2 * count * width * width,
-            bytes_accessed=2 * width * width + 12 * count * width,
-            transcendentals=0,
-        ),
+        compiler_params=pltpu.CompilerParams(vmem_limit_bytes=16 * MIB),
+        cost_estimate=FEED_COST,
         name="project",
-    )(lane, base, a1, a2, b1, b2, weight)
+    )(lane, base, *halves, weight)
 
 
 def turn(column):
@@ -237,7 +243,7 @@
 
 
 def route_kernel(
-    lane_ref, own_ref, r0, r1, r2, counts_ref, owners_ref, dest_ref, seg_ref, out_ref
+    lane_ref, own_ref, r0, r1, counts_ref, owners_ref, dest_ref, seg_ref, out_ref
 ):
     lane = lane_ref[0]
     rows, width = own_ref.shape
@@ -247,7 +253,6 @@
         own_ref[...]
         + r0[...].astype(jnp.float32)
         + r1[...].astype(jnp.float32)
-        + r2[...].astype(jnp.float32)
     ).astype(jnp.bfloat16)
     counts = counts_ref[...] // 4
     earlier = lax.broadcasted_iota(jnp.int32, (pieces, pieces), 1) < lax.broadcasted_iota(
@@ -296,11 +301,10 @@
     rows, width = own.shape
     pieces = lengths.shape[0]
     block = merge_dest.shape[0] // 4
-    vmem = pl.BlockSpec(memory_space=pltpu.VMEM)
     return pl.pallas_call(
         route_kernel,
-        in_specs=[pl.BlockSpec(memory_space=pltpu.SMEM)] + [vmem] * 8,
-        out_specs=vmem,
+        in_specs=[SMEM] + [VMEM] * 7,
+        out_specs=VMEM,
         out_shape=jax.ShapeDtypeStruct((2 * rows, width + 128), jnp.bfloat16),
         compiler_params=pltpu.CompilerParams(vmem_limit_bytes=24 * MIB),
         name="route",
@@ -379,34 +383,55 @@
     )(core, own, other)
 
 
-ORDERS = ((1, 4, 3, 12), (4, 3, 12, 1), (3, 12, 1, 4), (12, 1, 4, 3))
-
-
-def assemble(chip, streams, chips):
-    _, depth, size = streams[0][0].shape
-
-    def kernel(chip_ref, *refs):
-        out_ref = refs[-1]
+ORDERS = (((1, 4, 3, 12), (4, 3, 12, 1)), ((3, 12, 1, 4), (12, 1, 4, 3)))
+
+
+def masks(order):
+    found = [0]
+    for bit in order:
+        found += [bit ^ mask for mask in found]
+    return found
+
+
+def assemble(chip, core, streams, chips):
+    held, depth, size = streams[0][0].shape
+    arrays = len(streams[0])
+
+    def kernel(chip_ref, core_ref, *refs):
+        *held_refs, out_ref, token_ref, sems = refs
         chip_id = chip_ref[0]
-        for s, order in enumerate(ORDERS):
-            d1, d2, d3, d4 = order
-            inner = (0, d1, d2, d2 ^ d1)
-            for a, outer in enumerate((0, d3, d4, d4 ^ d3)):
-                for i, mask in enumerate(inner):
-                    out_ref[chip_id ^ (outer ^ mask), :, s * size : (s + 1) * size] = refs[
-                        4 * s + a
-                    ][i]
-
-    flat = [array for stream in streams for array in stream]
+        core_id = core_ref[0]
+        copies = []
+        for s, orders in enumerate(ORDERS):
+            for i, (low, high) in enumerate(zip(masks(orders[0]), masks(orders[1]))):
+                at = chip_id ^ jnp.where(core_id == 0, low, high)
+                copies.append(
+                    pltpu.make_async_copy(
+                        held_refs[arrays * s + i // held].at[i % held],
+                        out_ref.at[at, :, pl.ds(s * size, size)],
+                        sems.at[len(copies)],
+                    )
+                )
+        for copy in copies:
+            copy.start()
+        for copy in copies:
+            copy.wait()
+        token_ref[...] = jnp.zeros_like(token_ref)
+
+    flat = [in_hbm(array) for stream in streams for array in stream]
     return pl.pallas_call(
         kernel,
-        in_specs=[SMEM] + [VMEM] * len(flat),
-        out_specs=VMEM,
-        out_shape=jax.ShapeDtypeStruct((chips, depth, size * len(ORDERS)), jnp.bfloat16),
-        compiler_params=pltpu.CompilerParams(vmem_limit_bytes=30 * MIB),
-        cost_estimate=pl.CostEstimate(flops=0, bytes_accessed=1 << 24, transcendentals=0),
+        in_specs=[SMEM, SMEM] + [HBM] * len(flat),
+        out_specs=[VMEM, VMEM],
+        out_shape=[
+            pltpu.VMEM((chips, depth, size * len(ORDERS)), jnp.bfloat16),
+            jax.ShapeDtypeStruct((8, 128), jnp.float32),
+        ],
+        scratch_shapes=[pltpu.SemaphoreType.DMA((chips * len(ORDERS),))],
+        compiler_params=pltpu.CompilerParams(vmem_limit_bytes=4 * MIB),
+        cost_estimate=pl.CostEstimate(flops=1 << 30, bytes_accessed=1 << 24, transcendentals=0),
         name="assemble",
-    )(chip, *flat)
+    )(chip, core, *flat)
 
 
 def attention(heads_ref, base, tags, count, width, out_ref):
@@ -443,6 +468,7 @@
     gain_ref,
     bias_ref,
     weight_ref,
+    token_ref,
     merged_ref,
     other_ref,
     heads_out_ref,
@@ -497,13 +523,13 @@
         out_ref[:, half:] = mine_ref[...]
 
 
-def attend(core, mine, theirs, gain, bias, weight, sibling):
+def attend(core, mine, theirs, gain, bias, weight, token, sibling):
     count = mine.shape[0]
     width, columns = weight.shape
     bf16 = jnp.bfloat16
     merged, other, heads, tags = pl.pallas_call(
         attend_kernel,
-        in_specs=[SMEM] + [VMEM] * 5,
+        in_specs=[SMEM] + [VMEM] * 5 + [pl.BlockSpec(memory_space=pl.ANY)],
         out_specs=[VMEM] * 4,
         out_shape=[
             jax.ShapeDtypeStruct((count, width), bf16),
@@ -514,7 +540,7 @@
         scratch_shapes=[pltpu.VMEM((2 * count, columns), bf16)],
         compiler_params=pltpu.CompilerParams(vmem_limit_bytes=24 * MIB),
         name="attend",
-    )(core, mine, theirs, gain, bias, weight)
+    )(core, mine, theirs, gain, bias, weight, token)
     other = lax.ppermute(other, "req", sibling)
     own = pl.pallas_call(
         attend_own_kernel,
@@ -558,7 +584,6 @@
     lane = lax.axis_index("mlp").astype(jnp.int32).reshape(1)
     onward = [(i, (i + 1) % lanes) for i in range(lanes)]
     back = [(i, (i - 1) % lanes) for i in range(lanes)]
-    across = [(i, (i + 2) % lanes) for i in range(lanes)]
 
     def row(vector):
         return vector.reshape(1, -1)
@@ -571,80 +596,86 @@
     senders = lax.axis_size("req")
     sibling = [(i, i ^ 1) for i in range(senders)]
 
-    def swap(array, mask):
-        return lax.ppermute(array, "req", [(i, i ^ (2 * mask)) for i in range(senders)])
-
+    def swap(array, stream, step):
+        partners = [i ^ (2 * ORDERS[stream][i & 1][step]) for i in range(senders)]
+        return lax.ppermute(array, "req", list(enumerate(partners)))
+
+    def step(arrays, index):
+        return tuple(swap(array, s, index) for s, array in enumerate(arrays))
+
+    tie = lax.optimization_barrier
     keep, send = pack(core, next_weight.transpose(1, 0, 2))
-    chunks = pair(core, keep, lax.ppermute(send, "req", sibling), len(ORDERS))
-    got1 = [swap(chunks[s], order[0]) for s, order in enumerate(ORDERS)]
-    far_a, far_b, normed, own_rows = first(
-        lane,
-        residual_in,
-        merge_dest,
-        row(norm2_gain),
-        row(norm2_bias),
-        up_weight,
-        bias_up,
-        down_weight,
-    )
-    got2 = [
-        (swap(chunks[s], order[1]), swap(got1[s], order[1])) for s, order in enumerate(ORDERS)
-    ]
-    quads = [
-        jnp.concatenate([chunks[s], got1[s], got2[s][0], got2[s][1]], axis=0)
-        for s in range(len(ORDERS))
-    ]
-    got3 = [swap(quads[s], order[2]) for s, order in enumerate(ORDERS)]
-    got4 = [
-        (swap(quads[s], order[3]), swap(got3[s], order[3])) for s, order in enumerate(ORDERS)
-    ]
+    keep, residual_in = tie((keep, residual_in))
+    other = lax.ppermute(send, "req", sibling)
+    normed, own_rows, up_weight, down_weight = arrange(
+        lane, residual_in, merge_dest, norm2_gain, norm2_bias, up_weight, down_weight
+    )
+
+    def feed_step(index, *extra, pieces=1):
+        return feed(normed, index, up_weight, bias_up, down_weight, *extra, pieces=pieces)
+
+    other, normed = tie((other, normed))
+    chunks = pair(core, keep, other, len(ORDERS))
+    chunks, normed = tie((chunks, normed))
+    got = step(chunks, 0)
+    far_a, far_b = feed_step(0, pieces=2)
+    got, normed = tie((got, normed))
     far_a = lax.ppermute(far_a, "mlp", onward)
     far_b = lax.ppermute(far_b, "mlp", back)
-    next_a, next_b = feed(normed, 0, up_weight, bias_up, down_weight)
-    b1 = lax.ppermute(next_b, "mlp", onward)
-    prev_a, prev_b = feed(normed, 1, up_weight, bias_up, down_weight)
-    a2 = lax.ppermute(prev_a, "mlp", back)
+    two = tuple(jnp.concatenate(both, axis=0) for both in zip(chunks, got))
+    two, normed = tie((two, normed))
+    got2 = step(two, 1)
+    f0, f1 = feed_step(1, pieces=2)
+    p0, p1 = feed_step(2, pieces=2)
+    base = feed_step(3, (own_rows, row(down_bias)))
+    base, far_a, far_b, f0, f1, p0, p1, got2 = tie((base, far_a, far_b, f0, f1, p0, p1, got2))
 
     def join(first, second):
         return (first.astype(jnp.float32) + second.astype(jnp.float32)).astype(jnp.bfloat16)
 
-    a1 = lax.ppermute(join(far_a, next_a), "mlp", onward)
-    b2 = lax.ppermute(join(far_b, prev_b), "mlp", back)
-    base = feed(
-        normed,
-        2,
-        up_weight,
-        bias_up,
-        down_weight,
-        (own_rows, row(down_bias)),
-    )
-    p0, p1, p2, own = project(lane, base, a1, a2, b1, b2, proj_weight)
-    others = (
-        lax.ppermute(p0, "mlp", across),
-        lax.ppermute(p1, "mlp", onward),
-        lax.ppermute(p2, "mlp", back),
-    )
+    def hop(following, previous, far_a, far_b):
+        half = far_a.shape[0]
+        following = jnp.concatenate([join(following[:half], far_a), following[half:]], axis=0)
+        previous = jnp.concatenate([previous[:half], join(previous[half:], far_b)], axis=0)
+        return following, previous
+
+    def shift(following, previous):
+        return lax.ppermute(following, "mlp", onward), lax.ppermute(previous, "mlp", back)
+
+    four = tuple(jnp.concatenate(both, axis=0) for both in zip(two, got2))
+    joined = tie((join(f0, far_a), join(p1, far_b), four))
+    onward_top, back_low = shift(*joined[:2])
+    four = joined[2]
+    got3 = step(four, 2)
+    onward_top, back_low, got3, four, f1, p0 = tie((onward_top, back_low, got3, four, f1, p0))
+    onward_low, back_top = shift(f1, p0)
+    got4 = step(four, 3)
+    halves = (onward_top, onward_low, back_top, back_low)
+    halves, got4, got3 = tie((halves, got4, got3))
+    got5 = step(got3, 3)
+    far_a, far_b, following, previous, own = project(
+        lane, base, halves, proj_weight
+    )
+    far_a = lax.ppermute(far_a, "mlp", onward)
+    far_b = lax.ppermute(far_b, "mlp", back)
+    following, previous = hop(following, previous, far_a, far_b)
+    others = shift(following, previous)
     outgoing = route(lane, own, others, lengths, owners, merge_dest, segment_ids)
     groups = [[2 * i + c for i in range(senders // 2)] for c in range(2)]
     mine = lax.all_to_all(
         outgoing, "req", split_axis=0, concat_axis=0, axis_index_groups=groups, tiled=True
     )
+    full, token = assemble(chip, core, list(zip(four, got3, got4, got5)), senders // 2)
+    mine, token = tie((mine, token))
     theirs = lax.ppermute(mine, "req", sibling)
-    full = assemble(
-        chip,
-        [
-            (quads[s], got3[s], got4[s][0], got4[s][1])
-            for s in range(len(ORDERS))
-        ],
-        senders // 2,
-    )
     return attend(
         core,
         mine,
         theirs,
-        row(norm3_gain),
-        row(norm3_bias),
+        norm3_gain,
+        norm3_bias,
         full.reshape(width, -1),
+        token,
         sibling,
     )
 

time: 145 us -> 124 us (0.86)
  starting transfers between devices: 75.4 us -> 39.3 us
  waiting for transfers between devices: 19.2 us -> 37.5 us
  Pallas kernels: 35.9 us -> 34.1 us
    ppermute x32 -> x17, starting transfers between devices: 43.1 us -> 21.4 us  [the longest x10 11 us: swap(): return lax.ppermute(array, 'req', list(enumerate(partners)))]
    ppermute x32 -> x17, waiting for transfers between devices: 14 us -> 34.7 us  [the longest x3 16.9 us: shift(): lax.ppermute(following, 'mlp', onward)]
    ppermute x1, starting transfers between devices: 8.46 us -> 0.38 us  [attend(): other = lax.ppermute(other, 'req', sibling)]
    ppermute x1, starting transfers between devices: 15.9 us -> 7.88 us  [body(): theirs = lax.ppermute(mine, 'req', sibling)]
    all_to_all x1, waiting for transfers between devices: 5.19 us -> 0.11 us  [body(): lax.all_to_all(outgoing, 'req', split_axis=0, concat_axis=0, axis_index_g...]
    pallas_call x8 -> x9, Pallas kernels: 31.9 us -> 30.1 us  [the longest x4 11.8 us: feed(): pl.pallas_call(wrapped, in_specs=[VMEM] * len(args), out_specs=[VMEM] * p...]
    ppermute x1 -> x2, starting transfers between devices: 2.9 us -> 4.39 us  [body(): far_b = lax.ppermute(far_b, 'mlp', back)]
    unnamed x50 -> x44, local copies, waits for them, and re-layouts: 10.7 us -> 11.3 us
  transfers between devices with their start and end apart: 37 -> 24, of which waited for: 10 -> 14; matrix products, arithmetic and copies ran while one was open for 1% -> 0% of each run, Pallas kernels for 19% -> 19%
where the time goes in v3:
time: 124 us
  starting transfers between devices  39.3 us (32%)
  waiting for transfers between devices  37.5 us (30%)
  Pallas kernels  34.1 us (28%)
  local copies, waits for them, and re-layouts  11.4 us (9%)
    ppermute x3, waiting for transfers between devices, shift(): lax.ppermute(following, 'mlp', onward)  16.9 us
    ppermute x10, waiting for transfers between devices, swap(): return lax.ppermute(array, 'req', list(enumerate(partners)))  14.1 us
    pallas_call x4, Pallas kernels, feed(): pl.pallas_call(wrapped, in_specs=[VMEM] * len(args), out_specs=[VMEM] * p...  11.8 us
    unnamed x44, local copies, waits for them, and re-layouts  11.3 us
    ppermute x10, starting transfers between devices, swap(): return lax.ppermute(array, 'req', list(enumerate(partners)))  11 us
    ppermute x1, starting transfers between devices, body(): theirs = lax.ppermute(mine, 'req', sibling)  7.88 us
    ppermute x3, starting transfers between devices, shift(): lax.ppermute(previous, 'mlp', back)  6.8 us
    pallas_call x1, Pallas kernels, attend(): pl.pallas_call(attend_kernel, in_specs=[SMEM] + [VMEM] * 5 + [pl.BlockSpe...  6.14 us
  transfers between devices with their start and end apart: 24, of which 14 were waited for; matrix products, arithmetic and copies ran while one was open for 0% of the time, Pallas kernels for 19%

profile of v3, /device:TPU:1, one launch (start us, length us, event | category | flops | bytes accessed | tf_op | source)
XLA Modules:
  0.0 123.8 jit_solution(7071773967503330563)
XLA Ops:
  0.6 1.0 copy-done.2
  2.0 1.5 %collective-permute-start = (bf16[52,2560]{1,0:T(8,128)(2,1)S(1)}, bf16[52,2560]{1,0:T(8,128)(2,1)S(1)}, u32[]{:S(2)}, u32[]{:S(2)}) collective-permute-start(bf16[52,2560]{1,0:T(8,128)(2,1)S(1)} %get-tuple-element.73), channel_id=1, source_target_pairs={{0,4},{4,0},{8,12},{12,8},{16,20},{20,16},{24,28},{28,24},{32,36},... | collective-permute-start | bytes 798728 | tf_op jit(solution)/shard_map/ppermute | solution.py:609
  3.5 0.7 copy-done.4
  4.2 0.7 copy-done.6
  4.9 0.7 copy-done.7
  5.6 5.1 %arrange.1 = (bf16[4,256,1664]{2,1,0:T(8,128)(2,1)S(1)}, bf16[256,1664]{1,0:T(8,128)(2,1)S(1)}, bf16[1024,1664]{1,0:T(8,128)(2,1)S(1)}, bf16[1024,1664]{1,0:T(8,128)(2,1)S(1)}) custom-call(s32[1]{0:T(128)} %bitcast.1.lane_ref, bf16[1024,1664]{1,0:T(8,128)(2,1)} %rows_hbm, s32[4,1,256]{2,1,0:T(1,128)S(1)} %bitcast.22, f32[1664]{0:T(1024)S(1)} %copy-done.6, ...), custom_call_target="tpu_custom_call" | custom-call | flops 1048576 | bytes 65536 | tf_op jit(solution)/shard_map/arrange/pallas_call | solution.py:111
  10.7 0.4 pair.1
  11.1 1.8 %collective-permute-start.1 = (bf16[1,104,1280]{2,1,0:T(8,128)(2,1)S(1)}, bf16[1,104,1280]{2,1,0:T(8,128)(2,1)S(1)}, u32[]{:S(2)}, u32[]{:S(2)}) collective-permute-start(bf16[1,104,1280]{2,1,0:T(8,128)(2,1)S(1)} %get-tuple-element.80), channel_id=1, source_target_pairs={{0,8},{4,36},{8,0},{12,44},{16,24},{20,52},{24,16},{28,60},{32,40}... | collective-permute-start | bytes 798728 | tf_op jit(solution)/shard_map/ppermute | solution.py:601
  12.9 2.3 %collective-permute-start.2 = (bf16[1,104,1280]{2,1,0:T(8,128)(2,1)S(1)}, bf16[1,104,1280]{2,1,0:T(8,128)(2,1)S(1)}, u32[]{:S(2)}, u32[]{:S(2)}) collective-permute-start(bf16[1,104,1280]{2,1,0:T(8,128)(2,1)S(1)} %get-tuple-element.81), channel_id=1, source_target_pairs={{0,24},{4,100},{8,16},{12,108},{16,8},{20,116},{24,0},{28,124},{32... | collective-permute-start | bytes 798728 | tf_op jit(solution)/shard_map/ppermute | solution.py:601
  15.2 1.8 %collective-permute-done.1 = bf16[1,104,1280]{2,1,0:T(8,128)(2,1)S(1)} collective-permute-done((bf16[1,104,1280]{2,1,0:T(8,128)(2,1)S(1)}, bf16[1,104,1280]{2,1,0:T(8,128)(2,1)S(1)}, u32[]{:S(2)}, u32[]{:S(2)}) %collective-permute-start.1) | collective-permute-done | bytes 266272 | tf_op jit(solution)/shard_map/ppermute | solution.py:601
  17.0 2.7 %collective-permute-done.2 = bf16[1,104,1280]{2,1,0:T(8,128)(2,1)S(1)} collective-permute-done((bf16[1,104,1280]{2,1,0:T(8,128)(2,1)S(1)}, bf16[1,104,1280]{2,1,0:T(8,128)(2,1)S(1)}, u32[]{:S(2)}, u32[]{:S(2)}) %collective-permute-start.2) | collective-permute-done | bytes 266272 | tf_op jit(solution)/shard_map/ppermute | solution.py:601
  19.8 2.3 %collective-permute-start.5 = (bf16[2,104,1280]{2,1,0:T(8,128)(2,1)S(1)}, bf16[2,104,1280]{2,1,0:T(8,128)(2,1)S(1)}, u32[]{:S(2)}, u32[]{:S(2)}) collective-permute-start(bf16[2,104,1280]{2,1,0:T(8,128)(2,1)S(1)} %get-tuple-element.96), channel_id=1, source_target_pairs={{0,32},{4,28},{8,40},{12,20},{16,48},{20,12},{24,56},{28,4},{32,0}... | collective-permute-start | bytes 1597448 | tf_op jit(solution)/shard_map/ppermute | solution.py:601
  22.1 3.0 %feed.5 = (bf16[128,1664]{1,0:T(8,128)(2,1)S(1)}, bf16[128,1664]{1,0:T(8,128)(2,1)S(1)}) custom-call(bf16[4,256,1664]{2,1,0:T(8,128)(2,1)S(1)} %get-tuple-element.86.rows_ref, bf16[1024,1664]{1,0:T(8,128)(2,1)S(1)} %get-tuple-element.87.refs_0_, f32[1,1024]{1,0:T(1,128)S(1)} %bitcast.18, bf16[1024,1664]{1,0:T(8,128)(2,1)S(1)} %get-tuple-element.88.refs_2_), custom_call_target="tpu_custom_call" | custom-call | flops 1048576 | bytes 65536 | tf_op jit(solution)/shard_map/feed/pallas_call | solution.py:171
  25.0 1.4 %collective-permute-start.3 = (bf16[128,1664]{1,0:T(8,128)(2,1)S(1)}, bf16[128,1664]{1,0:T(8,128)(2,1)S(1)}, u32[]{:S(2)}, u32[]{:S(2)}) collective-permute-start(bf16[128,1664]{1,0:T(8,128)(2,1)S(1)} %get-tuple-element.90), channel_id=1, source_target_pairs={{0,1},{1,2},{2,3},{3,0},{4,5},{5,6},{6,7},{7,4},{8,9},{9,10},{10,1... | collective-permute-start | bytes 1277960 | tf_op jit(solution)/shard_map/ppermute | solution.py:623
  26.4 1.7 %collective-permute-start.4 = (bf16[128,1664]{1,0:T(8,128)(2,1)S(1)}, bf16[128,1664]{1,0:T(8,128)(2,1)S(1)}, u32[]{:S(2)}, u32[]{:S(2)}) collective-permute-start(bf16[128,1664]{1,0:T(8,128)(2,1)S(1)} %get-tuple-element.91), channel_id=1, source_target_pairs={{0,3},{1,0},{2,1},{3,2},{4,7},{5,4},{6,5},{7,6},{8,11},{9,8},{10,9... | collective-permute-start | bytes 1277960 | tf_op jit(solution)/shard_map/ppermute | solution.py:624
  28.1 2.9 %feed.7 = (bf16[128,1664]{1,0:T(8,128)(2,1)S(1)}, bf16[128,1664]{1,0:T(8,128)(2,1)S(1)}) custom-call(bf16[4,256,1664]{2,1,0:T(8,128)(2,1)S(1)} %get-tuple-element.86.rows_ref, bf16[1024,1664]{1,0:T(8,128)(2,1)S(1)} %get-tuple-element.87.refs_0_, f32[1,1024]{1,0:T(1,128)S(1)} %bitcast.19, bf16[1024,1664]{1,0:T(8,128)(2,1)S(1)} %get-tuple-element.88.refs_2_), custom_call_target="tpu_custom_call" | custom-call | flops 1048576 | bytes 65536 | tf_op jit(solution)/shard_map/feed/pallas_call | solution.py:171
  31.1 2.9 %feed.6 = (bf16[128,1664]{1,0:T(8,128)(2,1)S(1)}, bf16[128,1664]{1,0:T(8,128)(2,1)S(1)}) custom-call(bf16[4,256,1664]{2,1,0:T(8,128)(2,1)S(1)} %get-tuple-element.86.rows_ref, bf16[1024,1664]{1,0:T(8,128)(2,1)S(1)} %get-tuple-element.87.refs_0_, f32[1,1024]{1,0:T(1,128)S(1)} %bitcast.20, bf16[1024,1664]{1,0:T(8,128)(2,1)S(1)} %get-tuple-element.88.refs_2_), custom_call_target="tpu_custom_call" | custom-call | flops 1048576 | bytes 65536 | tf_op jit(solution)/shard_map/feed/pallas_call | solution.py:171
  34.1 3.0 %feed.4.base_ref = f32[256,1664]{1,0:T(8,128)S(1)} custom-call(bf16[4,256,1664]{2,1,0:T(8,128)(2,1)S(1)} %get-tuple-element.86.rows_ref, bf16[1024,1664]{1,0:T(8,128)(2,1)S(1)} %get-tuple-element.87.refs_0_, f32[1,1024]{1,0:T(1,128)S(1)} %bitcast.21, bf16[1024,1664]{1,0:T(8,128)(2,1)S(1)} %get-tuple-element.88.refs_2_, ...), custom_call_target="tpu_custom_call" | custom-call | flops 1048576 | bytes 65536 | tf_op jit(solution)/shard_map/feed/pallas_call | solution.py:171
  37.5 2.6 %collective-permute-start.9 = (bf16[4,104,1280]{2,1,0:T(8,128)(2,1)S(1)}, bf16[4,104,1280]{2,1,0:T(8,128)(2,1)}, u32[]{:S(2)}, u32[]{:S(2)}) collective-permute-start(bf16[4,104,1280]{2,1,0:T(8,128)(2,1)S(1)} %pad_maximum_fusion.refs_0_), channel_id=1, source_target_pairs={{0,24},{4,100},{8,16},{12,108},{16,8},{20,116},{24,0},{28,124},{32... | collective-permute-start | bytes 3194888 | tf_op jit(solution)/shard_map/ppermute | solution.py:601
  40.1 0.8 collective-permute-start.7
  40.9 1.9 %collective-permute-start.8 = (bf16[128,1664]{1,0:T(8,128)(2,1)S(1)}, bf16[128,1664]{1,0:T(8,128)(2,1)S(1)}, u32[]{:S(2)}, u32[]{:S(2)}) collective-permute-start(bf16[128,1664]{1,0:T(8,128)(2,1)S(1)} %add_convert_fusion), channel_id=1, source_target_pairs={{0,3},{1,0},{2,1},{3,2},{4,7},{5,4},{6,5},{7,6},{8,11},{9,8},{10,9... | collective-permute-start | bytes 1277960 | tf_op jit(solution)/shard_map/ppermute | solution.py:643
  42.8 7.2 %collective-permute-done.7.onward_top = bf16[128,1664]{1,0:T(8,128)(2,1)S(1)} collective-permute-done((bf16[128,1664]{1,0:T(8,128)(2,1)S(1)}, bf16[128,1664]{1,0:T(8,128)(2,1)S(1)}, u32[]{:S(2)}, u32[]{:S(2)}) %collective-permute-start.7) | collective-permute-done | bytes 426016 | tf_op jit(solution)/shard_map/ppermute | solution.py:643
  50.0 3.1 %collective-permute-done.9.refs_1_ = bf16[4,104,1280]{2,1,0:T(8,128)(2,1)} collective-permute-done((bf16[4,104,1280]{2,1,0:T(8,128)(2,1)S(1)}, bf16[4,104,1280]{2,1,0:T(8,128)(2,1)}, u32[]{:S(2)}, u32[]{:S(2)}) %collective-permute-start.9) | collective-permute-done | bytes 1064992 | tf_op jit(solution)/shard_map/ppermute | solution.py:601
  53.0 1.3 %collective-permute-done.10.refs_5_ = bf16[4,104,1280]{2,1,0:T(8,128)(2,1)} collective-permute-done((bf16[4,104,1280]{2,1,0:T(8,128)(2,1)S(1)}, bf16[4,104,1280]{2,1,0:T(8,128)(2,1)}, u32[]{:S(2)}, u32[]{:S(2)}) %collective-permute-start.10) | collective-permute-done | bytes 1064992 | tf_op jit(solution)/shard_map/ppermute | solution.py:601
  54.3 1.7 %collective-permute-start.13 = (bf16[4,104,1280]{2,1,0:T(8,128)(2,1)S(1)}, bf16[4,104,1280]{2,1,0:T(8,128)(2,1)S(1)}, u32[]{:S(2)}, u32[]{:S(2)}) collective-permute-start(bf16[4,104,1280]{2,1,0:T(8,128)(2,1)S(1)} %pad_maximum_fusion.refs_0_), channel_id=1, source_target_pairs={{0,96},{4,12},{8,104},{12,4},{16,112},{20,28},{24,120},{28,20},{32... | collective-permute-start | bytes 3194888 | tf_op jit(solution)/shard_map/ppermute | solution.py:601
  56.0 1.3 %collective-permute-start.11 = (bf16[128,1664]{1,0:T(8,128)(2,1)S(1)}, bf16[128,1664]{1,0:T(8,128)(2,1)S(1)}, u32[]{:S(2)}, u32[]{:S(2)}) collective-permute-start(bf16[128,1664]{1,0:T(8,128)(2,1)S(1)} %get-tuple-element.112), channel_id=1, source_target_pairs={{0,1},{1,2},{2,3},{3,0},{4,5},{5,6},{6,7},{7,4},{8,9},{9,10},{10,1... | collective-permute-start | bytes 1277960 | tf_op jit(solution)/shard_map/ppermute | solution.py:643
  57.3 1.6 %collective-permute-start.12 = (bf16[128,1664]{1,0:T(8,128)(2,1)S(1)}, bf16[128,1664]{1,0:T(8,128)(2,1)S(1)}, u32[]{:S(2)}, u32[]{:S(2)}) collective-permute-start(bf16[128,1664]{1,0:T(8,128)(2,1)S(1)} %get-tuple-element.113), channel_id=1, source_target_pairs={{0,3},{1,0},{2,1},{3,2},{4,7},{5,4},{6,5},{7,6},{8,11},{9,8},{10,9... | collective-permute-start | bytes 1277960 | tf_op jit(solution)/shard_map/ppermute | solution.py:643
  58.9 6.2 %collective-permute-done.11.onward_low = bf16[128,1664]{1,0:T(8,128)(2,1)S(1)} collective-permute-done((bf16[128,1664]{1,0:T(8,128)(2,1)S(1)}, bf16[128,1664]{1,0:T(8,128)(2,1)S(1)}, u32[]{:S(2)}, u32[]{:S(2)}) %collective-permute-start.11) | collective-permute-done | bytes 426016 | tf_op jit(solution)/shard_map/ppermute | solution.py:643
  65.0 1.0 collective-permute-done.12.back_top
  66.1 2.8 %collective-permute-done.13.refs_2_ = bf16[4,104,1280]{2,1,0:T(8,128)(2,1)S(1)} collective-permute-done((bf16[4,104,1280]{2,1,0:T(8,128)(2,1)S(1)}, bf16[4,104,1280]{2,1,0:T(8,128)(2,1)S(1)}, u32[]{:S(2)}, u32[]{:S(2)}) %collective-permute-start.13) | collective-permute-done | bytes 1064992 | tf_op jit(solution)/shard_map/ppermute | solution.py:601
  68.9 2.4 %collective-permute-done.14.refs_6_ = bf16[4,104,1280]{2,1,0:T(8,128)(2,1)S(1)} collective-permute-done((bf16[4,104,1280]{2,1,0:T(8,128)(2,1)S(1)}, bf16[4,104,1280]{2,1,0:T(8,128)(2,1)S(1)}, u32[]{:S(2)}, u32[]{:S(2)}) %collective-permute-start.14) | collective-permute-done | bytes 1064992 | tf_op jit(solution)/shard_map/ppermute | solution.py:601
  71.4 2.2 %project.1 = (bf16[32,1664]{1,0:T(8,128)(2,1)S(1)}, bf16[32,1664]{1,0:T(8,128)(2,1)S(1)}, bf16[64,1664]{1,0:T(8,128)(2,1)S(1)}, bf16[64,1664]{1,0:T(8,128)(2,1)S(1)}, f32[64,1664]{1,0:T(8,128)S(1)}) custom-call(s32[1]{0:T(128)} %bitcast.1.lane_ref, f32[256,1664]{1,0:T(8,128)S(1)} %feed.4.base_ref, bf16[128,1664]{1,0:T(8,128)(2,1)S(1)} %collective-permute-done.7.onward_top, ...), custom_call_target="tpu_custom_call" | custom-call | flops 1048576 | bytes 65536 | tf_op jit(solution)/shard_map/project/pallas_call | solution.py:223
  73.6 2.7 %collective-permute-start.17 = (bf16[32,1664]{1,0:T(8,128)(2,1)S(1)}, bf16[32,1664]{1,0:T(8,128)(2,1)S(1)}, u32[]{:S(2)}, u32[]{:S(2)}) collective-permute-start(bf16[32,1664]{1,0:T(8,128)(2,1)S(1)} %get-tuple-element.127), channel_id=1, source_target_pairs={{0,3},{1,0},{2,1},{3,2},{4,7},{5,4},{6,5},{7,6},{8,11},{9,8},{10,9... | collective-permute-start | bytes 319496 | tf_op jit(solution)/shard_map/ppermute | solution.py:660
  76.8 1.2 collective-permute-done.17
  78.1 3.3 %collective-permute-start.18 = (bf16[64,1664]{1,0:T(8,128)(2,1)S(1)}, bf16[64,1664]{1,0:T(8,128)(2,1)S(1)}, u32[]{:S(2)}, u32[]{:S(2)}) collective-permute-start(bf16[64,1664]{1,0:T(8,128)(2,1)S(1)} %pad_maximum_fusion.5), channel_id=1, source_target_pairs={{0,3},{1,0},{2,1},{3,2},{4,7},{5,4},{6,5},{7,6},{8,11},{9,8},{10,9... | collective-permute-start | bytes 638984 | tf_op jit(solution)/shard_map/ppermute | solution.py:643
  81.6 2.6 %collective-permute-done.18.r1 = bf16[64,1664]{1,0:T(8,128)(2,1)S(1)} collective-permute-done((bf16[64,1664]{1,0:T(8,128)(2,1)S(1)}, bf16[64,1664]{1,0:T(8,128)(2,1)S(1)}, u32[]{:S(2)}, u32[]{:S(2)}) %collective-permute-start.18) | collective-permute-done | bytes 213024 | tf_op jit(solution)/shard_map/ppermute | solution.py:643
  84.2 3.5 %collective-permute-done.16.r0 = bf16[64,1664]{1,0:T(8,128)(2,1)S(1)} collective-permute-done((bf16[64,1664]{1,0:T(8,128)(2,1)S(1)}, bf16[64,1664]{1,0:T(8,128)(2,1)S(1)}, u32[]{:S(2)}, u32[]{:S(2)}) %collective-permute-start.16) | collective-permute-done | bytes 213024 | tf_op jit(solution)/shard_map/ppermute | solution.py:643
  87.8 1.2 route.1
  89.0 3.7 %all-to-all-start = ((bf16[16,8,1792]{2,1,0:T(8,128)(2,1)}), bf16[16,8,1792]{2,1,0:T(8,128)(2,1)S(1)}, u32[]{:S(2)}, u32[]{:S(2)}) async-start(bf16[16,8,1792]{2,1,0:T(8,128)(2,1)} %bitcast.8), calls=%async_computation | async-start | bytes 917504 | tf_op jit(solution)/shard_map/all_to_all | solution.py:665
  92.7 1.0 copy-done.17
  94.1 3.7 %assemble.1 = (bf16[16,104,2560]{2,1,0:T(8,128)(2,1)S(1)}, f32[8,128]{1,0:T(8,128)S(1)}) custom-call(s32[1]{0:T(128)} %bitcast.10.chip_ref, s32[1]{0:T(128)} %bitcast.core_ref, bf16[4,104,1280]{2,1,0:T(8,128)(2,1)} %copy-done.13, bf16[4,104,1280]{2,1,0:T(8,128)(2,1)} %collective-permute-done.9.refs_1_, bf16[4,104,1280]{2,1,0:T(8,128)(2,1)} %copy-done.15, ...), custom_call_target="tpu_custom_call" | custom-call | flops 1073741824 | bytes 16777216 | tf_op jit(solution)/shard_map/assemble/pallas_call | solution.py:422
  97.8 3.3 %copy-done = bf16[16,104,2560]{2,1,0:T(8,128)(2,1)} copy-done((bf16[16,104,2560]{2,1,0:T(8,128)(2,1)}, bf16[16,104,2560]{2,1,0:T(8,128)(2,1)S(1)}, u32[]{:S(2)}) %copy-start) | copy-done | bytes 8519704
  101.3 7.9 %collective-permute-start.21 = (bf16[128,1792]{1,0:T(8,128)(2,1)S(1)}, bf16[128,1792]{1,0:T(8,128)(2,1)S(1)}, u32[]{:S(2)}, u32[]{:S(2)}) collective-permute-start(bf16[128,1792]{1,0:T(8,128)(2,1)S(1)} %bitcast.15), channel_id=1, source_target_pairs={{0,4},{4,0},{8,12},{12,8},{16,20},{20,16},{24,28},{28,24},{32,36},... | collective-permute-start | bytes 1376264 | tf_op jit(solution)/shard_map/ppermute | solution.py:670
  109.2 1.4 %collective-permute-done.21.theirs_ref = bf16[128,1792]{1,0:T(8,128)(2,1)S(1)} collective-permute-done((bf16[128,1792]{1,0:T(8,128)(2,1)S(1)}, bf16[128,1792]{1,0:T(8,128)(2,1)S(1)}, u32[]{:S(2)}, u32[]{:S(2)}) %collective-permute-start.21) | collective-permute-done | bytes 458784 | tf_op jit(solution)/shard_map/ppermute | solution.py:670
  110.6 3.4 %copy-done.1 = bf16[16,104,2560]{2,1,0:T(8,128)(2,1)S(1)} copy-done((bf16[16,104,2560]{2,1,0:T(8,128)(2,1)S(1)}, bf16[16,104,2560]{2,1,0:T(8,128)(2,1)}, u32[]{:S(2)}) %copy-start.1) | copy-done | bytes 8519704
  114.0 6.1 %attend.1 = (bf16[128,1664]{1,0:T(8,128)(2,1)}, bf16[128,832]{1,0:T(8,128)(2,1)S(1)}, bf16[128,2560]{1,0:T(8,128)(2,1)S(1)}, f32[128,128]{1,0:T(8,128)S(1)}) custom-call(s32[1]{0:T(128)} %bitcast.core_ref, bf16[128,1792]{1,0:T(8,128)(2,1)S(1)} %bitcast.16, bf16[128,1792]{1,0:T(8,128)(2,1)S(1)} %collective-permute-done.21.theirs_ref, f32[1664]{0:T(1024)S(1)} %copy-done.8, ...), custom_call_target="tpu_custom_call" | custom-call | tf_op jit(solution)/shard_map/attend/pallas_call | solution.py:530
  120.6 2.4 %attend_own.1.mine_ref = bf16[128,832]{1,0:T(8,128)(2,1)S(1)} custom-call(bf16[128,2560]{1,0:T(8,128)(2,1)S(1)} %get-tuple-element.137.heads_ref, f32[128,128]{1,0:T(8,128)S(1)} %get-tuple-element.138.tags_ref), custom_call_target="tpu_custom_call" | custom-call | flops 1073741824 | bytes 1048576 | tf_op jit(solution)/shard_map/attend_own/pallas_call | solution.py:545
  122.9 0.9 finish.1
  (70 shorter events, 2.5 us)
Async XLA Ops:
  0.6 1.1 copy-start.2
  2.0 8.6 %collective-permute-start = (bf16[52,2560]{1,0:T(8,128)(2,1)S(1)}, bf16[52,2560]{1,0:T(8,128)(2,1)S(1)}, u32[]{:S(2)}, u32[]{:S(2)}) collective-permute-start(bf16[52,2560]{1,0:T(8,128)(2,1)S(1)} %get-tuple-element.73), channel_id=1, source_target_pairs={{0,4},{4,0},{8,12},{12,8},{16,20},{20,16},{24,28},{28,24},{32,36},... | collective-permute-start | bytes 798728 | tf_op jit(solution)/shard_map/ppermute | solution.py:609
  3.5 0.7 copy-start.4
  4.2 0.7 copy-start.6
  4.9 0.7 copy-start.7
  11.1 11.0 %copy-start.3 = (f32[1024]{0:T(1024)S(1)}, f32[1024]{0:T(1024)}, u32[]{:S(2)}) copy-start(f32[1024]{0:T(1024)} %param.23) | copy-start | bytes 12292
  11.1 5.9 %collective-permute-start.1 = (bf16[1,104,1280]{2,1,0:T(8,128)(2,1)S(1)}, bf16[1,104,1280]{2,1,0:T(8,128)(2,1)S(1)}, u32[]{:S(2)}, u32[]{:S(2)}) collective-permute-start(bf16[1,104,1280]{2,1,0:T(8,128)(2,1)S(1)} %get-tuple-element.80), channel_id=1, source_target_pairs={{0,8},{4,36},{8,0},{12,44},{16,24},{20,52},{24,16},{28,60},{32,40}... | collective-permute-start | bytes 798728 | tf_op jit(solution)/shard_map/ppermute | solution.py:601
  12.9 6.8 %collective-permute-start.2 = (bf16[1,104,1280]{2,1,0:T(8,128)(2,1)S(1)}, bf16[1,104,1280]{2,1,0:T(8,128)(2,1)S(1)}, u32[]{:S(2)}, u32[]{:S(2)}) collective-permute-start(bf16[1,104,1280]{2,1,0:T(8,128)(2,1)S(1)} %get-tuple-element.81), channel_id=1, source_target_pairs={{0,24},{4,100},{8,16},{12,108},{16,8},{20,116},{24,0},{28,124},{32... | collective-permute-start | bytes 798728 | tf_op jit(solution)/shard_map/ppermute | solution.py:601
  19.8 17.2 %collective-permute-start.5 = (bf16[2,104,1280]{2,1,0:T(8,128)(2,1)S(1)}, bf16[2,104,1280]{2,1,0:T(8,128)(2,1)S(1)}, u32[]{:S(2)}, u32[]{:S(2)}) collective-permute-start(bf16[2,104,1280]{2,1,0:T(8,128)(2,1)S(1)} %get-tuple-element.96), channel_id=1, source_target_pairs={{0,32},{4,28},{8,40},{12,20},{16,48},{20,12},{24,56},{28,4},{32,0}... | collective-permute-start | bytes 1597448 | tf_op jit(solution)/shard_map/ppermute | solution.py:601
  22.1 15.0 %collective-permute-start.6 = (bf16[2,104,1280]{2,1,0:T(8,128)(2,1)S(1)}, bf16[2,104,1280]{2,1,0:T(8,128)(2,1)S(1)}, u32[]{:S(2)}, u32[]{:S(2)}) collective-permute-start(bf16[2,104,1280]{2,1,0:T(8,128)(2,1)S(1)} %get-tuple-element.97), channel_id=1, source_target_pairs={{0,96},{4,12},{8,104},{12,4},{16,112},{20,28},{24,120},{28,20},{32... | collective-permute-start | bytes 1597448 | tf_op jit(solution)/shard_map/ppermute | solution.py:601
  22.1 6.0 %copy-start.19 = (f32[1664]{0:T(1024)S(1)}, f32[1664]{0:T(1024)}, u32[]{:S(2)}) copy-start(f32[1664]{0:T(1024)} %param.25) | copy-start | bytes 19972
  25.0 12.0 %collective-permute-start.3 = (bf16[128,1664]{1,0:T(8,128)(2,1)S(1)}, bf16[128,1664]{1,0:T(8,128)(2,1)S(1)}, u32[]{:S(2)}, u32[]{:S(2)}) collective-permute-start(bf16[128,1664]{1,0:T(8,128)(2,1)S(1)} %get-tuple-element.90), channel_id=1, source_target_pairs={{0,1},{1,2},{2,3},{3,0},{4,5},{5,6},{6,7},{7,4},{8,9},{9,10},{10,1... | collective-permute-start | bytes 1277960 | tf_op jit(solution)/shard_map/ppermute | solution.py:623
  26.4 10.6 %collective-permute-start.4 = (bf16[128,1664]{1,0:T(8,128)(2,1)S(1)}, bf16[128,1664]{1,0:T(8,128)(2,1)S(1)}, u32[]{:S(2)}, u32[]{:S(2)}) collective-permute-start(bf16[128,1664]{1,0:T(8,128)(2,1)S(1)} %get-tuple-element.91), channel_id=1, source_target_pairs={{0,3},{1,0},{2,1},{3,2},{4,7},{5,4},{6,5},{7,6},{8,11},{9,8},{10,9... | collective-permute-start | bytes 1277960 | tf_op jit(solution)/shard_map/ppermute | solution.py:624
  34.0 37.3 %slice-start = ((s8[5537792]{0:T(1024)(128)(4,1)}), s8[4194304]{0:T(1024)(128)(4,1)S(1)}, s32[]{:S(2)}) async-start(s8[5537792]{0:T(1024)(128)(4,1)} %bitcast.13), calls=%async_computation.1 | async-start | bytes 8388608
  34.1 37.3 %slice-start.1 = ((s8[5537792]{0:T(1024)(128)(4,1)}), s8[1343488]{0:T(1024)(128)(4,1)S(1)}, s32[]{:S(2)}) async-start(s8[5537792]{0:T(1024)(128)(4,1)} %bitcast.13), calls=%async_computation.2 | async-start | bytes 2686976
  37.2 17.2 %copy-start.13 = (bf16[4,104,1280]{2,1,0:T(8,128)(2,1)}, bf16[4,104,1280]{2,1,0:T(8,128)(2,1)S(1)}, u32[]{:S(2)}) copy-start(bf16[4,104,1280]{2,1,0:T(8,128)(2,1)S(1)} %pad_maximum_fusion.refs_0_) | copy-start | bytes 3194884
  37.3 18.7 %copy-start.14 = (bf16[4,104,1280]{2,1,0:T(8,128)(2,1)}, bf16[4,104,1280]{2,1,0:T(8,128)(2,1)S(1)}, u32[]{:S(2)}) copy-start(bf16[4,104,1280]{2,1,0:T(8,128)(2,1)S(1)} %pad_maximum_fusion.1.refs_4_) | copy-start | bytes 3194884
  37.5 15.5 %collective-permute-start.9 = (bf16[4,104,1280]{2,1,0:T(8,128)(2,1)S(1)}, bf16[4,104,1280]{2,1,0:T(8,128)(2,1)}, u32[]{:S(2)}, u32[]{:S(2)}) collective-permute-start(bf16[4,104,1280]{2,1,0:T(8,128)(2,1)S(1)} %pad_maximum_fusion.refs_0_), channel_id=1, source_target_pairs={{0,24},{4,100},{8,16},{12,108},{16,8},{20,116},{24,0},{28,124},{32... | collective-permute-start | bytes 3194888 | tf_op jit(solution)/shard_map/ppermute | solution.py:601
  40.1 14.2 %collective-permute-start.10 = (bf16[4,104,1280]{2,1,0:T(8,128)(2,1)S(1)}, bf16[4,104,1280]{2,1,0:T(8,128)(2,1)}, u32[]{:S(2)}, u32[]{:S(2)}) collective-permute-start(bf16[4,104,1280]{2,1,0:T(8,128)(2,1)S(1)} %pad_maximum_fusion.1.refs_4_), channel_id=1, source_target_pairs={{0,8},{4,36},{8,0},{12,44},{16,24},{20,52},{24,16},{28,60},{32,40}... | collective-permute-start | bytes 3194888 | tf_op jit(solution)/shard_map/ppermute | solution.py:601
  40.1 9.9 %collective-permute-start.7 = (bf16[128,1664]{1,0:T(8,128)(2,1)S(1)}, bf16[128,1664]{1,0:T(8,128)(2,1)S(1)}, u32[]{:S(2)}, u32[]{:S(2)}) collective-permute-start(bf16[128,1664]{1,0:T(8,128)(2,1)S(1)} %add_convert_fusion.1), channel_id=1, source_target_pairs={{0,1},{1,2},{2,3},{3,0},{4,5},{5,6},{6,7},{7,4},{8,9},{9,10},{10,1... | collective-permute-start | bytes 1277960 | tf_op jit(solution)/shard_map/ppermute | solution.py:643
  40.9 9.1 %collective-permute-start.8 = (bf16[128,1664]{1,0:T(8,128)(2,1)S(1)}, bf16[128,1664]{1,0:T(8,128)(2,1)S(1)}, u32[]{:S(2)}, u32[]{:S(2)}) collective-permute-start(bf16[128,1664]{1,0:T(8,128)(2,1)S(1)} %add_convert_fusion), channel_id=1, source_target_pairs={{0,3},{1,0},{2,1},{3,2},{4,7},{5,4},{6,5},{7,6},{8,11},{9,8},{10,9... | collective-permute-start | bytes 1277960 | tf_op jit(solution)/shard_map/ppermute | solution.py:643
  54.3 14.6 %collective-permute-start.13 = (bf16[4,104,1280]{2,1,0:T(8,128)(2,1)S(1)}, bf16[4,104,1280]{2,1,0:T(8,128)(2,1)S(1)}, u32[]{:S(2)}, u32[]{:S(2)}) collective-permute-start(bf16[4,104,1280]{2,1,0:T(8,128)(2,1)S(1)} %pad_maximum_fusion.refs_0_), channel_id=1, source_target_pairs={{0,96},{4,12},{8,104},{12,4},{16,112},{20,28},{24,120},{28,20},{32... | collective-permute-start | bytes 3194888 | tf_op jit(solution)/shard_map/ppermute | solution.py:601
  56.0 15.3 %collective-permute-start.14 = (bf16[4,104,1280]{2,1,0:T(8,128)(2,1)S(1)}, bf16[4,104,1280]{2,1,0:T(8,128)(2,1)S(1)}, u32[]{:S(2)}, u32[]{:S(2)}) collective-permute-start(bf16[4,104,1280]{2,1,0:T(8,128)(2,1)S(1)} %pad_maximum_fusion.1.refs_4_), channel_id=1, source_target_pairs={{0,32},{4,28},{8,40},{12,20},{16,48},{20,12},{24,56},{28,4},{32,0}... | collective-permute-start | bytes 3194888 | tf_op jit(solution)/shard_map/ppermute | solution.py:601
  56.0 9.0 %collective-permute-start.11 = (bf16[128,1664]{1,0:T(8,128)(2,1)S(1)}, bf16[128,1664]{1,0:T(8,128)(2,1)S(1)}, u32[]{:S(2)}, u32[]{:S(2)}) collective-permute-start(bf16[128,1664]{1,0:T(8,128)(2,1)S(1)} %get-tuple-element.112), channel_id=1, source_target_pairs={{0,1},{1,2},{2,3},{3,0},{4,5},{5,6},{6,7},{7,4},{8,9},{9,10},{10,1... | collective-permute-start | bytes 1277960 | tf_op jit(solution)/shard_map/ppermute | solution.py:643
  57.3 8.8 %collective-permute-start.12 = (bf16[128,1664]{1,0:T(8,128)(2,1)S(1)}, bf16[128,1664]{1,0:T(8,128)(2,1)S(1)}, u32[]{:S(2)}, u32[]{:S(2)}) collective-permute-start(bf16[128,1664]{1,0:T(8,128)(2,1)S(1)} %get-tuple-element.113), channel_id=1, source_target_pairs={{0,3},{1,0},{2,1},{3,2},{4,7},{5,4},{6,5},{7,6},{8,11},{9,8},{10,9... | collective-permute-start | bytes 1277960 | tf_op jit(solution)/shard_map/ppermute | solution.py:643
  68.9 4.7 %copy-start.15 = (bf16[4,104,1280]{2,1,0:T(8,128)(2,1)}, bf16[4,104,1280]{2,1,0:T(8,128)(2,1)S(1)}, u32[]{:S(2)}) copy-start(bf16[4,104,1280]{2,1,0:T(8,128)(2,1)S(1)} %collective-permute-done.13.refs_2_) | copy-start | bytes 3194884
  71.4 2.2 %copy-start.16 = (bf16[4,104,1280]{2,1,0:T(8,128)(2,1)}, bf16[4,104,1280]{2,1,0:T(8,128)(2,1)S(1)}, u32[]{:S(2)}) copy-start(bf16[4,104,1280]{2,1,0:T(8,128)(2,1)S(1)} %collective-permute-done.14.refs_6_) | copy-start | bytes 3194884
  73.6 14.2 %copy-start.5 = (s32[1024]{0:T(1024)S(1)}, s32[1024]{0:T(1024)}, u32[]{:S(2)}) copy-start(s32[1024]{0:T(1024)} %param.18) | copy-start | bytes 12292
  73.6 14.2 %copy-start.10 = (s32[1024]{0:T(1024)S(1)}, s32[1024]{0:T(1024)}, u32[]{:S(2)}) copy-start(s32[1024]{0:T(1024)} %param.19) | copy-start | bytes 12292
  73.6 14.2 %copy-start.11 = (s32[32]{0:T(128)S(1)}, s32[32]{0:T(128)}, u32[]{:S(2)}) copy-start(s32[32]{0:T(128)} %param.16) | copy-start | bytes 388
  73.6 14.2 %copy-start.12 = (s32[32]{0:T(128)S(1)}, s32[32]{0:T(128)}, u32[]{:S(2)}) copy-start(s32[32]{0:T(128)} %param.17) | copy-start | bytes 388
  73.6 4.4 %collective-permute-start.17 = (bf16[32,1664]{1,0:T(8,128)(2,1)S(1)}, bf16[32,1664]{1,0:T(8,128)(2,1)S(1)}, u32[]{:S(2)}, u32[]{:S(2)}) collective-permute-start(bf16[32,1664]{1,0:T(8,128)(2,1)S(1)} %get-tuple-element.127), channel_id=1, source_target_pairs={{0,3},{1,0},{2,1},{3,2},{4,7},{5,4},{6,5},{7,6},{8,11},{9,8},{10,9... | collective-permute-start | bytes 319496 | tf_op jit(solution)/shard_map/ppermute | solution.py:660
  76.4 5.1 %collective-permute-start.15 = (bf16[32,1664]{1,0:T(8,128)(2,1)S(1)}, bf16[32,1664]{1,0:T(8,128)(2,1)S(1)}, u32[]{:S(2)}, u32[]{:S(2)}) collective-permute-start(bf16[32,1664]{1,0:T(8,128)(2,1)S(1)} %get-tuple-element.125), channel_id=1, source_target_pairs={{0,1},{1,2},{2,3},{3,0},{4,5},{5,6},{6,7},{7,4},{8,9},{9,10},{10,1... | collective-permute-start | bytes 319496 | tf_op jit(solution)/shard_map/ppermute | solution.py:659
  76.5 16.3 %collective-permute-start.19 = (bf16[4,104,1280]{2,1,0:T(8,128)(2,1)}, bf16[4,104,1280]{2,1,0:T(8,128)(2,1)S(1)}, u32[]{:S(2)}, u32[]{:S(2)}) collective-permute-start(bf16[4,104,1280]{2,1,0:T(8,128)(2,1)} %collective-permute-done.9.refs_1_), channel_id=1, source_target_pairs={{0,96},{4,12},{8,104},{12,4},{16,112},{20,28},{24,120},{28,20},{32... | collective-permute-start | bytes 3194888 | tf_op jit(solution)/shard_map/ppermute | solution.py:601
  76.5 16.2 %collective-permute-start.20 = (bf16[4,104,1280]{2,1,0:T(8,128)(2,1)}, bf16[4,104,1280]{2,1,0:T(8,128)(2,1)S(1)}, u32[]{:S(2)}, u32[]{:S(2)}) collective-permute-start(bf16[4,104,1280]{2,1,0:T(8,128)(2,1)} %collective-permute-done.10.refs_5_), channel_id=1, source_target_pairs={{0,32},{4,28},{8,40},{12,20},{16,48},{20,12},{24,56},{28,4},{32,0}... | collective-permute-start | bytes 3194888 | tf_op jit(solution)/shard_map/ppermute | solution.py:601
  78.1 6.1 %collective-permute-start.18 = (bf16[64,1664]{1,0:T(8,128)(2,1)S(1)}, bf16[64,1664]{1,0:T(8,128)(2,1)S(1)}, u32[]{:S(2)}, u32[]{:S(2)}) collective-permute-start(bf16[64,1664]{1,0:T(8,128)(2,1)S(1)} %pad_maximum_fusion.5), channel_id=1, source_target_pairs={{0,3},{1,0},{2,1},{3,2},{4,7},{5,4},{6,5},{7,6},{8,11},{9,8},{10,9... | collective-permute-start | bytes 638984 | tf_op jit(solution)/shard_map/ppermute | solution.py:643
  81.5 6.3 %collective-permute-start.16 = (bf16[64,1664]{1,0:T(8,128)(2,1)S(1)}, bf16[64,1664]{1,0:T(8,128)(2,1)S(1)}, u32[]{:S(2)}, u32[]{:S(2)}) collective-permute-start(bf16[64,1664]{1,0:T(8,128)(2,1)S(1)} %pad_maximum_fusion.4), channel_id=1, source_target_pairs={{0,1},{1,2},{2,3},{3,0},{4,5},{5,6},{6,7},{7,4},{8,9},{9,10},{10,1... | collective-permute-start | bytes 638984 | tf_op jit(solution)/shard_map/ppermute | solution.py:643
  89.0 12.3 %all-to-all-start = ((bf16[16,8,1792]{2,1,0:T(8,128)(2,1)}), bf16[16,8,1792]{2,1,0:T(8,128)(2,1)S(1)}, u32[]{:S(2)}, u32[]{:S(2)}) async-start(bf16[16,8,1792]{2,1,0:T(8,128)(2,1)} %bitcast.8), calls=%async_computation | async-start | bytes 917504 | tf_op jit(solution)/shard_map/all_to_all | solution.py:665
  92.7 1.0 copy-start.17
  92.7 1.4 %copy-start.18 = (bf16[4,104,1280]{2,1,0:T(8,128)(2,1)}, bf16[4,104,1280]{2,1,0:T(8,128)(2,1)S(1)}, u32[]{:S(2)}) copy-start(bf16[4,104,1280]{2,1,0:T(8,128)(2,1)S(1)} %collective-permute-done.20.refs_7_) | copy-start | bytes 3194884
  94.1 16.5 %copy-start.8 = (f32[1664]{0:T(1024)S(1)}, f32[1664]{0:T(1024)}, u32[]{:S(2)}) copy-start(f32[1664]{0:T(1024)} %gain_ref.3) | copy-start | bytes 19972
  94.1 16.5 %copy-start.9 = (f32[1664]{0:T(1024)S(1)}, f32[1664]{0:T(1024)}, u32[]{:S(2)}) copy-start(f32[1664]{0:T(1024)} %bias_ref.3) | copy-start | bytes 19972
  97.8 3.4 %copy-start = (bf16[16,104,2560]{2,1,0:T(8,128)(2,1)}, bf16[16,104,2560]{2,1,0:T(8,128)(2,1)S(1)}, u32[]{:S(2)}) copy-start(bf16[16,104,2560]{2,1,0:T(8,128)(2,1)S(1)} %get-tuple-element.134) | copy-start | bytes 25559044
  101.3 9.3 %collective-permute-start.21 = (bf16[128,1792]{1,0:T(8,128)(2,1)S(1)}, bf16[128,1792]{1,0:T(8,128)(2,1)S(1)}, u32[]{:S(2)}, u32[]{:S(2)}) collective-permute-start(bf16[128,1792]{1,0:T(8,128)(2,1)S(1)} %bitcast.15), channel_id=1, source_target_pairs={{0,4},{4,0},{8,12},{12,8},{16,20},{20,16},{24,28},{28,24},{32,36},... | collective-permute-start | bytes 1376264 | tf_op jit(solution)/shard_map/ppermute | solution.py:670
  110.6 3.4 %copy-start.1 = (bf16[16,104,2560]{2,1,0:T(8,128)(2,1)S(1)}, bf16[16,104,2560]{2,1,0:T(8,128)(2,1)}, u32[]{:S(2)}) copy-start(bf16[16,104,2560]{2,1,0:T(8,128)(2,1)} %copy-done) | copy-start | bytes 25559044
  120.2 2.7 %collective-permute-start.22 = (bf16[128,832]{1,0:T(8,128)(2,1)S(1)}, bf16[128,832]{1,0:T(8,128)(2,1)S(1)}, u32[]{:S(2)}, u32[]{:S(2)}) collective-permute-start(bf16[128,832]{1,0:T(8,128)(2,1)S(1)} %get-tuple-element.139), channel_id=1, source_target_pairs={{0,4},{4,0},{8,12},{12,8},{16,20},{20,16},{24,28},{28,24},{32,36},... | collective-permute-start | bytes 638984 | tf_op jit(solution)/shard_map/ppermute | solution.py:544
